TPU v7x, 128 devices: a whole 4x4x4 slice. The times are simulated.
128 devices in a mesh: row: 16 (over z, x_lo, core), col: 8 (over x_hi, y).
Axes of the slice: x: 4 (x_hi: 2, x_lo: 2; x = x_hi * 2 + x_lo), y: 4, z: 4, core: 2. Of those that a mesh axis runs over, the one named last changes fastest.
Arguments:
- base_weight: bfloat16 [16384, 49152], P('row', 'col'), may hold values from -6 to 6
- left_factor: float32 [16384, 256], P('row', 'col'), may hold values from -6 to 6
- right_factor: float32 [256, 49152], P('row', 'col'), may hold values from -0.375 to 0.375
Outputs:
- merged: bfloat16 [16384, 49152], P(None, ('row', 'col'))
All inputs are finite; a program needn't handle non-finite values.
Results may differ from a plain program's by a relative error of at most 0.001.
Values may be sent and summed in bfloat16 or wider, within the bound.
No kernel may reach another device: no remote copies, remote signals or barrier semaphores. Data moves between devices by JAX's collectives and lax.ppermute only.
A program may use at most 192 MiB of HBM per device.

v0:
```python
import jax
import jax.numpy as jnp
from jax import lax
from jax.sharding import PartitionSpec as P


def copy_for_each(value, axis):
    length = lax.axis_size(axis)
    return lax.all_to_all(
        jnp.broadcast_to(value[None], (length, *value.shape)), axis, 0, 0, tiled=True
    )


def joined_along(tiles, dim):
    tiles = jnp.moveaxis(tiles, 0, dim)
    lengths = tiles.shape
    return tiles.reshape(*lengths[:dim], lengths[dim] * lengths[dim + 1], *lengths[dim + 2 :])


def gathered_copies(value, axis, dim):
    tiles = copy_for_each(value, axis)
    return joined_along(tiles, dim)


def to_serving(stored):
    row_count = lax.axis_size("row")
    col_count = lax.axis_size("col")
    height = stored.shape[0]
    block_width = stored.shape[1] // row_count
    group_count = row_count // col_count
    shaped = stored.reshape(height, group_count, col_count, block_width)
    across = lax.all_to_all(shaped, "col", split_axis=2, concat_axis=1, tiled=True)
    served = lax.all_to_all(across, "row", split_axis=1, concat_axis=0, tiled=True)
    return served.reshape(height * row_count, block_width)


def body(base_weight, left_factor, right_factor):
    left_cols = gathered_copies(left_factor, "col", 1)
    delta = jnp.dot(
        left_cols,
        lax.all_gather(right_factor, "row", axis=0, tiled=True),
        precision=lax.Precision.HIGHEST,
        preferred_element_type=jnp.float32,
    )
    merged_block = (base_weight.astype(jnp.float32) + delta).astype(jnp.bfloat16)
    return to_serving(merged_block)


def solution(mesh):
    placed = (P("row", "col"), P("row", "col"), P("row", "col"))
    return jax.shard_map(
        body, mesh=mesh, in_specs=placed, out_specs=P(None, ("row", "col")), check_vma=False
    )
```

profile of v0, /device:TPU:15, one launch (start us, length us, event | category | flops | bytes accessed | tf_op | source)
XLA Modules:
  0.0 395.8 jit_solution(9621992016833128022)
XLA Ops:
  6.5 0.0 all-gather.2.cloned.1.call-start
  6.5 0.7 all-gather.2.cloned.1.call-update
  7.3 1.0 broadcast_in_dim.2
  8.3 21.6 %all_to_all.38 = f32[8,1024,32]{1,2,0:T(8,128)S(1)} all-to-all(f32[8,1024,32]{1,2,0:T(8,128)S(1)} %broadcast_in_dim.2), channel_id=1, replica_groups=mesh['row'=16,'col'=8] {'col'}, dimensions={0} | all-to-all | bytes 2097152 | tf_op jit(solution)/shard_map/all_to_all | solution.py:9
  29.9 30.1 %all-gather.2.cloned.1.call-done = f32[256,6144]{1,0:T(8,128)} async-done(((f32[16,6144]{1,0:T(8,128)}), f32[256,6144]{1,0:T(8,128)}) %all-gather.2.cloned.1.call-update) | async-done | bytes 6291472 | tf_op jit(solution)/shard_map/all_gather | solution.py:41
  60.0 23.9 %add_convert_fusion = bf16[1024,6144]{1,0:T(8,128)(2,1)S(1)} fusion(bf16[1024,6144]{1,0:T(8,128)(2,1)} %param.3, f32[1024,256]{0,1:T(8,128)S(1)} %bitcast.24, f32[256,6144]{1,0:T(8,128)} %all-gather.2.cloned.1.call-done), kind=kOutput, calls=%fused_computation | convolution fusion | flops 19346227200 | bytes 32505856 | tf_op jit(solution)/shard_map/dot_general | solution.py:39
  83.9 3.0 copy.8
  86.9 7.9 %copy.6 = bf16[1024,2,8,384]{3,0,1,2:T(8,128)(2,1)S(1)} copy(bf16[1024,2,8,384]{3,2,1,0:T(8,128)(2,1)S(1)} %bitcast.21) | data formatting | bytes 25165824 | tf_op jit(solution)/shard_map/reshape | solution.py:31
  94.9 144.2 %all_to_all.39 = bf16[1024,2,8,384]{3,0,1,2:T(8,128)(2,1)S(1)} all-to-all(bf16[1024,2,8,384]{3,0,1,2:T(8,128)(2,1)S(1)} %copy.6), channel_id=1, replica_groups=mesh['row'=16,'col'=8] {'col'}, dimensions={2} | all-to-all | bytes 25165824 | tf_op jit(solution)/shard_map/all_to_all | solution.py:32
  239.0 145.1 %all_to_all.40 = bf16[1024,16,1,384]{3,0,2,1:T(8,128)(2,1)S(1)} all-to-all(bf16[1024,16,1,384]{3,0,2,1:T(8,128)(2,1)S(1)} %bitcast.22), channel_id=1, replica_groups=mesh['row'=16,'col'=8] {'row'}, dimensions={1} | all-to-all | bytes 25165824 | tf_op jit(solution)/shard_map/all_to_all | solution.py:33
  384.1 4.8 %copy.10 = bf16[16384,384]{1,0:T(8,128)(2,1)} copy(bf16[16384,384]{1,0:T(8,128)(2,1)S(1)} %bitcast.23) | data formatting | bytes 25165824
Async XLA Ops:
  6.5 53.5 %all-gather.2.cloned.1.call-start = ((), (), s32[]{:S(2)}) async-start(), calls=%async_computation.3 | async-start | bytes 6684672 | tf_op jit(solution)/shard_map/all_gather | solution.py:41
Sparse Core Ops, SparseCore 0:
  9.1 50.9 all-gather.1
where the time goes:
time: 399 us; the launch traced here: 396 us
  blocking collectives  311 us (78%)
  waiting for transfers between devices  30.8 us (8%)
  matrix products  23.9 us (6%)
  local copies, waits for them, and re-layouts  16.7 us (4%)
  between operations  13.4 us (3%)
    all_to_all x1, blocking collectives, to_serving(): lax.all_to_all(across, 'row', split_axis=1, concat_axis=0, tiled=True)  145 us
    all_to_all x1, blocking collectives, to_serving(): lax.all_to_all(shaped, 'col', split_axis=2, concat_axis=1, tiled=True)  144 us
    all_gather x1, waiting for transfers between devices, body(): lax.all_gather(right_factor, 'row', axis=0, tiled=True)  30.1 us
    dot_general x1, matrix products, body(): jnp.dot(left_cols, lax.all_gather(right_factor, 'row', axis=0, tiled=True...  23.9 us
    all_to_all x1, blocking collectives, copy_for_each(): lax.all_to_all(jnp.broadcast_to(value[None], (length, *value.shape)), axi...  21.6 us
  transfers between devices with their start and end apart: 1, of which 1 were waited for; matrix products, arithmetic and copies ran while one was open for 0% of the time, Pallas kernels for 0%

commit v1 on v0

v1 whole, which is shorter than its diff:
```python
import jax
import jax.numpy as jnp
from jax import lax
from jax.sharding import Mesh
from jax.sharding import PartitionSpec as P

AXES = ("z", "xl", "c", "xh", "y")
SIZES = (4, 2, 2, 2, 4)
CHUNKS = 4


def split(value):
    high = lax.reduce_precision(value, 8, 7)
    return high.astype(jnp.bfloat16), (value - high).astype(jnp.bfloat16)


def number(z, xl, c, xh, y):
    return (((z * 2 + xl) * 2 + c) * 2 + xh) * 4 + y


def target(k, z, xl, c, xh):
    k2, k1, k0 = k >> 2, (k >> 1) & 1, k & 1
    return (z >> 1) ^ k2 ^ c, xl ^ k1, xh * 2 + ((z & 1) ^ k0)


def pairs(k):
    out = []
    for z in range(4):
        for xl in range(2):
            for c in range(2):
                for xh in range(2):
                    for y in range(4):
                        xh2, xl2, z2 = target(k, z, xl, c, xh)
                        out.append((number(z, xl, c, xh, y), number(z2, xl2, c, xh2, y)))
    return out


def body(base, left, right):
    height, width = base.shape
    block = width // 16
    rows = height // CHUNKS
    depth = right.shape[0]
    z, xl, c = (lax.axis_index(n) for n in ("z", "xl", "c"))

    lefts = jnp.stack(split(left))
    lefts = lax.all_gather(lefts, ("c", "xh", "y"), axis=0)
    lefts = lefts.reshape(2, 8, 2, height, left.shape[1])
    lefts = lefts.transpose(2, 0, 3, 1, 4).reshape(2, 2, height, 8 * left.shape[1])
    left_cat = jnp.concatenate([lefts[0], lefts[0], lefts[1]], -1)

    rights = jnp.stack(split(right))
    rights = rights.reshape(2, depth, 2, 2, 4, block).transpose(2, 4, 0, 1, 3, 5)
    rights = rights.reshape(8, 2, depth, 2, block)
    rights = lax.all_to_all(rights, ("c", "y"), 0, 0, tiled=True)
    rights = lax.all_gather(rights, ("z", "xl"), axis=0)
    rights = rights.reshape(8, 2, 4, 2, depth, 2, block).transpose(2, 5, 3, 0, 1, 4, 6)
    rights = rights.reshape(4, 2, 2, 16 * depth, block)
    right_cat = jnp.concatenate([rights[:, :, 0], rights[:, :, 1], rights[:, :, 0]], 2)

    order = []
    for k in range(8):
        k2, k1, k0 = k >> 2, (k >> 1) & 1, k & 1
        order.append((((z & 1) ^ k0) * 2 + (xl ^ k1), (z >> 1) ^ k2 ^ c))
    right_cat = jnp.concatenate(
        [lax.dynamic_slice(right_cat, (y, j2, 0, 0), (1, 1, *right_cat.shape[2:]))[0, 0] for y, j2 in order],
        1,
    )

    def first(part):
        part = part.reshape(rows, 2, 2, 4, block).transpose(1, 3, 2, 0, 4)
        part = lax.all_to_all(
            part.reshape(8, 2, rows, block), ("c", "y"), 0, 0, tiled=True
        )
        return part.reshape(2, 4, 2, rows, block)

    def add(i, part):
        part = jnp.concatenate(
            [lax.dynamic_slice(part, (0, y, j2, 0, 0), (2, 1, 1, rows, block))[:, 0, 0] for y, j2 in order],
            2,
        )
        delta = jnp.dot(
            left_cat[:, i * rows : (i + 1) * rows].reshape(2 * rows, -1),
            right_cat,
            preferred_element_type=jnp.float32,
        )
        sent = part.astype(jnp.float32) + delta.reshape(2, rows, 8 * block)
        sent = sent.astype(jnp.bfloat16)
        return [sent[..., k * block : (k + 1) * block] for k in range(8)]

    xh = lax.axis_index("xh")
    merged = jnp.zeros((8, 2, CHUNKS, rows, block), jnp.bfloat16)
    parts = [base[i * rows : (i + 1) * rows] for i in range(CHUNKS)]
    got, sent = [], add(0, first(parts[0]))
    for i in range(CHUNKS):
        if i + 1 < CHUNKS:
            got, sent, parts[i + 1] = lax.optimization_barrier((got, sent, parts[i + 1]))
        else:
            got, sent = lax.optimization_barrier((got, sent))
        arrived = first(parts[i + 1]) if i + 1 < CHUNKS else None
        new = [lax.ppermute(sent[k], AXES, pairs(k)) for k in range(8)]
        for k, one in enumerate(got):
            merged = place(merged, one, i - 1, k, z, xl, c, xh)
        got = new
        if arrived is not None:
            sent = add(i + 1, arrived)
    for k, one in enumerate(got):
        merged = place(merged, one, CHUNKS - 1, k, z, xl, c, xh)
    return merged.reshape(16 * height, block)


def place(merged, one, i, k, z, xl, c, xh):
    k2, k1, k0 = k >> 2, (k >> 1) & 1, k & 1
    slot = ((xh ^ k2 ^ c) * 2 + ((z & 1) ^ k0)) * 2 + (xl ^ k1)
    return lax.dynamic_update_slice(merged, one[None, :, None], (slot, 0, i, 0, 0))


def solution(mesh):
    fine = Mesh(mesh.devices.reshape(SIZES), AXES)
    placed = P(("z", "xl", "c"), ("xh", "y"))
    return jax.shard_map(
        body,
        mesh=fine,
        in_specs=(placed, placed, placed),
        out_specs=P(None, AXES),
        check_vma=False,
    )
```

time: 399 us -> 437 us (1.095)
  blocking collectives: 311 us -> 12.4 us
  local copies, waits for them, and re-layouts: 16.7 us -> 151 us
  starting transfers between devices: 0.01 us -> 98.7 us
  waiting for transfers between devices: 30.8 us -> 129 us
  other arithmetic: 0 us -> 7.04 us
    all_to_all x3 -> x1, blocking collectives: 311 us -> 12.4 us  [body(): rights = lax.all_to_all(rights, ('c', 'y'), 0, 0, tiled=True)]
    ppermute x0 -> x32, starting transfers between devices: none -> 76.2 us  [body(): new = [lax.ppermute(sent[k], AXES, pairs(k)) for k in range(8)]]
    all_to_all x0 -> x4, waiting for transfers between devices: none -> 62.3 us  [first(): lax.all_to_all(part.reshape(8, 2, rows, block), ('c', 'y'), 0, 0, tiled=T...]
    dynamic_update_slice x0 -> x33, local copies, waits for them, and re-layouts: none -> 51 us  [place(): lax.dynamic_update_slice(merged, one[None, :, None], (slot, 0, i, 0, 0))]
    ppermute x0 -> x32, waiting for transfers between devices: none -> 33.1 us  [body(): new = [lax.ppermute(sent[k], AXES, pairs(k)) for k in range(8)]]
    unnamed x2 -> x76, local copies, waits for them, and re-layouts: 7.78 us -> 35.4 us
    all_to_all x0 -> x4, starting transfers between devices: none -> 22.5 us  [first(): lax.all_to_all(part.reshape(8, 2, rows, block), ('c', 'y'), 0, 0, tiled=T...]
    transpose x0 -> x6, local copies, waits for them, and re-layouts: none -> 19.2 us  [the longest x4 16.7 us: first(): part = part.reshape(rows, 2, 2, 4, block).transpose(1, 3, 2, 0, 4)]
  transfers between devices with their start and end apart: 1 -> 38, of which waited for: 1 -> 13; matrix products, arithmetic and copies ran while one was open for 0% -> 35% of each run, Pallas kernels for 0% -> 0%
where the time goes in v1:
time: 437 us; the launch traced here: 434 us
  local copies, waits for them, and re-layouts  151 us (35%)
  waiting for transfers between devices  129 us (30%)
  starting transfers between devices  98.7 us (23%)
  matrix products  21.9 us (5%)
  between operations  14 us (3%)
  blocking collectives  12.4 us (3%)
  other arithmetic  7.04 us (2%)
    ppermute x32, starting transfers between devices, body(): new = [lax.ppermute(sent[k], AXES, pairs(k)) for k in range(8)]  76.2 us
    all_to_all x4, waiting for transfers between devices, first(): lax.all_to_all(part.reshape(8, 2, rows, block), ('c', 'y'), 0, 0, tiled=T...  62.3 us
    dynamic_update_slice x33, local copies, waits for them, and re-layouts, place(): lax.dynamic_update_slice(merged, one[None, :, None], (slot, 0, i, 0, 0))  51 us
    unnamed x76, local copies, waits for them, and re-layouts  35.4 us
    all_gather x1, waiting for transfers between devices, body(): rights = lax.all_gather(rights, ('z', 'xl'), axis=0)  33.2 us
    ppermute x32, waiting for transfers between devices, body(): new = [lax.ppermute(sent[k], AXES, pairs(k)) for k in range(8)]  33.1 us
    all_to_all x4, starting transfers between devices, first(): lax.all_to_all(part.reshape(8, 2, rows, block), ('c', 'y'), 0, 0, tiled=T...  22.5 us
    dot_general x4, matrix products, add(): jnp.dot(left_cat[:, i * rows:(i + 1) * rows].reshape(2 * rows, -1), right...  21.9 us
  transfers between devices with their start and end apart: 38, of which 13 were waited for; matrix products, arithmetic and copies ran while one was open for 35% of the time, Pallas kernels for 0%

profile of v1, /device:TPU:15, one launch (start us, length us, event | category | flops | bytes accessed | tf_op | source)
XLA Modules:
  0.0 434.0 jit_solution(3002286371246647491)
XLA Ops:
  9.9 12.4 %all_to_all.25 = bf16[8,2,16,2,384]{4,2,3,1,0:T(8,128)(2,1)} all-to-all(bf16[8,2,16,2,384]{4,2,3,1,0:T(8,128)(2,1)S(1)} %bitcast.275), channel_id=1, replica_groups=mesh['z'=4,'xl'=2,'c'=2,'xh'=2,'y'=4] {'c','y'}, dimensions={0} | all-to-all | bytes 786432 | tf_op jit(solution)/shard_map/all_to_all | solution.py:54
  22.3 8.7 %fusion.24 = (bf16[256,6144]{1,0:T(8,128)(2,1)S(1)}, bf16[256,6144]{1,0:T(8,128)(2,1)}, bf16[256,6144]{1,0:T(8,128)(2,1)}, bf16[256,6144]{1,0:T(8,128)(2,1)}) fusion(bf16[1024,6144]{1,0:T(8,128)(2,1)} %param.3), kind=kLoop, calls=%fused_computation.102 | loop fusion | bytes 25165824 | tf_op jit(solution)/shard_map/slice | solution.py:92
  31.1 4.6 %copy.140 = bf16[256,6144]{0,1:T(8,128)(2,1)} copy(bf16[256,6144]{1,0:T(8,128)(2,1)} %get-tuple-element.126) | data formatting | bytes 6291456
  35.7 4.6 %copy.101 = bf16[2,4,2,256,384]{4,3,2,1,0:T(8,128)(2,1)} copy(bf16[2,4,2,256,384]{3,4,1,2,0:T(8,128)(2,1)} %bitcast.270) | data formatting | bytes 6291456 | tf_op jit(solution)/shard_map/transpose | solution.py:70
  40.3 5.4 %all-to-all-start = ((bf16[8,2,256,384]{3,2,1,0:T(8,128)(2,1)}), bf16[8,2,256,384]{3,2,1,0:T(8,128)(2,1)}, u32[]{:S(2)}, u32[]{:S(2)}) async-start(bf16[8,2,256,384]{3,2,1,0:T(8,128)(2,1)} %bitcast.266), calls=%async_computation | async-start | bytes 6291456 | tf_op jit(solution)/shard_map/all_to_all | solution.py:71
  45.7 4.7 %copy.142 = bf16[256,6144]{0,1:T(8,128)(2,1)} copy(bf16[256,6144]{1,0:T(8,128)(2,1)} %get-tuple-element.125) | data formatting | bytes 6291456 | tf_op jit(solution)/shard_map/optimization_barrier | solution.py:96
  50.4 34.6 %all-to-all-done = bf16[8,2,256,384]{3,2,1,0:T(8,128)(2,1)} async-done(((bf16[8,2,256,384]{3,2,1,0:T(8,128)(2,1)}), bf16[8,2,256,384]{3,2,1,0:T(8,128)(2,1)}, u32[]{:S(2)}, u32[]{:S(2)}) %all-to-all-start) | async-done | bytes 3145760 | tf_op jit(solution)/shard_map/all_to_all | solution.py:71
  86.8 1.8 bitcast_dynamic-update-slice_fusion.70
  90.5 1.8 bitcast_dynamic-update-slice_fusion.68
  92.3 1.8 bitcast_dynamic-update-slice_fusion.67
  94.1 1.9 bitcast_dynamic-update-slice_fusion.66
  99.6 3.2 fusion.29
  102.8 2.3 copy.102
  105.1 2.3 copy.104
  107.4 3.6 pad_maximum_fusion.1
  111.0 33.2 %all-gather.7.cloned.1.call-done = bf16[64,2,16,2,384]{4,2,3,1,0:T(8,128)(2,1)} async-done(((bf16[8,2,16,2,384]{4,2,3,1,0:T(8,128)(2,1)}), bf16[64,2,16,2,384]{4,2,3,1,0:T(8,128)(2,1)}) %all-gather.7.cloned.1.call-update) | async-done | bytes 3145744 | tf_op jit(solution)/shard_map/all_gather | solution.py:55
  144.2 2.3 copy.106
  148.8 6.2 %add_convert_fusion.3 = bf16[2,256,3072]{2,1,0:T(8,128)(2,1)S(1)} fusion(bf16[2,256,3072]{2,1,0:T(8,128)(2,1)} %bitcast_dynamic-update-slice_fusion.64, bf16[768,3072]{1,0:T(8,128)(2,1)S(1)} %bitcast_dynamic-update-slice_fusion, bf16[2,1024,768]{2,1,0:T(8,128)(2,1)} %pad_maximum_fusion.1), kind=kOutput, calls=%fused_computation.3 | convolution fusion | flops 2420637696 | bytes 11796480 | tf_op jit(solution)/shard_map/dot_general | solution.py:81
  156.6 4.6 %copy.109 = bf16[2,4,2,256,384]{4,3,2,1,0:T(8,128)(2,1)} copy(bf16[2,4,2,256,384]{3,4,1,2,0:T(8,128)(2,1)} %bitcast.264) | data formatting | bytes 6291456 | tf_op jit(solution)/shard_map/transpose | solution.py:70
  161.2 5.2 %all-to-all-start.2 = ((bf16[8,2,256,384]{3,2,1,0:T(8,128)(2,1)}), bf16[8,2,256,384]{3,2,1,0:T(8,128)(2,1)}, u32[]{:S(2)}, u32[]{:S(2)}) async-start(bf16[8,2,256,384]{3,2,1,0:T(8,128)(2,1)} %bitcast.268), calls=%async_computation.2 | async-start | bytes 6291456 | tf_op jit(solution)/shard_map/all_to_all | solution.py:71
  166.4 4.7 %copy.143 = bf16[256,6144]{0,1:T(8,128)(2,1)} copy(bf16[256,6144]{1,0:T(8,128)(2,1)} %get-tuple-element.124) | data formatting | bytes 6291456 | tf_op jit(solution)/shard_map/optimization_barrier | solution.py:96
  171.1 4.5 %collective-permute-start = (bf16[2,256,384]{2,1,0:T(8,128)(2,1)}, bf16[2,256,384]{2,1,0:T(8,128)(2,1)}, u32[]{:S(2)}, u32[]{:S(2)}) collective-permute-start(bf16[2,256,384]{2,1,0:T(8,128)(2,1)} %get-tuple-element.64), channel_id=1, source_target_pairs={{0,0},{1,1},{2,2},{3,3},{4,64},{5,65},{6,66},{7,67},{8,12},{9,13},... | collective-permute-start | bytes 1179656 | tf_op jit(solution)/shard_map/ppermute | solution.py:100
  175.7 2.2 collective-permute-start.2
  178.1 5.7 %collective-permute-start.4 = (bf16[2,256,384]{2,1,0:T(8,128)(2,1)}, bf16[2,256,384]{2,1,0:T(8,128)(2,1)}, u32[]{:S(2)}, u32[]{:S(2)}) collective-permute-start(bf16[2,256,384]{2,1,0:T(8,128)(2,1)} %get-tuple-element.68), channel_id=1, source_target_pairs={{0,4},{1,5},{2,6},{3,7},{4,68},{5,69},{6,70},{7,71},{8,8},{9,9},{1... | collective-permute-start | bytes 1179656 | tf_op jit(solution)/shard_map/ppermute | solution.py:100
  183.8 19.6 %all-to-all-done.2 = bf16[8,2,256,384]{3,2,1,0:T(8,128)(2,1)} async-done(((bf16[8,2,256,384]{3,2,1,0:T(8,128)(2,1)}), bf16[8,2,256,384]{3,2,1,0:T(8,128)(2,1)}, u32[]{:S(2)}, u32[]{:S(2)}) %all-to-all-start.2) | async-done | bytes 3145760 | tf_op jit(solution)/shard_map/all_to_all | solution.py:71
  212.3 2.0 collective-permute-start.5
  214.3 2.8 collective-permute-start.6
  217.1 2.4 collective-permute-start.7
  219.5 5.2 %add_convert_fusion.2 = bf16[2,256,3072]{2,1,0:T(8,128)(2,1)S(1)} fusion(bf16[2,256,3072]{2,1,0:T(8,128)(2,1)S(1)} %bitcast_dynamic-update-slice_fusion.56, bf16[768,3072]{1,0:T(8,128)(2,1)} %copy-done.19, bf16[2,1024,768]{2,1,0:T(8,128)(2,1)} %pad_maximum_fusion.1), kind=kOutput, calls=%fused_computation.2 | convolution fusion | flops 2420637696 | bytes 11796480 | tf_op jit(solution)/shard_map/dot_general | solution.py:81
  226.3 2.3 collective-permute-done.6
  228.6 3.6 collective-permute-done.7
  232.2 4.6 %copy.113 = bf16[2,4,2,256,384]{4,3,2,1,0:T(8,128)(2,1)} copy(bf16[2,4,2,256,384]{3,4,1,2,0:T(8,128)(2,1)} %bitcast.265) | data formatting | bytes 6291456 | tf_op jit(solution)/shard_map/transpose | solution.py:70
  236.8 5.0 %all-to-all-start.3 = ((bf16[8,2,256,384]{3,2,1,0:T(8,128)(2,1)}), bf16[8,2,256,384]{3,2,1,0:T(8,128)(2,1)}, u32[]{:S(2)}, u32[]{:S(2)}) async-start(bf16[8,2,256,384]{3,2,1,0:T(8,128)(2,1)} %bitcast.263), calls=%async_computation.3 | async-start | bytes 6291456 | tf_op jit(solution)/shard_map/all_to_all | solution.py:71
  241.8 2.8 copy.144
  246.8 5.8 %collective-permute-start.12 = (bf16[2,256,384]{2,1,0:T(8,128)(2,1)}, bf16[2,256,384]{2,1,0:T(8,128)(2,1)S(1)}, u32[]{:S(2)}, u32[]{:S(2)}) collective-permute-start(bf16[2,256,384]{2,1,0:T(8,128)(2,1)} %get-tuple-element.85), channel_id=1, source_target_pairs={{0,4},{1,5},{2,6},{3,7},{4,68},{5,69},{6,70},{7,71},{8,8},{9,9},{1... | collective-permute-start | bytes 1179656 | tf_op jit(solution)/shard_map/ppermute | solution.py:100
  254.1 2.7 collective-permute-start.14
  256.7 6.6 %broadcast_in_dim.99 = bf16[8,2,4,256,384]{4,3,1,2,0:T(8,128)(2,1)} broadcast(bf16[]{:T(256)} %constant.8.clone.1), dimensions={} | broadcast | bytes 12582914 | tf_op jit(solution)/shard_map/broadcast_in_dim | solution.py:91
  270.5 8.1 %all-to-all-done.3 = bf16[8,2,256,384]{3,2,1,0:T(8,128)(2,1)} async-done(((bf16[8,2,256,384]{3,2,1,0:T(8,128)(2,1)}), bf16[8,2,256,384]{3,2,1,0:T(8,128)(2,1)}, u32[]{:S(2)}, u32[]{:S(2)}) %all-to-all-start.3) | async-done | bytes 3145760 | tf_op jit(solution)/shard_map/all_to_all | solution.py:71
  287.5 2.3 collective-permute-start.15
  289.8 2.7 collective-permute-start.8
  292.5 2.0 collective-permute-start.9
  294.5 5.2 %add_convert_fusion.1 = bf16[2,256,3072]{2,1,0:T(8,128)(2,1)S(1)} fusion(bf16[2,256,3072]{2,1,0:T(8,128)(2,1)S(1)} %bitcast_dynamic-update-slice_fusion.41, bf16[768,3072]{1,0:T(8,128)(2,1)} %copy-done.19, bf16[2,1024,768]{2,1,0:T(8,128)(2,1)} %pad_maximum_fusion.1), kind=kOutput, calls=%fused_computation.1 | convolution fusion | flops 2420637696 | bytes 11796480 | tf_op jit(solution)/shard_map/dot_general | solution.py:81
  301.5 4.3 collective-permute-done.9
  306.6 2.8 copy.123
  309.4 6.9 %all-to-all-start.4 = ((bf16[8,2,256,384]{3,2,1,0:T(8,128)(2,1)}), bf16[8,2,256,384]{3,2,1,0:T(8,128)(2,1)S(1)}, u32[]{:S(2)}, u32[]{:S(2)}) async-start(bf16[8,2,256,384]{3,2,1,0:T(8,128)(2,1)} %bitcast.267), calls=%async_computation.4 | async-start | bytes 6291456 | tf_op jit(solution)/shard_map/all_to_all | solution.py:71
  316.4 1.8 bitcast_dynamic-update-slice_fusion.51
  321.8 10.8 %copy.111 = bf16[8,2,4,256,384]{4,3,2,1,0:T(8,128)(2,1)} copy(bf16[8,2,4,256,384]{4,3,1,2,0:T(8,128)(2,1)} %bitcast_dynamic-update-slice_fusion.49) | data formatting | bytes 25165824 | tf_op jit(solution)/shard_map/dynamic_update_slice | solution.py:114
  332.6 1.9 bitcast_dynamic-update-slice_fusion.32
  334.5 1.9 collective-permute-start.16
  336.4 3.6 collective-permute-start.17
  341.5 4.7 %collective-permute-start.20 = (bf16[2,256,384]{2,1,0:T(8,128)(2,1)S(1)}, bf16[2,256,384]{2,1,0:T(8,128)(2,1)}, u32[]{:S(2)}, u32[]{:S(2)}) collective-permute-start(bf16[2,256,384]{2,1,0:T(8,128)(2,1)S(1)} %copy-done.6), channel_id=1, source_target_pairs={{0,4},{1,5},{2,6},{3,7},{4,68},{5,69},{6,70},{7,71},{8,8},{9,9},{1... | collective-permute-start | bytes 1179656 | tf_op jit(solution)/shard_map/ppermute | solution.py:100
  355.5 2.2 collective-permute-start.21
  357.7 3.9 collective-permute-start.22
  362.6 5.2 %add_convert_fusion = bf16[2,256,3072]{2,1,0:T(8,128)(2,1)S(1)} fusion(bf16[2,256,3072]{2,1,0:T(8,128)(2,1)S(1)} %bitcast_dynamic-update-slice_fusion.33, bf16[768,3072]{1,0:T(8,128)(2,1)} %copy-done.19, bf16[2,1024,768]{2,1,0:T(8,128)(2,1)} %pad_maximum_fusion.1), kind=kOutput, calls=%fused_computation | convolution fusion | flops 2420637696 | bytes 11796480 | tf_op jit(solution)/shard_map/dot_general | solution.py:81
  368.3 2.8 collective-permute-done.21
  371.1 6.5 %collective-permute-done.22 = bf16[2,256,384]{2,1,0:T(8,128)(2,1)S(1)} collective-permute-done((bf16[2,256,384]{2,1,0:T(8,128)(2,1)S(1)}, bf16[2,256,384]{2,1,0:T(8,128)(2,1)S(1)}, u32[]{:S(2)}, u32[]{:S(2)}) %collective-permute-start.22) | collective-permute-done | bytes 393248 | tf_op jit(solution)/shard_map/ppermute | solution.py:100
  377.5 3.5 collective-permute-done.23
  381.0 1.9 collective-permute-start.24
  382.9 2.6 collective-permute-start.25
  388.0 4.4 %collective-permute-start.28 = (bf16[2,256,384]{2,1,0:T(8,128)(2,1)S(1)}, bf16[2,256,384]{2,1,0:T(8,128)(2,1)S(1)}, u32[]{:S(2)}, u32[]{:S(2)}) collective-permute-start(bf16[2,256,384]{2,1,0:T(8,128)(2,1)S(1)} %get-tuple-element.119), channel_id=1, source_target_pairs={{0,4},{1,5},{2,6},{3,7},{4,68},{5,69},{6,70},{7,71},{8,8},{9,9},{1... | collective-permute-start | bytes 1179656 | tf_op jit(solution)/shard_map/ppermute | solution.py:100
  406.2 3.3 collective-permute-start.30
  410.2 2.1 collective-permute-start.31
  414.7 2.3 collective-permute-done.29
  417.8 6.3 %collective-permute-done.30 = bf16[2,256,384]{2,1,0:T(8,128)(2,1)S(1)} collective-permute-done((bf16[2,256,384]{2,1,0:T(8,128)(2,1)S(1)}, bf16[2,256,384]{2,1,0:T(8,128)(2,1)S(1)}, u32[]{:S(2)}, u32[]{:S(2)}) %collective-permute-start.30) | collective-permute-done | bytes 393248 | tf_op jit(solution)/shard_map/ppermute | solution.py:100
  (160 shorter events, 86.0 us)
Async XLA Ops:
  6.5 93.1 %all-gather.5.cloned.1.call-start = ((), (), s32[]{:S(2)}) async-start(), calls=%async_computation.5 | async-start | bytes 2228224 | tf_op jit(solution)/shard_map/all_gather | solution.py:46
  8.2 136.1 %all-gather.7.cloned.1.call-start = ((), (), s32[]{:S(2)}) async-start(), calls=%async_computation.6 | async-start | bytes 3538944 | tf_op jit(solution)/shard_map/all_gather | solution.py:55
  40.3 44.7 %all-to-all-start = ((bf16[8,2,256,384]{3,2,1,0:T(8,128)(2,1)}), bf16[8,2,256,384]{3,2,1,0:T(8,128)(2,1)}, u32[]{:S(2)}, u32[]{:S(2)}) async-start(bf16[8,2,256,384]{3,2,1,0:T(8,128)(2,1)} %bitcast.266), calls=%async_computation | async-start | bytes 6291456 | tf_op jit(solution)/shard_map/all_to_all | solution.py:71
  148.7 6.2 %copy-start.19 = (bf16[768,3072]{1,0:T(8,128)(2,1)}, bf16[768,3072]{1,0:T(8,128)(2,1)S(1)}, u32[]{:S(2)}) copy-start(bf16[768,3072]{1,0:T(8,128)(2,1)S(1)} %bitcast_dynamic-update-slice_fusion) | copy-start | bytes 14155780
  161.2 42.2 %all-to-all-start.2 = ((bf16[8,2,256,384]{3,2,1,0:T(8,128)(2,1)}), bf16[8,2,256,384]{3,2,1,0:T(8,128)(2,1)}, u32[]{:S(2)}, u32[]{:S(2)}) async-start(bf16[8,2,256,384]{3,2,1,0:T(8,128)(2,1)} %bitcast.268), calls=%async_computation.2 | async-start | bytes 6291456 | tf_op jit(solution)/shard_map/all_to_all | solution.py:71
  171.1 41.1 %collective-permute-start = (bf16[2,256,384]{2,1,0:T(8,128)(2,1)}, bf16[2,256,384]{2,1,0:T(8,128)(2,1)}, u32[]{:S(2)}, u32[]{:S(2)}) collective-permute-start(bf16[2,256,384]{2,1,0:T(8,128)(2,1)} %get-tuple-element.64), channel_id=1, source_target_pairs={{0,0},{1,1},{2,2},{3,3},{4,64},{5,65},{6,66},{7,67},{8,12},{9,13},... | collective-permute-start | bytes 1179656 | tf_op jit(solution)/shard_map/ppermute | solution.py:100
  175.6 38.7 %collective-permute-start.1 = (bf16[2,256,384]{2,1,0:T(8,128)(2,1)}, bf16[2,256,384]{2,1,0:T(8,128)(2,1)}, u32[]{:S(2)}, u32[]{:S(2)}) collective-permute-start(bf16[2,256,384]{2,1,0:T(8,128)(2,1)} %get-tuple-element.65), channel_id=1, source_target_pairs={{0,32},{1,33},{2,34},{3,35},{4,96},{5,97},{6,98},{7,99},{8,44},{9,... | collective-permute-start | bytes 1179656 | tf_op jit(solution)/shard_map/ppermute | solution.py:100
  175.7 41.4 %collective-permute-start.2 = (bf16[2,256,384]{2,1,0:T(8,128)(2,1)S(1)}, bf16[2,256,384]{2,1,0:T(8,128)(2,1)}, u32[]{:S(2)}, u32[]{:S(2)}) collective-permute-start(bf16[2,256,384]{2,1,0:T(8,128)(2,1)S(1)} %get-tuple-element.66), channel_id=1, source_target_pairs={{0,16},{1,17},{2,18},{3,19},{4,80},{5,81},{6,82},{7,83},{8,28},{9,... | collective-permute-start | bytes 1179656 | tf_op jit(solution)/shard_map/ppermute | solution.py:100
  177.8 48.5 %collective-permute-start.3 = (bf16[2,256,384]{2,1,0:T(8,128)(2,1)}, bf16[2,256,384]{2,1,0:T(8,128)(2,1)}, u32[]{:S(2)}, u32[]{:S(2)}) collective-permute-start(bf16[2,256,384]{2,1,0:T(8,128)(2,1)} %get-tuple-element.67), channel_id=1, source_target_pairs={{0,48},{1,49},{2,50},{3,51},{4,112},{5,113},{6,114},{7,115},{8,60}... | collective-permute-start | bytes 1179656 | tf_op jit(solution)/shard_map/ppermute | solution.py:100
  178.1 48.2 %collective-permute-start.4 = (bf16[2,256,384]{2,1,0:T(8,128)(2,1)}, bf16[2,256,384]{2,1,0:T(8,128)(2,1)}, u32[]{:S(2)}, u32[]{:S(2)}) collective-permute-start(bf16[2,256,384]{2,1,0:T(8,128)(2,1)} %get-tuple-element.68), channel_id=1, source_target_pairs={{0,4},{1,5},{2,6},{3,7},{4,68},{5,69},{6,70},{7,71},{8,8},{9,9},{1... | collective-permute-start | bytes 1179656 | tf_op jit(solution)/shard_map/ppermute | solution.py:100
  212.3 14.1 %collective-permute-start.5 = (bf16[2,256,384]{2,1,0:T(8,128)(2,1)}, bf16[2,256,384]{2,1,0:T(8,128)(2,1)}, u32[]{:S(2)}, u32[]{:S(2)}) collective-permute-start(bf16[2,256,384]{2,1,0:T(8,128)(2,1)} %get-tuple-element.69), channel_id=1, source_target_pairs={{0,36},{1,37},{2,38},{3,39},{4,100},{5,101},{6,102},{7,103},{8,40}... | collective-permute-start | bytes 1179656 | tf_op jit(solution)/shard_map/ppermute | solution.py:100
  214.3 14.4 %collective-permute-start.6 = (bf16[2,256,384]{2,1,0:T(8,128)(2,1)}, bf16[2,256,384]{2,1,0:T(8,128)(2,1)}, u32[]{:S(2)}, u32[]{:S(2)}) collective-permute-start(bf16[2,256,384]{2,1,0:T(8,128)(2,1)} %get-tuple-element.70), channel_id=1, source_target_pairs={{0,20},{1,21},{2,22},{3,23},{4,84},{5,85},{6,86},{7,87},{8,24},{9,... | collective-permute-start | bytes 1179656 | tf_op jit(solution)/shard_map/ppermute | solution.py:100
  217.1 15.1 %collective-permute-start.7 = (bf16[2,256,384]{2,1,0:T(8,128)(2,1)}, bf16[2,256,384]{2,1,0:T(8,128)(2,1)}, u32[]{:S(2)}, u32[]{:S(2)}) collective-permute-start(bf16[2,256,384]{2,1,0:T(8,128)(2,1)} %get-tuple-element.71), channel_id=1, source_target_pairs={{0,52},{1,53},{2,54},{3,55},{4,116},{5,117},{6,118},{7,119},{8,56}... | collective-permute-start | bytes 1179656 | tf_op jit(solution)/shard_map/ppermute | solution.py:100
  236.8 41.7 %all-to-all-start.3 = ((bf16[8,2,256,384]{3,2,1,0:T(8,128)(2,1)}), bf16[8,2,256,384]{3,2,1,0:T(8,128)(2,1)}, u32[]{:S(2)}, u32[]{:S(2)}) async-start(bf16[8,2,256,384]{3,2,1,0:T(8,128)(2,1)} %bitcast.263), calls=%async_computation.3 | async-start | bytes 6291456 | tf_op jit(solution)/shard_map/all_to_all | solution.py:71
  244.6 42.8 %collective-permute-start.10 = (bf16[2,256,384]{2,1,0:T(8,128)(2,1)}, bf16[2,256,384]{2,1,0:T(8,128)(2,1)S(1)}, u32[]{:S(2)}, u32[]{:S(2)}) collective-permute-start(bf16[2,256,384]{2,1,0:T(8,128)(2,1)} %get-tuple-element.83), channel_id=1, source_target_pairs={{0,16},{1,17},{2,18},{3,19},{4,80},{5,81},{6,82},{7,83},{8,28},{9,... | collective-permute-start | bytes 1179656 | tf_op jit(solution)/shard_map/ppermute | solution.py:100
  246.3 43.5 %collective-permute-start.11 = (bf16[2,256,384]{2,1,0:T(8,128)(2,1)}, bf16[2,256,384]{2,1,0:T(8,128)(2,1)S(1)}, u32[]{:S(2)}, u32[]{:S(2)}) collective-permute-start(bf16[2,256,384]{2,1,0:T(8,128)(2,1)} %get-tuple-element.84), channel_id=1, source_target_pairs={{0,48},{1,49},{2,50},{3,51},{4,112},{5,113},{6,114},{7,115},{8,60}... | collective-permute-start | bytes 1179656 | tf_op jit(solution)/shard_map/ppermute | solution.py:100
  246.8 45.7 %collective-permute-start.12 = (bf16[2,256,384]{2,1,0:T(8,128)(2,1)}, bf16[2,256,384]{2,1,0:T(8,128)(2,1)S(1)}, u32[]{:S(2)}, u32[]{:S(2)}) collective-permute-start(bf16[2,256,384]{2,1,0:T(8,128)(2,1)} %get-tuple-element.85), channel_id=1, source_target_pairs={{0,4},{1,5},{2,6},{3,7},{4,68},{5,69},{6,70},{7,71},{8,8},{9,9},{1... | collective-permute-start | bytes 1179656 | tf_op jit(solution)/shard_map/ppermute | solution.py:100
  252.6 48.9 %collective-permute-start.13 = (bf16[2,256,384]{2,1,0:T(8,128)(2,1)}, bf16[2,256,384]{2,1,0:T(8,128)(2,1)}, u32[]{:S(2)}, u32[]{:S(2)}) collective-permute-start(bf16[2,256,384]{2,1,0:T(8,128)(2,1)} %get-tuple-element.86), channel_id=1, source_target_pairs={{0,36},{1,37},{2,38},{3,39},{4,100},{5,101},{6,102},{7,103},{8,40}... | collective-permute-start | bytes 1179656 | tf_op jit(solution)/shard_map/ppermute | solution.py:100
  254.1 47.4 %collective-permute-start.14 = (bf16[2,256,384]{2,1,0:T(8,128)(2,1)}, bf16[2,256,384]{2,1,0:T(8,128)(2,1)}, u32[]{:S(2)}, u32[]{:S(2)}) collective-permute-start(bf16[2,256,384]{2,1,0:T(8,128)(2,1)} %get-tuple-element.87), channel_id=1, source_target_pairs={{0,20},{1,21},{2,22},{3,23},{4,84},{5,85},{6,86},{7,87},{8,24},{9,... | collective-permute-start | bytes 1179656 | tf_op jit(solution)/shard_map/ppermute | solution.py:100
  278.6 8.9 %copy-start.2 = (bf16[2,256,384]{2,1,0:T(8,128)(2,1)S(1)}, bf16[2,256,384]{2,1,0:T(8,128)(2,1)}, u32[]{:S(2)}) copy-start(bf16[2,256,384]{2,1,0:T(8,128)(2,1)} %get-tuple-element.88) | copy-start | bytes 1179652
  278.6 11.2 %copy-start.1 = (bf16[2,256,384]{2,1,0:T(8,128)(2,1)S(1)}, bf16[2,256,384]{2,1,0:T(8,128)(2,1)}, u32[]{:S(2)}) copy-start(bf16[2,256,384]{2,1,0:T(8,128)(2,1)} %get-tuple-element.81) | copy-start | bytes 1179652
  287.5 7.0 %copy-start.7 = (bf16[2,256,384]{2,1,0:T(8,128)(2,1)}, bf16[2,256,384]{2,1,0:T(8,128)(2,1)S(1)}, u32[]{:S(2)}) copy-start(bf16[2,256,384]{2,1,0:T(8,128)(2,1)S(1)} %collective-permute-done.10) | copy-start | bytes 1179652
  287.5 14.0 %collective-permute-start.15 = (bf16[2,256,384]{2,1,0:T(8,128)(2,1)S(1)}, bf16[2,256,384]{2,1,0:T(8,128)(2,1)S(1)}, u32[]{:S(2)}, u32[]{:S(2)}) collective-permute-start(bf16[2,256,384]{2,1,0:T(8,128)(2,1)S(1)} %copy-done.2), channel_id=1, source_target_pairs={{0,52},{1,53},{2,54},{3,55},{4,116},{5,117},{6,118},{7,119},{8,56}... | collective-permute-start | bytes 1179656 | tf_op jit(solution)/shard_map/ppermute | solution.py:100
  289.8 4.7 %copy-start.9 = (bf16[2,256,384]{2,1,0:T(8,128)(2,1)}, bf16[2,256,384]{2,1,0:T(8,128)(2,1)S(1)}, u32[]{:S(2)}) copy-start(bf16[2,256,384]{2,1,0:T(8,128)(2,1)S(1)} %collective-permute-done.11) | copy-start | bytes 1179652
  289.8 11.7 %collective-permute-start.8 = (bf16[2,256,384]{2,1,0:T(8,128)(2,1)S(1)}, bf16[2,256,384]{2,1,0:T(8,128)(2,1)S(1)}, u32[]{:S(2)}, u32[]{:S(2)}) collective-permute-start(bf16[2,256,384]{2,1,0:T(8,128)(2,1)S(1)} %copy-done.1), channel_id=1, source_target_pairs={{0,0},{1,1},{2,2},{3,3},{4,64},{5,65},{6,66},{7,67},{8,12},{9,13},... | collective-permute-start | bytes 1179656 | tf_op jit(solution)/shard_map/ppermute | solution.py:100
  292.5 2.0 copy-start.11
  292.5 13.4 %collective-permute-start.9 = (bf16[2,256,384]{2,1,0:T(8,128)(2,1)S(1)}, bf16[2,256,384]{2,1,0:T(8,128)(2,1)S(1)}, u32[]{:S(2)}, u32[]{:S(2)}) collective-permute-start(bf16[2,256,384]{2,1,0:T(8,128)(2,1)S(1)} %get-tuple-element.82), channel_id=1, source_target_pairs={{0,32},{1,33},{2,34},{3,35},{4,96},{5,97},{6,98},{7,99},{8,44},{9,... | collective-permute-start | bytes 1179656 | tf_op jit(solution)/shard_map/ppermute | solution.py:100
  299.7 6.9 %copy-start = (bf16[256,6144]{0,1:T(8,128)(2,1)S(1)}, bf16[256,6144]{0,1:T(8,128)(2,1)}, u32[]{:S(2)}) copy-start(bf16[256,6144]{0,1:T(8,128)(2,1)} %copy.144) | copy-start | bytes 9437188
  301.5 4.4 %copy-start.13 = (bf16[2,256,384]{2,1,0:T(8,128)(2,1)}, bf16[2,256,384]{2,1,0:T(8,128)(2,1)S(1)}, u32[]{:S(2)}) copy-start(bf16[2,256,384]{2,1,0:T(8,128)(2,1)S(1)} %collective-permute-done.15) | copy-start | bytes 1179652
  301.5 4.3 %copy-start.15 = (bf16[2,256,384]{2,1,0:T(8,128)(2,1)}, bf16[2,256,384]{2,1,0:T(8,128)(2,1)S(1)}, u32[]{:S(2)}) copy-start(bf16[2,256,384]{2,1,0:T(8,128)(2,1)S(1)} %collective-permute-done.8) | copy-start | bytes 1179652
  305.9 0.7 copy-start.17
  309.4 45.0 %all-to-all-start.4 = ((bf16[8,2,256,384]{3,2,1,0:T(8,128)(2,1)}), bf16[8,2,256,384]{3,2,1,0:T(8,128)(2,1)S(1)}, u32[]{:S(2)}, u32[]{:S(2)}) async-start(bf16[8,2,256,384]{3,2,1,0:T(8,128)(2,1)} %bitcast.267), calls=%async_computation.4 | async-start | bytes 6291456 | tf_op jit(solution)/shard_map/all_to_all | solution.py:71
  321.8 19.7 %copy-start.6 = (bf16[2,256,384]{2,1,0:T(8,128)(2,1)S(1)}, bf16[2,256,384]{2,1,0:T(8,128)(2,1)}, u32[]{:S(2)}) copy-start(bf16[2,256,384]{2,1,0:T(8,128)(2,1)} %get-tuple-element.102) | copy-start | bytes 1179652
  321.8 24.4 %copy-start.16 = (bf16[2,256,384]{2,1,0:T(8,128)(2,1)S(1)}, bf16[2,256,384]{2,1,0:T(8,128)(2,1)}, u32[]{:S(2)}) copy-start(bf16[2,256,384]{2,1,0:T(8,128)(2,1)} %copy-done.15) | copy-start | bytes 1179652
  321.8 25.2 %copy-start.18 = (bf16[2,256,384]{2,1,0:T(8,128)(2,1)S(1)}, bf16[2,256,384]{2,1,0:T(8,128)(2,1)}, u32[]{:S(2)}) copy-start(bf16[2,256,384]{2,1,0:T(8,128)(2,1)} %copy-done.17) | copy-start | bytes 1179652
  321.8 26.0 %copy-start.8 = (bf16[2,256,384]{2,1,0:T(8,128)(2,1)S(1)}, bf16[2,256,384]{2,1,0:T(8,128)(2,1)}, u32[]{:S(2)}) copy-start(bf16[2,256,384]{2,1,0:T(8,128)(2,1)} %copy-done.7) | copy-start | bytes 1179652
  332.6 16.0 %copy-start.10 = (bf16[2,256,384]{2,1,0:T(8,128)(2,1)S(1)}, bf16[2,256,384]{2,1,0:T(8,128)(2,1)}, u32[]{:S(2)}) copy-start(bf16[2,256,384]{2,1,0:T(8,128)(2,1)} %copy-done.9) | copy-start | bytes 1179652
  332.6 16.8 %copy-start.12 = (bf16[2,256,384]{2,1,0:T(8,128)(2,1)S(1)}, bf16[2,256,384]{2,1,0:T(8,128)(2,1)}, u32[]{:S(2)}) copy-start(bf16[2,256,384]{2,1,0:T(8,128)(2,1)} %copy-done.11) | copy-start | bytes 1179652
  332.6 21.1 %copy-start.14 = (bf16[2,256,384]{2,1,0:T(8,128)(2,1)S(1)}, bf16[2,256,384]{2,1,0:T(8,128)(2,1)}, u32[]{:S(2)}) copy-start(bf16[2,256,384]{2,1,0:T(8,128)(2,1)} %copy-done.13) | copy-start | bytes 1179652
  334.5 20.9 %collective-permute-start.16 = (bf16[2,256,384]{2,1,0:T(8,128)(2,1)}, bf16[2,256,384]{2,1,0:T(8,128)(2,1)}, u32[]{:S(2)}, u32[]{:S(2)}) collective-permute-start(bf16[2,256,384]{2,1,0:T(8,128)(2,1)} %get-tuple-element.98), channel_id=1, source_target_pairs={{0,0},{1,1},{2,2},{3,3},{4,64},{5,65},{6,66},{7,67},{8,12},{9,13},... | collective-permute-start | bytes 1179656 | tf_op jit(solution)/shard_map/ppermute | solution.py:100
  336.4 21.3 %collective-permute-start.17 = (bf16[2,256,384]{2,1,0:T(8,128)(2,1)}, bf16[2,256,384]{2,1,0:T(8,128)(2,1)}, u32[]{:S(2)}, u32[]{:S(2)}) collective-permute-start(bf16[2,256,384]{2,1,0:T(8,128)(2,1)} %get-tuple-element.99), channel_id=1, source_target_pairs={{0,32},{1,33},{2,34},{3,35},{4,96},{5,97},{6,98},{7,99},{8,44},{9,... | collective-permute-start | bytes 1179656 | tf_op jit(solution)/shard_map/ppermute | solution.py:100
  339.9 21.7 %collective-permute-start.18 = (bf16[2,256,384]{2,1,0:T(8,128)(2,1)}, bf16[2,256,384]{2,1,0:T(8,128)(2,1)}, u32[]{:S(2)}, u32[]{:S(2)}) collective-permute-start(bf16[2,256,384]{2,1,0:T(8,128)(2,1)} %get-tuple-element.100), channel_id=1, source_target_pairs={{0,16},{1,17},{2,18},{3,19},{4,80},{5,81},{6,82},{7,83},{8,28},{9,... | collective-permute-start | bytes 1179656 | tf_op jit(solution)/shard_map/ppermute | solution.py:100
  340.9 27.4 %collective-permute-start.19 = (bf16[2,256,384]{2,1,0:T(8,128)(2,1)}, bf16[2,256,384]{2,1,0:T(8,128)(2,1)}, u32[]{:S(2)}, u32[]{:S(2)}) collective-permute-start(bf16[2,256,384]{2,1,0:T(8,128)(2,1)} %get-tuple-element.101), channel_id=1, source_target_pairs={{0,48},{1,49},{2,50},{3,51},{4,112},{5,113},{6,114},{7,115},{8,60}... | collective-permute-start | bytes 1179656 | tf_op jit(solution)/shard_map/ppermute | solution.py:100
  341.5 26.8 %collective-permute-start.20 = (bf16[2,256,384]{2,1,0:T(8,128)(2,1)S(1)}, bf16[2,256,384]{2,1,0:T(8,128)(2,1)}, u32[]{:S(2)}, u32[]{:S(2)}) collective-permute-start(bf16[2,256,384]{2,1,0:T(8,128)(2,1)S(1)} %copy-done.6), channel_id=1, source_target_pairs={{0,4},{1,5},{2,6},{3,7},{4,68},{5,69},{6,70},{7,71},{8,8},{9,9},{1... | collective-permute-start | bytes 1179656 | tf_op jit(solution)/shard_map/ppermute | solution.py:100
  354.5 1.0 copy-start.5
  354.5 3.2 copy-start.4
  354.5 7.2 %copy-start.3 = (bf16[2,256,384]{2,1,0:T(8,128)(2,1)S(1)}, bf16[2,256,384]{2,1,0:T(8,128)(2,1)}, u32[]{:S(2)}) copy-start(bf16[2,256,384]{2,1,0:T(8,128)(2,1)} %get-tuple-element.105) | copy-start | bytes 1179652
  355.5 15.6 %collective-permute-start.21 = (bf16[2,256,384]{2,1,0:T(8,128)(2,1)S(1)}, bf16[2,256,384]{2,1,0:T(8,128)(2,1)S(1)}, u32[]{:S(2)}, u32[]{:S(2)}) collective-permute-start(bf16[2,256,384]{2,1,0:T(8,128)(2,1)S(1)} %copy-done.5), channel_id=1, source_target_pairs={{0,36},{1,37},{2,38},{3,39},{4,100},{5,101},{6,102},{7,103},{8,40}... | collective-permute-start | bytes 1179656 | tf_op jit(solution)/shard_map/ppermute | solution.py:100
  357.7 19.8 %collective-permute-start.22 = (bf16[2,256,384]{2,1,0:T(8,128)(2,1)S(1)}, bf16[2,256,384]{2,1,0:T(8,128)(2,1)S(1)}, u32[]{:S(2)}, u32[]{:S(2)}) collective-permute-start(bf16[2,256,384]{2,1,0:T(8,128)(2,1)S(1)} %copy-done.4), channel_id=1, source_target_pairs={{0,20},{1,21},{2,22},{3,23},{4,84},{5,85},{6,86},{7,87},{8,24},{9,... | collective-permute-start | bytes 1179656 | tf_op jit(solution)/shard_map/ppermute | solution.py:100
  361.7 19.4 %collective-permute-start.23 = (bf16[2,256,384]{2,1,0:T(8,128)(2,1)S(1)}, bf16[2,256,384]{2,1,0:T(8,128)(2,1)S(1)}, u32[]{:S(2)}, u32[]{:S(2)}) collective-permute-start(bf16[2,256,384]{2,1,0:T(8,128)(2,1)S(1)} %copy-done.3), channel_id=1, source_target_pairs={{0,52},{1,53},{2,54},{3,55},{4,116},{5,117},{6,118},{7,119},{8,56}... | collective-permute-start | bytes 1179656 | tf_op jit(solution)/shard_map/ppermute | solution.py:100
  381.0 22.7 %collective-permute-start.24 = (bf16[2,256,384]{2,1,0:T(8,128)(2,1)S(1)}, bf16[2,256,384]{2,1,0:T(8,128)(2,1)S(1)}, u32[]{:S(2)}, u32[]{:S(2)}) collective-permute-start(bf16[2,256,384]{2,1,0:T(8,128)(2,1)S(1)} %get-tuple-element.115), channel_id=1, source_target_pairs={{0,0},{1,1},{2,2},{3,3},{4,64},{5,65},{6,66},{7,67},{8,12},{9,13},... | collective-permute-start | bytes 1179656 | tf_op jit(solution)/shard_map/ppermute | solution.py:100
  382.9 23.2 %collective-permute-start.25 = (bf16[2,256,384]{2,1,0:T(8,128)(2,1)S(1)}, bf16[2,256,384]{2,1,0:T(8,128)(2,1)S(1)}, u32[]{:S(2)}, u32[]{:S(2)}) collective-permute-start(bf16[2,256,384]{2,1,0:T(8,128)(2,1)S(1)} %get-tuple-element.116), channel_id=1, source_target_pairs={{0,32},{1,33},{2,34},{3,35},{4,96},{5,97},{6,98},{7,99},{8,44},{9,... | collective-permute-start | bytes 1179656 | tf_op jit(solution)/shard_map/ppermute | solution.py:100
  385.6 24.7 %collective-permute-start.26 = (bf16[2,256,384]{2,1,0:T(8,128)(2,1)S(1)}, bf16[2,256,384]{2,1,0:T(8,128)(2,1)S(1)}, u32[]{:S(2)}, u32[]{:S(2)}) collective-permute-start(bf16[2,256,384]{2,1,0:T(8,128)(2,1)S(1)} %get-tuple-element.117), channel_id=1, source_target_pairs={{0,16},{1,17},{2,18},{3,19},{4,80},{5,81},{6,82},{7,83},{8,28},{9,... | collective-permute-start | bytes 1179656 | tf_op jit(solution)/shard_map/ppermute | solution.py:100
  386.9 26.2 %collective-permute-start.27 = (bf16[2,256,384]{2,1,0:T(8,128)(2,1)S(1)}, bf16[2,256,384]{2,1,0:T(8,128)(2,1)S(1)}, u32[]{:S(2)}, u32[]{:S(2)}) collective-permute-start(bf16[2,256,384]{2,1,0:T(8,128)(2,1)S(1)} %get-tuple-element.118), channel_id=1, source_target_pairs={{0,48},{1,49},{2,50},{3,51},{4,112},{5,113},{6,114},{7,115},{8,60}... | collective-permute-start | bytes 1179656 | tf_op jit(solution)/shard_map/ppermute | solution.py:100
  388.0 25.9 %collective-permute-start.28 = (bf16[2,256,384]{2,1,0:T(8,128)(2,1)S(1)}, bf16[2,256,384]{2,1,0:T(8,128)(2,1)S(1)}, u32[]{:S(2)}, u32[]{:S(2)}) collective-permute-start(bf16[2,256,384]{2,1,0:T(8,128)(2,1)S(1)} %get-tuple-element.119), channel_id=1, source_target_pairs={{0,4},{1,5},{2,6},{3,7},{4,68},{5,69},{6,70},{7,71},{8,8},{9,9},{1... | collective-permute-start | bytes 1179656 | tf_op jit(solution)/shard_map/ppermute | solution.py:100
  403.7 13.3 %collective-permute-start.29 = (bf16[2,256,384]{2,1,0:T(8,128)(2,1)S(1)}, bf16[2,256,384]{2,1,0:T(8,128)(2,1)S(1)}, u32[]{:S(2)}, u32[]{:S(2)}) collective-permute-start(bf16[2,256,384]{2,1,0:T(8,128)(2,1)S(1)} %get-tuple-element.120), channel_id=1, source_target_pairs={{0,36},{1,37},{2,38},{3,39},{4,100},{5,101},{6,102},{7,103},{8,40}... | collective-permute-start | bytes 1179656 | tf_op jit(solution)/shard_map/ppermute | solution.py:100
  406.2 17.9 %collective-permute-start.30 = (bf16[2,256,384]{2,1,0:T(8,128)(2,1)S(1)}, bf16[2,256,384]{2,1,0:T(8,128)(2,1)S(1)}, u32[]{:S(2)}, u32[]{:S(2)}) collective-permute-start(bf16[2,256,384]{2,1,0:T(8,128)(2,1)S(1)} %get-tuple-element.121), channel_id=1, source_target_pairs={{0,20},{1,21},{2,22},{3,23},{4,84},{5,85},{6,86},{7,87},{8,24},{9,... | collective-permute-start | bytes 1179656 | tf_op jit(solution)/shard_map/ppermute | solution.py:100
  410.2 16.1 %collective-permute-start.31 = (bf16[2,256,384]{2,1,0:T(8,128)(2,1)S(1)}, bf16[2,256,384]{2,1,0:T(8,128)(2,1)S(1)}, u32[]{:S(2)}, u32[]{:S(2)}) collective-permute-start(bf16[2,256,384]{2,1,0:T(8,128)(2,1)S(1)} %get-tuple-element.122), channel_id=1, source_target_pairs={{0,52},{1,53},{2,54},{3,55},{4,116},{5,117},{6,118},{7,119},{8,56}... | collective-permute-start | bytes 1179656 | tf_op jit(solution)/shard_map/ppermute | solution.py:100
Sparse Core Ops, SparseCore 0:
  9.8 58.1 all-gather.4
  69.7 74.4 all-gather.6

commit v2 on v0

v2 whole, which is shorter than its diff:
```python
import functools

import jax
import jax.numpy as jnp
from jax import lax
from jax.experimental import pallas as pl
from jax.experimental.pallas import tpu as pltpu
from jax.sharding import Mesh
from jax.sharding import PartitionSpec as P

AXES = ("z", "xl", "c", "xh", "y")
SIZES = (4, 2, 2, 2, 4)
CHUNKS = 4
AHEAD = 5
VMEM = 60 << 20
ANY = pl.BlockSpec(memory_space=pl.ANY)
SMEM = pl.BlockSpec(memory_space=pltpu.SMEM)
BF16 = jnp.bfloat16


def split(value):
    high = lax.reduce_precision(value, 8, 7)
    return high.astype(BF16), (value - high).astype(BF16)


def number(z, xl, c, xh, y):
    return (((z * 2 + xl) * 2 + c) * 2 + xh) * 4 + y


def bits(k):
    return k >> 2, (k >> 1) & 1, k & 1


def pairs(k):
    k2, k1, k0 = bits(k)
    out = []
    for z in range(4):
        for xl in range(2):
            for c in range(2):
                for xh in range(2):
                    for y in range(4):
                        xh2, xl2 = (z >> 1) ^ k2 ^ c, xl ^ k1
                        z2 = xh * 2 + ((z & 1) ^ k0)
                        out.append((number(z, xl, c, xh, y), number(z2, xl2, c, xh2, y)))
    return out


def moved(change):
    out = []
    for z in range(4):
        for xl in range(2):
            for c in range(2):
                for xh in range(2):
                    for y in range(4):
                        out.append((number(z, xl, c, xh, y), number(*change(z, xl, c, xh, y))))
    return out


def start_all(copies):
    for one in copies:
        one.start()
    return copies


def wait_all(copies):
    for one in copies:
        one.wait()


def pack_kernel(i, rows, block, base, out, buf, sems):
    incoming, outgoing = [], []
    for n in range(16):
        c, y, j = n >> 3, (n >> 1) & 3, n & 1
        column = (c * 8 + j * 4 + y) * block
        source = base.at[pl.ds(i * rows, rows), pl.ds(column, block)]
        incoming.append(pltpu.make_async_copy(source, buf.at[n], sems.at[n]))
        outgoing.append(
            pltpu.make_async_copy(buf.at[n], out.at[n >> 1, j], sems.at[16 + n])
        )
    start_all(incoming)
    for one, two in zip(incoming, outgoing):
        one.wait()
        two.start()
    wait_all(outgoing)


def pack(base, i, rows, block):
    size = 8 * 2 * rows * block * 2
    return pl.pallas_call(
        functools.partial(pack_kernel, i, rows, block),
        out_shape=jax.ShapeDtypeStruct((8, 2, rows, block), BF16),
        in_specs=[ANY],
        out_specs=ANY,
        scratch_shapes=[
            pltpu.VMEM((16, rows, block), BF16),
            pltpu.SemaphoreType.DMA((32,)),
        ],
        compiler_params=pltpu.CompilerParams(vmem_limit_bytes=VMEM),
        cost_estimate=pl.CostEstimate(flops=0, bytes_accessed=2 * size, transcendentals=0),
    )(base)


def add_kernel(i, rows, block, picks, part, own, other, r0, r1, r2, r3, *refs):
    outs = refs[:8]
    lbuf, tbuf, rbuf, pbuf, obuf, sems = refs[8:]
    core = picks[32]
    copies = [pltpu.make_async_copy(part, pbuf, sems.at[8])]
    for n in range(8):
        for flip, source in ((0, own), (1, other)):
            lane = pl.multiple_of((core ^ flip) * rows, rows)
            copies.append(
                pltpu.make_async_copy(
                    source.at[n, :, :, pl.ds(i * rows, rows)],
                    lbuf.at[:, picks[24 + n], :, pl.ds(lane, rows)],
                    sems.at[9 + n * 2 + flip],
                )
            )
        source = (r0, r1, r2, r3)[n >> 1]
        for c in range(2):
            copies.append(
                pltpu.make_async_copy(
                    source.at[n & 1, c],
                    rbuf.at[:, :, picks[16 + n], c],
                    sems.at[25 + n * 2 + c],
                )
            )
    wait_all(start_all(copies))
    depth = 8 * lbuf.shape[2]
    for p in range(2):
        tbuf[p] = lbuf[p].reshape(depth, 2 * rows).T

    @pl.loop(0, 8)
    def _(k):
        y = picks[k]
        lanes = pl.ds(pl.multiple_of(picks[8 + k] * block, block), block)
        high, low = tbuf[0], tbuf[1]
        rhigh = rbuf[y, 0, :, :, :, lanes].reshape(depth, block)
        rlow = rbuf[y, 1, :, :, :, lanes].reshape(depth, block)
        dot = functools.partial(jnp.dot, preferred_element_type=jnp.float32)
        delta = dot(high, rhigh) + dot(high, rlow) + dot(low, rhigh)
        for c in range(2):
            stored = pbuf[c * 4 + y, picks[8 + k]].astype(jnp.float32)
            obuf[k, c] = (stored + delta[c * rows : (c + 1) * rows]).astype(BF16)

    wait_all(
        start_all(
            [pltpu.make_async_copy(obuf.at[k], outs[k], sems.at[k]) for k in range(8)]
        )
    )


def add(i, rows, block, picks, part, lefts, rights):
    depth = rights[0].shape[4]
    return pl.pallas_call(
        functools.partial(add_kernel, i, rows, block),
        out_shape=[jax.ShapeDtypeStruct((2, rows, block), BF16)] * 8,
        in_specs=[SMEM] + [ANY] * 7,
        out_specs=[ANY] * 8,
        scratch_shapes=[
            pltpu.VMEM((2, 8, lefts[0].shape[2], 2 * rows), BF16),
            pltpu.VMEM((2, 2 * rows, 8 * lefts[0].shape[2]), BF16),
            pltpu.VMEM((4, 2, 8, 2, depth, 2 * block), BF16),
            pltpu.VMEM((8, 2, rows, block), BF16),
            pltpu.VMEM((8, 2, rows, block), BF16),
            pltpu.SemaphoreType.DMA((41,)),
        ],
        compiler_params=pltpu.CompilerParams(vmem_limit_bytes=VMEM),
        cost_estimate=pl.CostEstimate(
            flops=2 * 16 * rows * block * 768, bytes_accessed=12 << 20, transcendentals=0
        ),
    )(picks, part, *lefts, *rights)


def place_kernel(i, rows, height, slots, *refs):
    got = refs[:8]
    out, buf, sems = refs[-3:]
    incoming, outgoing = [], []
    for k in range(8):
        incoming.append(pltpu.make_async_copy(got[k], buf.at[k], sems.at[k]))
        for c in range(2):
            start = (slots[k] * 2 + c) * height + i * rows
            outgoing.append(
                pltpu.make_async_copy(
                    buf.at[k, c],
                    out.at[pl.ds(pl.multiple_of(start, rows), rows)],
                    sems.at[8 + k * 2 + c],
                )
            )
    start_all(incoming)
    for k in range(8):
        incoming[k].wait()
        start_all(outgoing[2 * k : 2 * k + 2])
    wait_all(outgoing)


def place(i, rows, height, block, slots, got, merged):
    old = [] if merged is None else [merged]
    return pl.pallas_call(
        functools.partial(place_kernel, i, rows, height),
        out_shape=jax.ShapeDtypeStruct((16 * height, block), BF16),
        in_specs=[SMEM] + [ANY] * (8 + len(old)),
        out_specs=ANY,
        scratch_shapes=[
            pltpu.VMEM((8, 2, rows, block), BF16),
            pltpu.SemaphoreType.DMA((24,)),
        ],
        input_output_aliases={9: 0} if old else {},
        compiler_params=pltpu.CompilerParams(vmem_limit_bytes=VMEM),
        cost_estimate=pl.CostEstimate(
            flops=0, bytes_accessed=64 * rows * block, transcendentals=0
        ),
    )(slots, *got, *old)


def body(base, left, right):
    height, width = base.shape
    block = width // 16
    rows = height // CHUNKS
    depth, rank = right.shape[0], left.shape[1]
    z, xl, c, xh, y = (lax.axis_index(n) for n in AXES)
    tie = lax.optimization_barrier

    def across(value, change):
        return lax.ppermute(value, AXES, moved(change))

    rights = jnp.stack(split(right)).reshape(2, depth, 2, 2, 4, block)
    rights = rights.transpose(2, 4, 0, 1, 3, 5).reshape(8, 2 * depth, 2 * block)
    rights = lax.all_to_all(
        jnp.concatenate([rights, rights]), ("xl", "c", "y"), 0, 0, tiled=True
    ).reshape(2, 8, 2 * depth, 2 * block)
    lefts = jnp.stack(split(left.T))
    lefts = jnp.stack(
        [lefts]
        + [
            across(lefts, lambda z, xl, c, xh, y: (z, xl, c, xh, (y - d) % 4))
            for d in (1, 2, 3)
        ]
    )
    packed = [pack(base, i, rows, block) for i in range(CHUNKS)]
    packed[0], lefts, rights = tie((packed[0], lefts, rights))

    def first(i):
        return lax.all_to_all(packed[i], ("c", "y"), 0, 0, tiled=True)

    rights = [rights] + [
        across(rights, lambda z, xl, c, xh, y: ((z - d) % 4, xl, c, xh, y))
        for d in (1, 2, 3)
    ]
    rights = [one.reshape(2, 2, 4, 2, depth, 2 * block) for one in rights]
    far = across(lefts, lambda z, xl, c, xh, y: (z, xl, c, xh ^ 1, y))
    lefts = jnp.concatenate([lefts, far])
    lefts = [lefts, across(lefts, lambda z, xl, c, xh, y: (z, xl, c ^ 1, xh, y))]

    ys, js, zs, ls, slots = [], [], [], [], []
    for k in range(8):
        k2, k1, k0 = bits(k)
        ys.append(((z & 1) ^ k0) * 2 + (xl ^ k1))
        js.append((z >> 1) ^ k2 ^ c)
        zs.append(((z + (k >> 1)) & 3) * 2 + k0)
        ls.append((xh ^ k2) * 4 + ((y + (k & 3)) & 3))
        slots.append(((xh ^ k2 ^ c) * 2 + ((z & 1) ^ k0)) * 2 + (xl ^ k1))
    picks = jnp.stack([*ys, *js, *zs, *ls, c]).astype(jnp.int32)
    slots = jnp.stack(slots).astype(jnp.int32)

    merged = None
    arrived = first(0)
    packed[1], rights = tie((packed[1], rights))
    got, sent = [], add(0, rows, block, picks, arrived, lefts, rights)
    arrived = first(1)
    for i in range(CHUNKS):
        got, sent = tie((got, sent))
        new = [lax.ppermute(sent[k], AXES, pairs(k)) for k in range(8)]
        if got:
            merged = place(i - 1, rows, height, block, slots, got, merged)
        got = new
        if i + 1 < CHUNKS:
            landed = arrived
            if i + 2 < CHUNKS:
                packed[i + 2], landed, new[:AHEAD] = tie(
                    (packed[i + 2], landed, new[:AHEAD])
                )
                arrived = first(i + 2)
            sent = add(i + 1, rows, block, picks, landed, lefts, rights)
    return place(CHUNKS - 1, rows, height, block, slots, got, merged)


def solution(mesh):
    fine = Mesh(mesh.devices.reshape(SIZES), AXES)
    placed = P(("z", "xl", "c"), ("xh", "y"))
    return jax.shard_map(
        body,
        mesh=fine,
        in_specs=(placed, placed, placed),
        out_specs=P(None, AXES),
        check_vma=False,
    )
```

time: 399 us -> 327 us (0.82)
  blocking collectives: 311 us -> 0 us
  starting transfers between devices: 0.01 us -> 118 us
  waiting for transfers between devices: 30.8 us -> 121 us
  Pallas kernels: 0 us -> 69 us
  matrix products: 23.9 us -> 0 us
  between operations: 13.4 us -> 0.71 us
    all_to_all x3 -> x0, blocking collectives: 311 us -> none  [the longest x1 145 us: to_serving(): lax.all_to_all(across, 'row', split_axis=1, concat_axis=0, tiled=True)]
    ppermute x0 -> x40, waiting for transfers between devices: none -> 121 us  [the longest x32 67.4 us: body(): new = [lax.ppermute(sent[k], AXES, pairs(k)) for k in range(8)]]
    ppermute x0 -> x40, starting transfers between devices: none -> 85.9 us  [the longest x32 74.5 us: body(): new = [lax.ppermute(sent[k], AXES, pairs(k)) for k in range(8)]]
    pallas_call x0 -> x12, Pallas kernels: none -> 69 us  [the longest x4 41.8 us: add(): pl.pallas_call(functools.partial(add_kernel, i, rows, block), out_shape=[...]
    all_to_all x0 -> x5, starting transfers between devices: none -> 31.9 us  [the longest x4 25.7 us: first(): return lax.all_to_all(packed[i], ('c', 'y'), 0, 0, tiled=True)]
    all_gather x1 -> x0, waiting for transfers between devices: 30.1 us -> none  [body(): lax.all_gather(right_factor, 'row', axis=0, tiled=True)]
    dot_general x1 -> x0, matrix products: 23.9 us -> none  [body(): jnp.dot(left_cols, lax.all_gather(right_factor, 'row', axis=0, tiled=True...]
    reshape x1, local copies, waits for them, and re-layouts: 7.91 us -> 0.25 us  [body(): rights = rights.transpose(2, 4, 0, 1, 3, 5).reshape(8, 2 * depth, 2 * block)]
  transfers between devices with their start and end apart: 1 -> 45, of which waited for: 1 -> 23; matrix products, arithmetic and copies ran while one was open for 0% -> 2% of each run, Pallas kernels for 0% -> 20%
where the time goes in v2:
time: 327 us; the launch traced here: 325 us
  waiting for transfers between devices  121 us (37%)
  starting transfers between devices  118 us (36%)
  Pallas kernels  69 us (21%)
  local copies, waits for them, and re-layouts  13 us (4%)
  other arithmetic  3.4 us (1%)
    ppermute x32, starting transfers between devices, body(): new = [lax.ppermute(sent[k], AXES, pairs(k)) for k in range(8)]  74.5 us
    ppermute x32, waiting for transfers between devices, body(): new = [lax.ppermute(sent[k], AXES, pairs(k)) for k in range(8)]  67.4 us
    ppermute x8, waiting for transfers between devices, across(): return lax.ppermute(value, AXES, moved(change))  53.8 us
    pallas_call x4, Pallas kernels, add(): pl.pallas_call(functools.partial(add_kernel, i, rows, block), out_shape=[...  41.8 us
    all_to_all x4, starting transfers between devices, first(): return lax.all_to_all(packed[i], ('c', 'y'), 0, 0, tiled=True)  25.7 us
    pallas_call x4, Pallas kernels, place(): pl.pallas_call(functools.partial(place_kernel, i, rows, height), out_shap...  14.1 us
    pallas_call x4, Pallas kernels, pack(): pl.pallas_call(functools.partial(pack_kernel, i, rows, block), out_shape=...  13.1 us
    ppermute x8, starting transfers between devices, across(): return lax.ppermute(value, AXES, moved(change))  11.3 us
  transfers between devices with their start and end apart: 45, of which 23 were waited for; matrix products, arithmetic and copies ran while one was open for 2% of the time, Pallas kernels for 20%

profile of v2, /device:TPU:15, one launch (start us, length us, event | category | flops | bytes accessed | tf_op | source)
XLA Modules:
  0.0 325.1 jit_solution(6691665925658894614)
XLA Ops:
  3.3 6.1 %all-to-all-start = ((bf16[16,32,768]{2,1,0:T(8,128)(2,1)}), bf16[16,32,768]{2,1,0:T(8,128)(2,1)S(1)}, u32[]{:S(2)}, u32[]{:S(2)}) async-start(bf16[16,32,768]{2,1,0:T(8,128)(2,1)} %pad_maximum_fusion), calls=%async_computation | async-start | bytes 1572864 | tf_op jit(solution)/shard_map/all_to_all | solution.py:228
  9.6 1.9 collective-permute-start.1
  12.9 3.3 %shard_map.40 = bf16[8,2,256,384]{3,2,1,0:T(8,128)(2,1)} custom-call(bf16[1024,6144]{1,0:T(8,128)(2,1)} %base.7), custom_call_target="tpu_custom_call" | custom-call | bytes 6291456 | tf_op jit(solution)/shard_map/pallas_call | solution.py:89
  16.2 7.3 %collective-permute-done.1 = bf16[2,32,1024]{2,1,0:T(8,128)(2,1)S(1)} collective-permute-done((bf16[2,32,1024]{2,1,0:T(8,128)(2,1)S(1)}, bf16[2,32,1024]{2,1,0:T(8,128)(2,1)S(1)}, u32[]{:S(2)}, u32[]{:S(2)}) %collective-permute-start.1) | collective-permute-done | bytes 131104 | tf_op jit(solution)/shard_map/ppermute | solution.py:224
  23.5 2.2 collective-permute-done
  27.5 5.8 %all-to-all-start.2 = ((bf16[8,2,256,384]{3,2,1,0:T(8,128)(2,1)}), bf16[8,2,256,384]{3,2,1,0:T(8,128)(2,1)S(1)}, u32[]{:S(2)}, u32[]{:S(2)}) async-start(bf16[8,2,256,384]{3,2,1,0:T(8,128)(2,1)} %shard_map.40), calls=%async_computation.2 | async-start | bytes 6291456 | tf_op jit(solution)/shard_map/all_to_all | solution.py:243
  35.0 3.3 %collective-permute-start.4 = (bf16[2,8,32,768]{3,2,1,0:T(8,128)(2,1)}, bf16[2,8,32,768]{3,2,1,0:T(8,128)(2,1)}, u32[]{:S(2)}, u32[]{:S(2)}) collective-permute-start(bf16[2,8,32,768]{3,2,1,0:T(8,128)(2,1)} %bitcast.55), channel_id=1, source_target_pairs={{0,64},{1,65},{2,66},{3,67},{4,68},{5,69},{6,70},{7,71},{8,72},{9,... | collective-permute-start | bytes 2359304 | tf_op jit(solution)/shard_map/ppermute | solution.py:224
  39.0 3.3 %shard_map.39 = bf16[8,2,256,384]{3,2,1,0:T(8,128)(2,1)} custom-call(bf16[1024,6144]{1,0:T(8,128)(2,1)} %base.7), custom_call_target="tpu_custom_call" | custom-call | bytes 6291456 | tf_op jit(solution)/shard_map/pallas_call | solution.py:89
  42.3 12.8 %collective-permute-done.5 = bf16[2,8,32,768]{3,2,1,0:T(8,128)(2,1)} collective-permute-done((bf16[2,8,32,768]{3,2,1,0:T(8,128)(2,1)}, bf16[2,8,32,768]{3,2,1,0:T(8,128)(2,1)}, u32[]{:S(2)}, u32[]{:S(2)}) %collective-permute-start.5) | collective-permute-done | bytes 786464 | tf_op jit(solution)/shard_map/ppermute | solution.py:224
  55.0 17.7 %collective-permute-done.4 = bf16[2,8,32,768]{3,2,1,0:T(8,128)(2,1)} collective-permute-done((bf16[2,8,32,768]{3,2,1,0:T(8,128)(2,1)}, bf16[2,8,32,768]{3,2,1,0:T(8,128)(2,1)}, u32[]{:S(2)}, u32[]{:S(2)}) %collective-permute-start.4) | collective-permute-done | bytes 786464 | tf_op jit(solution)/shard_map/ppermute | solution.py:224
  72.7 1.7 copy-done.1
  74.5 5.6 %all-to-all-start.1 = ((bf16[8,2,256,384]{3,2,1,0:T(8,128)(2,1)}), bf16[8,2,256,384]{3,2,1,0:T(8,128)(2,1)S(1)}, u32[]{:S(2)}, u32[]{:S(2)}) async-start(bf16[8,2,256,384]{3,2,1,0:T(8,128)(2,1)} %shard_map.39), calls=%async_computation.1 | async-start | bytes 6291456 | tf_op jit(solution)/shard_map/all_to_all | solution.py:243
  81.2 1.9 constant_dynamic-update-slice_fusion.1
  83.1 11.8 %collective-permute-done.6 = bf16[4,2,32,1024]{3,2,1,0:T(8,128)(2,1)S(1)} collective-permute-done((bf16[4,2,32,1024]{3,2,1,0:T(8,128)(2,1)}, bf16[4,2,32,1024]{3,2,1,0:T(8,128)(2,1)S(1)}, u32[]{:S(2)}, u32[]{:S(2)}) %collective-permute-start.6) | collective-permute-done | bytes 524320 | tf_op jit(solution)/shard_map/ppermute | solution.py:224
  97.6 2.0 collective-permute-done.7.other
  99.6 10.4 %shard_map.41 = (bf16[2,256,384]{2,1,0:T(8,128)(2,1)}, bf16[2,256,384]{2,1,0:T(8,128)(2,1)}, bf16[2,256,384]{2,1,0:T(8,128)(2,1)}, bf16[2,256,384]{2,1,0:T(8,128...) custom-call(s32[33]{0:T(128)} %stack.185.picks, ...), custom_call_target="tpu_custom_call" | custom-call | flops 2415919104 | bytes 12582912 | tf_op jit(solution)/shard_map/pallas_call | solution.py:154
  110.1 3.9 %collective-permute-start.8 = (bf16[2,256,384]{2,1,0:T(8,128)(2,1)}, bf16[2,256,384]{2,1,0:T(8,128)(2,1)S(1)}, u32[]{:S(2)}, u32[]{:S(2)}) collective-permute-start(bf16[2,256,384]{2,1,0:T(8,128)(2,1)} %get-tuple-element.115), channel_id=1, source_target_pairs={{0,0},{1,1},{2,2},{3,3},{4,64},{5,65},{6,66},{7,67},{8,12},{9,13},... | collective-permute-start | bytes 1179656 | tf_op jit(solution)/shard_map/ppermute | solution.py:272
  114.9 1.8 collective-permute-start.10
  117.1 5.2 %collective-permute-start.12 = (bf16[2,256,384]{2,1,0:T(8,128)(2,1)}, bf16[2,256,384]{2,1,0:T(8,128)(2,1)}, u32[]{:S(2)}, u32[]{:S(2)}) collective-permute-start(bf16[2,256,384]{2,1,0:T(8,128)(2,1)} %get-tuple-element.119), channel_id=1, source_target_pairs={{0,4},{1,5},{2,6},{3,7},{4,68},{5,69},{6,70},{7,71},{8,8},{9,9},{1... | collective-permute-start | bytes 1179656 | tf_op jit(solution)/shard_map/ppermute | solution.py:272
  122.3 3.3 %shard_map.38 = bf16[8,2,256,384]{3,2,1,0:T(8,128)(2,1)} custom-call(bf16[1024,6144]{1,0:T(8,128)(2,1)} %base.7), custom_call_target="tpu_custom_call" | custom-call | bytes 6291456 | tf_op jit(solution)/shard_map/pallas_call | solution.py:89
  125.6 8.3 %collective-permute-done.9.refs_1_ = bf16[2,256,384]{2,1,0:T(8,128)(2,1)S(1)} collective-permute-done((bf16[2,256,384]{2,1,0:T(8,128)(2,1)}, bf16[2,256,384]{2,1,0:T(8,128)(2,1)S(1)}, u32[]{:S(2)}, u32[]{:S(2)}) %collective-permute-start.9) | collective-permute-done | bytes 393248 | tf_op jit(solution)/shard_map/ppermute | solution.py:272
  133.9 5.3 %collective-permute-done.11.refs_3_ = bf16[2,256,384]{2,1,0:T(8,128)(2,1)} collective-permute-done((bf16[2,256,384]{2,1,0:T(8,128)(2,1)}, bf16[2,256,384]{2,1,0:T(8,128)(2,1)}, u32[]{:S(2)}, u32[]{:S(2)}) %collective-permute-start.11) | collective-permute-done | bytes 393248 | tf_op jit(solution)/shard_map/ppermute | solution.py:272
  139.3 2.1 collective-permute-done.12.refs_4_
  143.0 6.6 %all-to-all-start.3 = ((bf16[8,2,256,384]{3,2,1,0:T(8,128)(2,1)}), bf16[8,2,256,384]{3,2,1,0:T(8,128)(2,1)}, u32[]{:S(2)}, u32[]{:S(2)}) async-start(bf16[8,2,256,384]{3,2,1,0:T(8,128)(2,1)} %shard_map.38), calls=%async_computation.3 | async-start | bytes 6291456 | tf_op jit(solution)/shard_map/all_to_all | solution.py:243
  149.5 2.8 collective-permute-start.13
  153.8 2.7 collective-permute-start.15
  156.4 10.5 %shard_map.42 = (bf16[2,256,384]{2,1,0:T(8,128)(2,1)}, bf16[2,256,384]{2,1,0:T(8,128)(2,1)}, bf16[2,256,384]{2,1,0:T(8,128)(2,1)}, bf16[2,256,384]{2,1,0:T(8,128...) custom-call(s32[33]{0:T(128)} %stack.185.picks, ...), custom_call_target="tpu_custom_call" | custom-call | flops 2415919104 | bytes 12582912 | tf_op jit(solution)/shard_map/pallas_call | solution.py:154
  166.9 2.7 collective-permute-done.15.refs_7_
  169.7 1.9 collective-permute-start.16
  171.6 2.2 collective-permute-start.17
  174.5 2.2 collective-permute-start.19
  176.7 3.8 %collective-permute-start.20 = (bf16[2,256,384]{2,1,0:T(8,128)(2,1)}, bf16[2,256,384]{2,1,0:T(8,128)(2,1)S(1)}, u32[]{:S(2)}, u32[]{:S(2)}) collective-permute-start(bf16[2,256,384]{2,1,0:T(8,128)(2,1)} %get-tuple-element.142), channel_id=1, source_target_pairs={{0,4},{1,5},{2,6},{3,7},{4,68},{5,69},{6,70},{7,71},{8,8},{9,9},{1... | collective-permute-start | bytes 1179656 | tf_op jit(solution)/shard_map/ppermute | solution.py:272
  180.5 3.3 %shard_map.37 = bf16[8,2,256,384]{3,2,1,0:T(8,128)(2,1)} custom-call(bf16[1024,6144]{1,0:T(8,128)(2,1)} %base.7), custom_call_target="tpu_custom_call" | custom-call | bytes 6291456 | tf_op jit(solution)/shard_map/pallas_call | solution.py:89
  183.9 7.0 %collective-permute-done.17.refs_1_ = bf16[2,256,384]{2,1,0:T(8,128)(2,1)S(1)} collective-permute-done((bf16[2,256,384]{2,1,0:T(8,128)(2,1)}, bf16[2,256,384]{2,1,0:T(8,128)(2,1)S(1)}, u32[]{:S(2)}, u32[]{:S(2)}) %collective-permute-start.17) | collective-permute-done | bytes 393248 | tf_op jit(solution)/shard_map/ppermute | solution.py:272
  192.6 7.8 %collective-permute-done.20.refs_4_ = bf16[2,256,384]{2,1,0:T(8,128)(2,1)S(1)} collective-permute-done((bf16[2,256,384]{2,1,0:T(8,128)(2,1)}, bf16[2,256,384]{2,1,0:T(8,128)(2,1)S(1)}, u32[]{:S(2)}, u32[]{:S(2)}) %collective-permute-start.20) | collective-permute-done | bytes 393248 | tf_op jit(solution)/shard_map/ppermute | solution.py:272
  201.1 7.7 %all-to-all-start.4 = ((bf16[8,2,256,384]{3,2,1,0:T(8,128)(2,1)}), bf16[8,2,256,384]{3,2,1,0:T(8,128)(2,1)S(1)}, u32[]{:S(2)}, u32[]{:S(2)}) async-start(bf16[8,2,256,384]{3,2,1,0:T(8,128)(2,1)} %shard_map.37), calls=%async_computation.4 | async-start | bytes 6291456 | tf_op jit(solution)/shard_map/all_to_all | solution.py:243
  208.8 1.7 collective-permute-start.21
  211.6 3.8 %collective-permute-start.23 = (bf16[2,256,384]{2,1,0:T(8,128)(2,1)}, bf16[2,256,384]{2,1,0:T(8,128)(2,1)}, u32[]{:S(2)}, u32[]{:S(2)}) collective-permute-start(bf16[2,256,384]{2,1,0:T(8,128)(2,1)} %get-tuple-element.150), channel_id=1, source_target_pairs={{0,52},{1,53},{2,54},{3,55},{4,116},{5,117},{6,118},{7,119},{8,56}... | collective-permute-start | bytes 1179656 | tf_op jit(solution)/shard_map/ppermute | solution.py:272
  215.4 10.4 %shard_map.43 = (bf16[2,256,384]{2,1,0:T(8,128)(2,1)}, bf16[2,256,384]{2,1,0:T(8,128)(2,1)}, bf16[2,256,384]{2,1,0:T(8,128)(2,1)}, bf16[2,256,384]{2,1,0:T(8,128...) custom-call(s32[33]{0:T(128)} %stack.185.picks, ...), custom_call_target="tpu_custom_call" | custom-call | flops 2415919104 | bytes 12582912 | tf_op jit(solution)/shard_map/pallas_call | solution.py:154
  225.9 2.5 collective-permute-done.23.refs_7_
  228.4 1.9 collective-permute-start.24
  230.3 2.4 collective-permute-start.25
  233.1 2.3 collective-permute-start.27
  235.4 3.7 %collective-permute-start.28 = (bf16[2,256,384]{2,1,0:T(8,128)(2,1)}, bf16[2,256,384]{2,1,0:T(8,128)(2,1)}, u32[]{:S(2)}, u32[]{:S(2)}) collective-permute-start(bf16[2,256,384]{2,1,0:T(8,128)(2,1)} %get-tuple-element.164), channel_id=1, source_target_pairs={{0,4},{1,5},{2,6},{3,7},{4,68},{5,69},{6,70},{7,71},{8,8},{9,9},{1... | collective-permute-start | bytes 1179656 | tf_op jit(solution)/shard_map/ppermute | solution.py:272
  239.1 3.2 collective-permute-done.24.refs_0_
  242.3 2.8 collective-permute-start.29
  245.1 4.6 %collective-permute-done.25.refs_1_ = bf16[2,256,384]{2,1,0:T(8,128)(2,1)S(1)} collective-permute-done((bf16[2,256,384]{2,1,0:T(8,128)(2,1)}, bf16[2,256,384]{2,1,0:T(8,128)(2,1)S(1)}, u32[]{:S(2)}, u32[]{:S(2)}) %collective-permute-start.25) | collective-permute-done | bytes 393248 | tf_op jit(solution)/shard_map/ppermute | solution.py:272
  249.7 2.8 collective-permute-start.30
  253.3 3.9 %collective-permute-start.31 = (bf16[2,256,384]{2,1,0:T(8,128)(2,1)}, bf16[2,256,384]{2,1,0:T(8,128)(2,1)}, u32[]{:S(2)}, u32[]{:S(2)}) collective-permute-start(bf16[2,256,384]{2,1,0:T(8,128)(2,1)} %get-tuple-element.167), channel_id=1, source_target_pairs={{0,52},{1,53},{2,54},{3,55},{4,116},{5,117},{6,118},{7,119},{8,56}... | collective-permute-start | bytes 1179656 | tf_op jit(solution)/shard_map/ppermute | solution.py:272
  258.9 10.4 %shard_map.44 = (bf16[2,256,384]{2,1,0:T(8,128)(2,1)}, bf16[2,256,384]{2,1,0:T(8,128)(2,1)}, bf16[2,256,384]{2,1,0:T(8,128)(2,1)}, bf16[2,256,384]{2,1,0:T(8,128...) custom-call(s32[33]{0:T(128)} %stack.185.picks, ...), custom_call_target="tpu_custom_call" | custom-call | flops 2415919104 | bytes 12582912 | tf_op jit(solution)/shard_map/pallas_call | solution.py:154
  269.3 2.1 collective-permute-done.30.refs_6_
  271.5 3.7 %collective-permute-done.31.refs_7_ = bf16[2,256,384]{2,1,0:T(8,128)(2,1)} collective-permute-done((bf16[2,256,384]{2,1,0:T(8,128)(2,1)}, bf16[2,256,384]{2,1,0:T(8,128)(2,1)}, u32[]{:S(2)}, u32[]{:S(2)}) %collective-permute-start.31) | collective-permute-done | bytes 393248 | tf_op jit(solution)/shard_map/ppermute | solution.py:272
  275.2 1.9 collective-permute-start.32
  277.1 1.9 collective-permute-start.33
  279.2 3.0 collective-permute-start.35
  282.2 3.5 %collective-permute-start.36 = (bf16[2,256,384]{2,1,0:T(8,128)(2,1)}, bf16[2,256,384]{2,1,0:T(8,128)(2,1)S(1)}, u32[]{:S(2)}, u32[]{:S(2)}) collective-permute-start(bf16[2,256,384]{2,1,0:T(8,128)(2,1)} %get-tuple-element.181), channel_id=1, source_target_pairs={{0,4},{1,5},{2,6},{3,7},{4,68},{5,69},{6,70},{7,71},{8,8},{9,9},{1... | collective-permute-start | bytes 1179656 | tf_op jit(solution)/shard_map/ppermute | solution.py:272
  285.7 4.2 %collective-permute-done.32.refs_0_ = bf16[2,256,384]{2,1,0:T(8,128)(2,1)S(1)} collective-permute-done((bf16[2,256,384]{2,1,0:T(8,128)(2,1)}, bf16[2,256,384]{2,1,0:T(8,128)(2,1)S(1)}, u32[]{:S(2)}, u32[]{:S(2)}) %collective-permute-start.32) | collective-permute-done | bytes 393248 | tf_op jit(solution)/shard_map/ppermute | solution.py:272
  291.5 7.2 %collective-permute-done.33.refs_1_ = bf16[2,256,384]{2,1,0:T(8,128)(2,1)S(1)} collective-permute-done((bf16[2,256,384]{2,1,0:T(8,128)(2,1)}, bf16[2,256,384]{2,1,0:T(8,128)(2,1)S(1)}, u32[]{:S(2)}, u32[]{:S(2)}) %collective-permute-start.33) | collective-permute-done | bytes 393248 | tf_op jit(solution)/shard_map/ppermute | solution.py:272
  300.2 4.3 %collective-permute-start.39 = (bf16[2,256,384]{2,1,0:T(8,128)(2,1)}, bf16[2,256,384]{2,1,0:T(8,128)(2,1)S(1)}, u32[]{:S(2)}, u32[]{:S(2)}) collective-permute-start(bf16[2,256,384]{2,1,0:T(8,128)(2,1)} %get-tuple-element.184), channel_id=1, source_target_pairs={{0,52},{1,53},{2,54},{3,55},{4,116},{5,117},{6,118},{7,119},{8,56}... | collective-permute-start | bytes 1179656 | tf_op jit(solution)/shard_map/ppermute | solution.py:272
  305.1 3.5 %shard_map.45.refs_8_ = bf16[16384,384]{1,0:T(8,128)(2,1)} custom-call(s32[8]{0:T(128)} %stack.150.slots, bf16[2,256,384]{2,1,0:T(8,128)(2,1)} %copy-done.4, bf16[2,256,384]{2,1,0:T(8,128)(2,1)} %copy-done.5, bf16[2,256,384]{2,1,0:T(8,128)(2,1)} %collective-permute-done.10.refs_2_, bf16[2,256,384]{2,1,0:T(8,128)(2,1)} %collective-permute-done.11.refs_3_, ...), custom_call_target="tpu_custom_call" | custom-call | bytes 6291456 | tf_op jit(solution)/shard_map/pallas_call | solution.py:198
  308.7 3.5 %shard_map.46.refs_8_ = bf16[16384,384]{1,0:T(8,128)(2,1)} custom-call(s32[8]{0:T(128)} %stack.150.slots, bf16[2,256,384]{2,1,0:T(8,128)(2,1)} %copy-done.9, bf16[2,256,384]{2,1,0:T(8,128)(2,1)} %copy-done.10, bf16[2,256,384]{2,1,0:T(8,128)(2,1)} %copy-done.11, bf16[2,256,384]{2,1,0:T(8,128)(2,1)} %copy-done.12, ...), custom_call_target="tpu_custom_call", output_to_operand_aliasing={{}: (9, {})} | custom-call | bytes 6291456 | tf_op jit(solution)/shard_map/pallas_call | solution.py:198
  312.2 3.5 %shard_map.47.refs_8_ = bf16[16384,384]{1,0:T(8,128)(2,1)} custom-call(s32[8]{0:T(128)} %stack.150.slots, bf16[2,256,384]{2,1,0:T(8,128)(2,1)} %copy-done.16, bf16[2,256,384]{2,1,0:T(8,128)(2,1)} %copy-done.17, bf16[2,256,384]{2,1,0:T(8,128)(2,1)} %copy-done.18, ...), custom_call_target="tpu_custom_call", output_to_operand_aliasing={{}: (9, {})} | custom-call | bytes 6291456 | tf_op jit(solution)/shard_map/pallas_call | solution.py:198
  317.4 3.2 collective-permute-done.39.refs_7_
  321.4 3.5 %shard_map.48 = bf16[16384,384]{1,0:T(8,128)(2,1)} custom-call(s32[8]{0:T(128)} %stack.150.slots, bf16[2,256,384]{2,1,0:T(8,128)(2,1)} %copy-done.19, bf16[2,256,384]{2,1,0:T(8,128)(2,1)} %copy-done.20, bf16[2,256,384]{2,1,0:T(8,128)(2,1)} %copy-done.21, bf16[2,256,384]{2,1,0:T(8,128)(2,1)} %copy-done.22, ...), custom_call_target="tpu_custom_call", output_to_operand_aliasing={{}: (9, {})} | custom-call | bytes 6291456 | tf_op jit(solution)/shard_map/pallas_call | solution.py:198
  (109 shorter events, 30.6 us)
Async XLA Ops:
  1.0 8.5 %copy-start.27 = (f32[1024,32]{0,1:T(8,128)S(1)}, f32[1024,32]{0,1:T(8,128)}, u32[]{:S(2)}) copy-start(f32[1024,32]{0,1:T(8,128)} %param.4) | copy-start | bytes 393220
  3.3 23.2 %all-to-all-start = ((bf16[16,32,768]{2,1,0:T(8,128)(2,1)}), bf16[16,32,768]{2,1,0:T(8,128)(2,1)S(1)}, u32[]{:S(2)}, u32[]{:S(2)}) async-start(bf16[16,32,768]{2,1,0:T(8,128)(2,1)} %pad_maximum_fusion), calls=%async_computation | async-start | bytes 1572864 | tf_op jit(solution)/shard_map/all_to_all | solution.py:228
  9.6 14.0 %collective-permute-start.1 = (bf16[2,32,1024]{2,1,0:T(8,128)(2,1)S(1)}, bf16[2,32,1024]{2,1,0:T(8,128)(2,1)S(1)}, u32[]{:S(2)}, u32[]{:S(2)}) collective-permute-start(bf16[2,32,1024]{2,1,0:T(8,128)(2,1)S(1)} %get-tuple-element.212), channel_id=1, source_target_pairs={{0,2},{1,3},{2,0},{3,1},{4,6},{5,7},{6,4},{7,5},{8,10},{9,11},{10,... | collective-permute-start | bytes 393224 | tf_op jit(solution)/shard_map/ppermute | solution.py:224
  11.4 14.3 %collective-permute-start = (bf16[2,32,1024]{2,1,0:T(8,128)(2,1)S(1)}, bf16[2,32,1024]{2,1,0:T(8,128)(2,1)S(1)}, u32[]{:S(2)}, u32[]{:S(2)}) collective-permute-start(bf16[2,32,1024]{2,1,0:T(8,128)(2,1)S(1)} %get-tuple-element.212), channel_id=1, source_target_pairs={{0,3},{1,0},{2,1},{3,2},{4,7},{5,4},{6,5},{7,6},{8,11},{9,8},{10,9... | collective-permute-start | bytes 393224 | tf_op jit(solution)/shard_map/ppermute | solution.py:224
  12.6 13.1 %collective-permute-start.2 = (bf16[2,32,1024]{2,1,0:T(8,128)(2,1)S(1)}, bf16[2,32,1024]{2,1,0:T(8,128)(2,1)S(1)}, u32[]{:S(2)}, u32[]{:S(2)}) collective-permute-start(bf16[2,32,1024]{2,1,0:T(8,128)(2,1)S(1)} %get-tuple-element.212), channel_id=1, source_target_pairs={{0,1},{1,2},{2,3},{3,0},{4,5},{5,6},{6,7},{7,4},{8,9},{9,10},{10,1... | collective-permute-start | bytes 393224 | tf_op jit(solution)/shard_map/ppermute | solution.py:224
  27.5 45.3 %all-to-all-start.2 = ((bf16[8,2,256,384]{3,2,1,0:T(8,128)(2,1)}), bf16[8,2,256,384]{3,2,1,0:T(8,128)(2,1)S(1)}, u32[]{:S(2)}, u32[]{:S(2)}) async-start(bf16[8,2,256,384]{3,2,1,0:T(8,128)(2,1)} %shard_map.40), calls=%async_computation.2 | async-start | bytes 6291456 | tf_op jit(solution)/shard_map/all_to_all | solution.py:243
  33.3 21.7 %collective-permute-start.5 = (bf16[2,8,32,768]{3,2,1,0:T(8,128)(2,1)}, bf16[2,8,32,768]{3,2,1,0:T(8,128)(2,1)}, u32[]{:S(2)}, u32[]{:S(2)}) collective-permute-start(bf16[2,8,32,768]{3,2,1,0:T(8,128)(2,1)} %bitcast.54), channel_id=1, source_target_pairs={{0,32},{1,33},{2,34},{3,35},{4,36},{5,37},{6,38},{7,39},{8,40},{9,... | collective-permute-start | bytes 2359304 | tf_op jit(solution)/shard_map/ppermute | solution.py:224
  35.0 37.8 %collective-permute-start.4 = (bf16[2,8,32,768]{3,2,1,0:T(8,128)(2,1)}, bf16[2,8,32,768]{3,2,1,0:T(8,128)(2,1)}, u32[]{:S(2)}, u32[]{:S(2)}) collective-permute-start(bf16[2,8,32,768]{3,2,1,0:T(8,128)(2,1)} %bitcast.55), channel_id=1, source_target_pairs={{0,64},{1,65},{2,66},{3,67},{4,68},{5,69},{6,70},{7,71},{8,72},{9,... | collective-permute-start | bytes 2359304 | tf_op jit(solution)/shard_map/ppermute | solution.py:224
  38.3 34.5 %collective-permute-start.3 = (bf16[2,8,32,768]{3,2,1,0:T(8,128)(2,1)}, bf16[2,8,32,768]{3,2,1,0:T(8,128)(2,1)}, u32[]{:S(2)}, u32[]{:S(2)}) collective-permute-start(bf16[2,8,32,768]{3,2,1,0:T(8,128)(2,1)} %bitcast.56), channel_id=1, source_target_pairs={{0,96},{1,97},{2,98},{3,99},{4,100},{5,101},{6,102},{7,103},{8,104... | collective-permute-start | bytes 2359304 | tf_op jit(solution)/shard_map/ppermute | solution.py:224
  74.5 66.8 %all-to-all-start.1 = ((bf16[8,2,256,384]{3,2,1,0:T(8,128)(2,1)}), bf16[8,2,256,384]{3,2,1,0:T(8,128)(2,1)S(1)}, u32[]{:S(2)}, u32[]{:S(2)}) async-start(bf16[8,2,256,384]{3,2,1,0:T(8,128)(2,1)} %shard_map.39), calls=%async_computation.1 | async-start | bytes 6291456 | tf_op jit(solution)/shard_map/all_to_all | solution.py:243
  80.1 14.9 %collective-permute-start.6 = (bf16[4,2,32,1024]{3,2,1,0:T(8,128)(2,1)}, bf16[4,2,32,1024]{3,2,1,0:T(8,128)(2,1)S(1)}, u32[]{:S(2)}, u32[]{:S(2)}) collective-permute-start(bf16[4,2,32,1024]{3,2,1,0:T(8,128)(2,1)} %pad_maximum_fusion.1), channel_id=1, source_target_pairs={{0,4},{1,5},{2,6},{3,7},{4,0},{5,1},{6,2},{7,3},{8,12},{9,13},{10,... | collective-permute-start | bytes 1572872 | tf_op jit(solution)/shard_map/ppermute | solution.py:224
  95.8 3.8 %collective-permute-start.7 = (bf16[8,2,32,1024]{3,2,1,0:T(8,128)(2,1)}, bf16[8,2,32,1024]{3,2,1,0:T(8,128)(2,1)}, u32[]{:S(2)}, u32[]{:S(2)}) collective-permute-start(bf16[8,2,32,1024]{3,2,1,0:T(8,128)(2,1)} %constant_dynamic-update-slice_fusion.own), channel_id=1, source_target_pairs={{0,8},{1,9},{2,10},{3,11},{4,12},{5,13},{6,14},{7,15},{8,0},{9,1},... | collective-permute-start | bytes 3145736 | tf_op jit(solution)/shard_map/ppermute | solution.py:224
  110.1 15.5 %collective-permute-start.8 = (bf16[2,256,384]{2,1,0:T(8,128)(2,1)}, bf16[2,256,384]{2,1,0:T(8,128)(2,1)S(1)}, u32[]{:S(2)}, u32[]{:S(2)}) collective-permute-start(bf16[2,256,384]{2,1,0:T(8,128)(2,1)} %get-tuple-element.115), channel_id=1, source_target_pairs={{0,0},{1,1},{2,2},{3,3},{4,64},{5,65},{6,66},{7,67},{8,12},{9,13},... | collective-permute-start | bytes 1179656 | tf_op jit(solution)/shard_map/ppermute | solution.py:272
  113.9 20.0 %collective-permute-start.9 = (bf16[2,256,384]{2,1,0:T(8,128)(2,1)}, bf16[2,256,384]{2,1,0:T(8,128)(2,1)S(1)}, u32[]{:S(2)}, u32[]{:S(2)}) collective-permute-start(bf16[2,256,384]{2,1,0:T(8,128)(2,1)} %get-tuple-element.116), channel_id=1, source_target_pairs={{0,32},{1,33},{2,34},{3,35},{4,96},{5,97},{6,98},{7,99},{8,44},{9,... | collective-permute-start | bytes 1179656 | tf_op jit(solution)/shard_map/ppermute | solution.py:272
  114.9 19.0 %collective-permute-start.10 = (bf16[2,256,384]{2,1,0:T(8,128)(2,1)}, bf16[2,256,384]{2,1,0:T(8,128)(2,1)}, u32[]{:S(2)}, u32[]{:S(2)}) collective-permute-start(bf16[2,256,384]{2,1,0:T(8,128)(2,1)} %get-tuple-element.117), channel_id=1, source_target_pairs={{0,16},{1,17},{2,18},{3,19},{4,80},{5,81},{6,82},{7,83},{8,28},{9,... | collective-permute-start | bytes 1179656 | tf_op jit(solution)/shard_map/ppermute | solution.py:272
  116.7 22.5 %collective-permute-start.11 = (bf16[2,256,384]{2,1,0:T(8,128)(2,1)}, bf16[2,256,384]{2,1,0:T(8,128)(2,1)}, u32[]{:S(2)}, u32[]{:S(2)}) collective-permute-start(bf16[2,256,384]{2,1,0:T(8,128)(2,1)} %get-tuple-element.118), channel_id=1, source_target_pairs={{0,48},{1,49},{2,50},{3,51},{4,112},{5,113},{6,114},{7,115},{8,60}... | collective-permute-start | bytes 1179656 | tf_op jit(solution)/shard_map/ppermute | solution.py:272
  117.1 24.2 %collective-permute-start.12 = (bf16[2,256,384]{2,1,0:T(8,128)(2,1)}, bf16[2,256,384]{2,1,0:T(8,128)(2,1)}, u32[]{:S(2)}, u32[]{:S(2)}) collective-permute-start(bf16[2,256,384]{2,1,0:T(8,128)(2,1)} %get-tuple-element.119), channel_id=1, source_target_pairs={{0,4},{1,5},{2,6},{3,7},{4,68},{5,69},{6,70},{7,71},{8,8},{9,9},{1... | collective-permute-start | bytes 1179656 | tf_op jit(solution)/shard_map/ppermute | solution.py:272
  125.6 15.7 %copy-start.4 = (bf16[2,256,384]{2,1,0:T(8,128)(2,1)}, bf16[2,256,384]{2,1,0:T(8,128)(2,1)S(1)}, u32[]{:S(2)}) copy-start(bf16[2,256,384]{2,1,0:T(8,128)(2,1)S(1)} %collective-permute-done.8.refs_0_) | copy-start | bytes 1179652
  133.9 5.4 %copy-start.5 = (bf16[2,256,384]{2,1,0:T(8,128)(2,1)}, bf16[2,256,384]{2,1,0:T(8,128)(2,1)S(1)}, u32[]{:S(2)}) copy-start(bf16[2,256,384]{2,1,0:T(8,128)(2,1)S(1)} %collective-permute-done.9.refs_1_) | copy-start | bytes 1179652
  143.0 57.4 %all-to-all-start.3 = ((bf16[8,2,256,384]{3,2,1,0:T(8,128)(2,1)}), bf16[8,2,256,384]{3,2,1,0:T(8,128)(2,1)}, u32[]{:S(2)}, u32[]{:S(2)}) async-start(bf16[8,2,256,384]{3,2,1,0:T(8,128)(2,1)} %shard_map.38), calls=%async_computation.3 | async-start | bytes 6291456 | tf_op jit(solution)/shard_map/all_to_all | solution.py:243
  149.5 17.3 %collective-permute-start.13 = (bf16[2,256,384]{2,1,0:T(8,128)(2,1)}, bf16[2,256,384]{2,1,0:T(8,128)(2,1)S(1)}, u32[]{:S(2)}, u32[]{:S(2)}) collective-permute-start(bf16[2,256,384]{2,1,0:T(8,128)(2,1)} %get-tuple-element.126), channel_id=1, source_target_pairs={{0,36},{1,37},{2,38},{3,39},{4,100},{5,101},{6,102},{7,103},{8,40}... | collective-permute-start | bytes 1179656 | tf_op jit(solution)/shard_map/ppermute | solution.py:272
  152.3 14.6 %collective-permute-start.14 = (bf16[2,256,384]{2,1,0:T(8,128)(2,1)}, bf16[2,256,384]{2,1,0:T(8,128)(2,1)S(1)}, u32[]{:S(2)}, u32[]{:S(2)}) collective-permute-start(bf16[2,256,384]{2,1,0:T(8,128)(2,1)} %get-tuple-element.127), channel_id=1, source_target_pairs={{0,20},{1,21},{2,22},{3,23},{4,84},{5,85},{6,86},{7,87},{8,24},{9,... | collective-permute-start | bytes 1179656 | tf_op jit(solution)/shard_map/ppermute | solution.py:272
  153.8 15.9 %collective-permute-start.15 = (bf16[2,256,384]{2,1,0:T(8,128)(2,1)}, bf16[2,256,384]{2,1,0:T(8,128)(2,1)S(1)}, u32[]{:S(2)}, u32[]{:S(2)}) collective-permute-start(bf16[2,256,384]{2,1,0:T(8,128)(2,1)} %get-tuple-element.128), channel_id=1, source_target_pairs={{0,52},{1,53},{2,54},{3,55},{4,116},{5,117},{6,118},{7,119},{8,56}... | collective-permute-start | bytes 1179656 | tf_op jit(solution)/shard_map/ppermute | solution.py:272
  166.9 16.9 %copy-start.6 = (bf16[2,256,384]{2,1,0:T(8,128)(2,1)}, bf16[2,256,384]{2,1,0:T(8,128)(2,1)S(1)}, u32[]{:S(2)}) copy-start(bf16[2,256,384]{2,1,0:T(8,128)(2,1)S(1)} %collective-permute-done.13.refs_5_) | copy-start | bytes 1179652
  166.9 16.9 %copy-start.7 = (bf16[2,256,384]{2,1,0:T(8,128)(2,1)}, bf16[2,256,384]{2,1,0:T(8,128)(2,1)S(1)}, u32[]{:S(2)}) copy-start(bf16[2,256,384]{2,1,0:T(8,128)(2,1)S(1)} %collective-permute-done.14.refs_6_) | copy-start | bytes 1179652
  169.7 14.1 %copy-start.8 = (bf16[2,256,384]{2,1,0:T(8,128)(2,1)}, bf16[2,256,384]{2,1,0:T(8,128)(2,1)S(1)}, u32[]{:S(2)}) copy-start(bf16[2,256,384]{2,1,0:T(8,128)(2,1)S(1)} %collective-permute-done.15.refs_7_) | copy-start | bytes 1179652
  169.7 14.2 %collective-permute-start.16 = (bf16[2,256,384]{2,1,0:T(8,128)(2,1)}, bf16[2,256,384]{2,1,0:T(8,128)(2,1)S(1)}, u32[]{:S(2)}, u32[]{:S(2)}) collective-permute-start(bf16[2,256,384]{2,1,0:T(8,128)(2,1)} %get-tuple-element.138), channel_id=1, source_target_pairs={{0,0},{1,1},{2,2},{3,3},{4,64},{5,65},{6,66},{7,67},{8,12},{9,13},... | collective-permute-start | bytes 1179656 | tf_op jit(solution)/shard_map/ppermute | solution.py:272
  171.6 19.3 %collective-permute-start.17 = (bf16[2,256,384]{2,1,0:T(8,128)(2,1)}, bf16[2,256,384]{2,1,0:T(8,128)(2,1)S(1)}, u32[]{:S(2)}, u32[]{:S(2)}) collective-permute-start(bf16[2,256,384]{2,1,0:T(8,128)(2,1)} %get-tuple-element.139), channel_id=1, source_target_pairs={{0,32},{1,33},{2,34},{3,35},{4,96},{5,97},{6,98},{7,99},{8,44},{9,... | collective-permute-start | bytes 1179656 | tf_op jit(solution)/shard_map/ppermute | solution.py:272
  173.8 17.1 %collective-permute-start.18 = (bf16[2,256,384]{2,1,0:T(8,128)(2,1)}, bf16[2,256,384]{2,1,0:T(8,128)(2,1)S(1)}, u32[]{:S(2)}, u32[]{:S(2)}) collective-permute-start(bf16[2,256,384]{2,1,0:T(8,128)(2,1)} %get-tuple-element.140), channel_id=1, source_target_pairs={{0,16},{1,17},{2,18},{3,19},{4,80},{5,81},{6,82},{7,83},{8,28},{9,... | collective-permute-start | bytes 1179656 | tf_op jit(solution)/shard_map/ppermute | solution.py:272
  174.5 18.1 %collective-permute-start.19 = (bf16[2,256,384]{2,1,0:T(8,128)(2,1)}, bf16[2,256,384]{2,1,0:T(8,128)(2,1)S(1)}, u32[]{:S(2)}, u32[]{:S(2)}) collective-permute-start(bf16[2,256,384]{2,1,0:T(8,128)(2,1)} %get-tuple-element.141), channel_id=1, source_target_pairs={{0,48},{1,49},{2,50},{3,51},{4,112},{5,113},{6,114},{7,115},{8,60}... | collective-permute-start | bytes 1179656 | tf_op jit(solution)/shard_map/ppermute | solution.py:272
  176.7 23.7 %collective-permute-start.20 = (bf16[2,256,384]{2,1,0:T(8,128)(2,1)}, bf16[2,256,384]{2,1,0:T(8,128)(2,1)S(1)}, u32[]{:S(2)}, u32[]{:S(2)}) collective-permute-start(bf16[2,256,384]{2,1,0:T(8,128)(2,1)} %get-tuple-element.142), channel_id=1, source_target_pairs={{0,4},{1,5},{2,6},{3,7},{4,68},{5,69},{6,70},{7,71},{8,8},{9,9},{1... | collective-permute-start | bytes 1179656 | tf_op jit(solution)/shard_map/ppermute | solution.py:272
  183.9 16.5 %copy-start.9 = (bf16[2,256,384]{2,1,0:T(8,128)(2,1)}, bf16[2,256,384]{2,1,0:T(8,128)(2,1)S(1)}, u32[]{:S(2)}) copy-start(bf16[2,256,384]{2,1,0:T(8,128)(2,1)S(1)} %collective-permute-done.16.refs_0_) | copy-start | bytes 1179652
  190.9 9.5 %copy-start.10 = (bf16[2,256,384]{2,1,0:T(8,128)(2,1)}, bf16[2,256,384]{2,1,0:T(8,128)(2,1)S(1)}, u32[]{:S(2)}) copy-start(bf16[2,256,384]{2,1,0:T(8,128)(2,1)S(1)} %collective-permute-done.17.refs_1_) | copy-start | bytes 1179652
  190.9 9.5 %copy-start.11 = (bf16[2,256,384]{2,1,0:T(8,128)(2,1)}, bf16[2,256,384]{2,1,0:T(8,128)(2,1)S(1)}, u32[]{:S(2)}) copy-start(bf16[2,256,384]{2,1,0:T(8,128)(2,1)S(1)} %collective-permute-done.18.refs_2_) | copy-start | bytes 1179652
  192.6 7.8 %copy-start.12 = (bf16[2,256,384]{2,1,0:T(8,128)(2,1)}, bf16[2,256,384]{2,1,0:T(8,128)(2,1)S(1)}, u32[]{:S(2)}) copy-start(bf16[2,256,384]{2,1,0:T(8,128)(2,1)S(1)} %collective-permute-done.19.refs_3_) | copy-start | bytes 1179652
  201.1 56.1 %all-to-all-start.4 = ((bf16[8,2,256,384]{3,2,1,0:T(8,128)(2,1)}), bf16[8,2,256,384]{3,2,1,0:T(8,128)(2,1)S(1)}, u32[]{:S(2)}, u32[]{:S(2)}) async-start(bf16[8,2,256,384]{3,2,1,0:T(8,128)(2,1)} %shard_map.37), calls=%async_computation.4 | async-start | bytes 6291456 | tf_op jit(solution)/shard_map/all_to_all | solution.py:243
  208.8 17.1 %collective-permute-start.21 = (bf16[2,256,384]{2,1,0:T(8,128)(2,1)}, bf16[2,256,384]{2,1,0:T(8,128)(2,1)S(1)}, u32[]{:S(2)}, u32[]{:S(2)}) collective-permute-start(bf16[2,256,384]{2,1,0:T(8,128)(2,1)} %get-tuple-element.148), channel_id=1, source_target_pairs={{0,36},{1,37},{2,38},{3,39},{4,100},{5,101},{6,102},{7,103},{8,40}... | collective-permute-start | bytes 1179656 | tf_op jit(solution)/shard_map/ppermute | solution.py:272
  210.4 15.4 %collective-permute-start.22 = (bf16[2,256,384]{2,1,0:T(8,128)(2,1)}, bf16[2,256,384]{2,1,0:T(8,128)(2,1)S(1)}, u32[]{:S(2)}, u32[]{:S(2)}) collective-permute-start(bf16[2,256,384]{2,1,0:T(8,128)(2,1)} %get-tuple-element.149), channel_id=1, source_target_pairs={{0,20},{1,21},{2,22},{3,23},{4,84},{5,85},{6,86},{7,87},{8,24},{9,... | collective-permute-start | bytes 1179656 | tf_op jit(solution)/shard_map/ppermute | solution.py:272
  211.6 16.8 %collective-permute-start.23 = (bf16[2,256,384]{2,1,0:T(8,128)(2,1)}, bf16[2,256,384]{2,1,0:T(8,128)(2,1)}, u32[]{:S(2)}, u32[]{:S(2)}) collective-permute-start(bf16[2,256,384]{2,1,0:T(8,128)(2,1)} %get-tuple-element.150), channel_id=1, source_target_pairs={{0,52},{1,53},{2,54},{3,55},{4,116},{5,117},{6,118},{7,119},{8,56}... | collective-permute-start | bytes 1179656 | tf_op jit(solution)/shard_map/ppermute | solution.py:272
  225.9 82.8 %copy-start.14 = (bf16[2,256,384]{2,1,0:T(8,128)(2,1)}, bf16[2,256,384]{2,1,0:T(8,128)(2,1)S(1)}, u32[]{:S(2)}) copy-start(bf16[2,256,384]{2,1,0:T(8,128)(2,1)S(1)} %collective-permute-done.21.refs_5_) | copy-start | bytes 1179652
  225.9 26.7 %copy-start.15 = (bf16[2,256,384]{2,1,0:T(8,128)(2,1)}, bf16[2,256,384]{2,1,0:T(8,128)(2,1)S(1)}, u32[]{:S(2)}) copy-start(bf16[2,256,384]{2,1,0:T(8,128)(2,1)S(1)} %collective-permute-done.22.refs_6_) | copy-start | bytes 1179652
  228.4 13.9 %collective-permute-start.24 = (bf16[2,256,384]{2,1,0:T(8,128)(2,1)}, bf16[2,256,384]{2,1,0:T(8,128)(2,1)S(1)}, u32[]{:S(2)}, u32[]{:S(2)}) collective-permute-start(bf16[2,256,384]{2,1,0:T(8,128)(2,1)} %get-tuple-element.160), channel_id=1, source_target_pairs={{0,0},{1,1},{2,2},{3,3},{4,64},{5,65},{6,66},{7,67},{8,12},{9,13},... | collective-permute-start | bytes 1179656 | tf_op jit(solution)/shard_map/ppermute | solution.py:272
  230.3 19.4 %collective-permute-start.25 = (bf16[2,256,384]{2,1,0:T(8,128)(2,1)}, bf16[2,256,384]{2,1,0:T(8,128)(2,1)S(1)}, u32[]{:S(2)}, u32[]{:S(2)}) collective-permute-start(bf16[2,256,384]{2,1,0:T(8,128)(2,1)} %get-tuple-element.161), channel_id=1, source_target_pairs={{0,32},{1,33},{2,34},{3,35},{4,96},{5,97},{6,98},{7,99},{8,44},{9,... | collective-permute-start | bytes 1179656 | tf_op jit(solution)/shard_map/ppermute | solution.py:272
  232.7 19.8 %collective-permute-start.26 = (bf16[2,256,384]{2,1,0:T(8,128)(2,1)}, bf16[2,256,384]{2,1,0:T(8,128)(2,1)S(1)}, u32[]{:S(2)}, u32[]{:S(2)}) collective-permute-start(bf16[2,256,384]{2,1,0:T(8,128)(2,1)} %get-tuple-element.162), channel_id=1, source_target_pairs={{0,16},{1,17},{2,18},{3,19},{4,80},{5,81},{6,82},{7,83},{8,28},{9,... | collective-permute-start | bytes 1179656 | tf_op jit(solution)/shard_map/ppermute | solution.py:272
  233.1 36.2 %collective-permute-start.27 = (bf16[2,256,384]{2,1,0:T(8,128)(2,1)}, bf16[2,256,384]{2,1,0:T(8,128)(2,1)}, u32[]{:S(2)}, u32[]{:S(2)}) collective-permute-start(bf16[2,256,384]{2,1,0:T(8,128)(2,1)} %get-tuple-element.163), channel_id=1, source_target_pairs={{0,48},{1,49},{2,50},{3,51},{4,112},{5,113},{6,114},{7,115},{8,60}... | collective-permute-start | bytes 1179656 | tf_op jit(solution)/shard_map/ppermute | solution.py:272
  235.4 33.9 %collective-permute-start.28 = (bf16[2,256,384]{2,1,0:T(8,128)(2,1)}, bf16[2,256,384]{2,1,0:T(8,128)(2,1)}, u32[]{:S(2)}, u32[]{:S(2)}) collective-permute-start(bf16[2,256,384]{2,1,0:T(8,128)(2,1)} %get-tuple-element.164), channel_id=1, source_target_pairs={{0,4},{1,5},{2,6},{3,7},{4,68},{5,69},{6,70},{7,71},{8,8},{9,9},{1... | collective-permute-start | bytes 1179656 | tf_op jit(solution)/shard_map/ppermute | solution.py:272
  242.3 10.2 %copy-start.16 = (bf16[2,256,384]{2,1,0:T(8,128)(2,1)}, bf16[2,256,384]{2,1,0:T(8,128)(2,1)S(1)}, u32[]{:S(2)}) copy-start(bf16[2,256,384]{2,1,0:T(8,128)(2,1)S(1)} %collective-permute-done.24.refs_0_) | copy-start | bytes 1179652
  242.3 27.0 %collective-permute-start.29 = (bf16[2,256,384]{2,1,0:T(8,128)(2,1)}, bf16[2,256,384]{2,1,0:T(8,128)(2,1)}, u32[]{:S(2)}, u32[]{:S(2)}) collective-permute-start(bf16[2,256,384]{2,1,0:T(8,128)(2,1)} %get-tuple-element.165), channel_id=1, source_target_pairs={{0,36},{1,37},{2,38},{3,39},{4,100},{5,101},{6,102},{7,103},{8,40}... | collective-permute-start | bytes 1179656 | tf_op jit(solution)/shard_map/ppermute | solution.py:272
  249.7 21.8 %collective-permute-start.30 = (bf16[2,256,384]{2,1,0:T(8,128)(2,1)}, bf16[2,256,384]{2,1,0:T(8,128)(2,1)}, u32[]{:S(2)}, u32[]{:S(2)}) collective-permute-start(bf16[2,256,384]{2,1,0:T(8,128)(2,1)} %get-tuple-element.166), channel_id=1, source_target_pairs={{0,20},{1,21},{2,22},{3,23},{4,84},{5,85},{6,86},{7,87},{8,24},{9,... | collective-permute-start | bytes 1179656 | tf_op jit(solution)/shard_map/ppermute | solution.py:272
  253.3 21.9 %collective-permute-start.31 = (bf16[2,256,384]{2,1,0:T(8,128)(2,1)}, bf16[2,256,384]{2,1,0:T(8,128)(2,1)}, u32[]{:S(2)}, u32[]{:S(2)}) collective-permute-start(bf16[2,256,384]{2,1,0:T(8,128)(2,1)} %get-tuple-element.167), channel_id=1, source_target_pairs={{0,52},{1,53},{2,54},{3,55},{4,116},{5,117},{6,118},{7,119},{8,56}... | collective-permute-start | bytes 1179656 | tf_op jit(solution)/shard_map/ppermute | solution.py:272
  275.2 14.8 %collective-permute-start.32 = (bf16[2,256,384]{2,1,0:T(8,128)(2,1)}, bf16[2,256,384]{2,1,0:T(8,128)(2,1)S(1)}, u32[]{:S(2)}, u32[]{:S(2)}) collective-permute-start(bf16[2,256,384]{2,1,0:T(8,128)(2,1)} %get-tuple-element.177), channel_id=1, source_target_pairs={{0,0},{1,1},{2,2},{3,3},{4,64},{5,65},{6,66},{7,67},{8,12},{9,13},... | collective-permute-start | bytes 1179656 | tf_op jit(solution)/shard_map/ppermute | solution.py:272
  277.1 21.6 %collective-permute-start.33 = (bf16[2,256,384]{2,1,0:T(8,128)(2,1)}, bf16[2,256,384]{2,1,0:T(8,128)(2,1)S(1)}, u32[]{:S(2)}, u32[]{:S(2)}) collective-permute-start(bf16[2,256,384]{2,1,0:T(8,128)(2,1)} %get-tuple-element.178), channel_id=1, source_target_pairs={{0,32},{1,33},{2,34},{3,35},{4,96},{5,97},{6,98},{7,99},{8,44},{9,... | collective-permute-start | bytes 1179656 | tf_op jit(solution)/shard_map/ppermute | solution.py:272
  279.0 21.2 %collective-permute-start.34 = (bf16[2,256,384]{2,1,0:T(8,128)(2,1)}, bf16[2,256,384]{2,1,0:T(8,128)(2,1)S(1)}, u32[]{:S(2)}, u32[]{:S(2)}) collective-permute-start(bf16[2,256,384]{2,1,0:T(8,128)(2,1)} %get-tuple-element.179), channel_id=1, source_target_pairs={{0,16},{1,17},{2,18},{3,19},{4,80},{5,81},{6,82},{7,83},{8,28},{9,... | collective-permute-start | bytes 1179656 | tf_op jit(solution)/shard_map/ppermute | solution.py:272
  279.2 36.6 %collective-permute-start.35 = (bf16[2,256,384]{2,1,0:T(8,128)(2,1)}, bf16[2,256,384]{2,1,0:T(8,128)(2,1)S(1)}, u32[]{:S(2)}, u32[]{:S(2)}) collective-permute-start(bf16[2,256,384]{2,1,0:T(8,128)(2,1)} %get-tuple-element.180), channel_id=1, source_target_pairs={{0,48},{1,49},{2,50},{3,51},{4,112},{5,113},{6,114},{7,115},{8,60}... | collective-permute-start | bytes 1179656 | tf_op jit(solution)/shard_map/ppermute | solution.py:272
  282.2 33.5 %collective-permute-start.36 = (bf16[2,256,384]{2,1,0:T(8,128)(2,1)}, bf16[2,256,384]{2,1,0:T(8,128)(2,1)S(1)}, u32[]{:S(2)}, u32[]{:S(2)}) collective-permute-start(bf16[2,256,384]{2,1,0:T(8,128)(2,1)} %get-tuple-element.181), channel_id=1, source_target_pairs={{0,4},{1,5},{2,6},{3,7},{4,68},{5,69},{6,70},{7,71},{8,8},{9,9},{1... | collective-permute-start | bytes 1179656 | tf_op jit(solution)/shard_map/ppermute | solution.py:272
  290.0 18.6 %copy-start.19 = (bf16[2,256,384]{2,1,0:T(8,128)(2,1)}, bf16[2,256,384]{2,1,0:T(8,128)(2,1)S(1)}, u32[]{:S(2)}) copy-start(bf16[2,256,384]{2,1,0:T(8,128)(2,1)S(1)} %collective-permute-done.32.refs_0_) | copy-start | bytes 1179652
  290.0 25.8 %collective-permute-start.37 = (bf16[2,256,384]{2,1,0:T(8,128)(2,1)}, bf16[2,256,384]{2,1,0:T(8,128)(2,1)S(1)}, u32[]{:S(2)}, u32[]{:S(2)}) collective-permute-start(bf16[2,256,384]{2,1,0:T(8,128)(2,1)} %get-tuple-element.182), channel_id=1, source_target_pairs={{0,36},{1,37},{2,38},{3,39},{4,100},{5,101},{6,102},{7,103},{8,40}... | collective-permute-start | bytes 1179656 | tf_op jit(solution)/shard_map/ppermute | solution.py:272
  298.7 10.0 %copy-start.20 = (bf16[2,256,384]{2,1,0:T(8,128)(2,1)}, bf16[2,256,384]{2,1,0:T(8,128)(2,1)S(1)}, u32[]{:S(2)}) copy-start(bf16[2,256,384]{2,1,0:T(8,128)(2,1)S(1)} %collective-permute-done.33.refs_1_) | copy-start | bytes 1179652
  298.7 18.7 %collective-permute-start.38 = (bf16[2,256,384]{2,1,0:T(8,128)(2,1)}, bf16[2,256,384]{2,1,0:T(8,128)(2,1)S(1)}, u32[]{:S(2)}, u32[]{:S(2)}) collective-permute-start(bf16[2,256,384]{2,1,0:T(8,128)(2,1)} %get-tuple-element.183), channel_id=1, source_target_pairs={{0,20},{1,21},{2,22},{3,23},{4,84},{5,85},{6,86},{7,87},{8,24},{9,... | collective-permute-start | bytes 1179656 | tf_op jit(solution)/shard_map/ppermute | solution.py:272
  300.2 8.5 %copy-start.21 = (bf16[2,256,384]{2,1,0:T(8,128)(2,1)}, bf16[2,256,384]{2,1,0:T(8,128)(2,1)S(1)}, u32[]{:S(2)}) copy-start(bf16[2,256,384]{2,1,0:T(8,128)(2,1)S(1)} %collective-permute-done.34.refs_2_) | copy-start | bytes 1179652
  300.2 20.4 %collective-permute-start.39 = (bf16[2,256,384]{2,1,0:T(8,128)(2,1)}, bf16[2,256,384]{2,1,0:T(8,128)(2,1)S(1)}, u32[]{:S(2)}, u32[]{:S(2)}) collective-permute-start(bf16[2,256,384]{2,1,0:T(8,128)(2,1)} %get-tuple-element.184), channel_id=1, source_target_pairs={{0,52},{1,53},{2,54},{3,55},{4,116},{5,117},{6,118},{7,119},{8,56}... | collective-permute-start | bytes 1179656 | tf_op jit(solution)/shard_map/ppermute | solution.py:272
  315.7 4.9 %copy-start.22 = (bf16[2,256,384]{2,1,0:T(8,128)(2,1)}, bf16[2,256,384]{2,1,0:T(8,128)(2,1)S(1)}, u32[]{:S(2)}) copy-start(bf16[2,256,384]{2,1,0:T(8,128)(2,1)S(1)} %collective-permute-done.35.refs_3_) | copy-start | bytes 1179652
  315.8 4.9 %copy-start.23 = (bf16[2,256,384]{2,1,0:T(8,128)(2,1)}, bf16[2,256,384]{2,1,0:T(8,128)(2,1)S(1)}, u32[]{:S(2)}) copy-start(bf16[2,256,384]{2,1,0:T(8,128)(2,1)S(1)} %collective-permute-done.36.refs_4_) | copy-start | bytes 1179652
  315.8 4.8 %copy-start.24 = (bf16[2,256,384]{2,1,0:T(8,128)(2,1)}, bf16[2,256,384]{2,1,0:T(8,128)(2,1)S(1)}, u32[]{:S(2)}) copy-start(bf16[2,256,384]{2,1,0:T(8,128)(2,1)S(1)} %collective-permute-done.37.refs_5_) | copy-start | bytes 1179652
  (9 other events, 14.3 us)

commit v3 on v2

v3 whole, which is shorter than its diff:
```python
import functools

import jax
import jax.numpy as jnp
from jax import lax
from jax.experimental import pallas as pl
from jax.experimental.pallas import tpu as pltpu
from jax.sharding import Mesh
from jax.sharding import PartitionSpec as P

AXES = ("z", "xl", "c", "xh", "y")
SIZES = (4, 2, 2, 2, 4)
CHUNKS = ((0, 256), (256, 384), (640, 384))
HALF = 4
ORDER = (0, 4, 1, 5, 2, 6, 3, 7)
AHEAD = 8
VMEM = 60 << 20
ANY = pl.BlockSpec(memory_space=pl.ANY)
SMEM = pl.BlockSpec(memory_space=pltpu.SMEM)
BF16 = jnp.bfloat16


def split(value):
    high = lax.reduce_precision(value, 8, 7)
    return high.astype(BF16), (value - high).astype(BF16)


def number(z, xl, c, xh, y):
    return (((z * 2 + xl) * 2 + c) * 2 + xh) * 4 + y


def bits(k):
    return k >> 2, (k >> 1) & 1, k & 1


def pairs(k):
    k2, k1, k0 = bits(k)
    out = []
    for z in range(4):
        for xl in range(2):
            for c in range(2):
                for xh in range(2):
                    for y in range(4):
                        xh2, xl2 = (z >> 1) ^ k2 ^ c, xl ^ k1
                        z2 = xh * 2 + ((z & 1) ^ k0)
                        out.append((number(z, xl, c, xh, y), number(z2, xl2, c, xh2, y)))
    return out


def moved(change):
    out = []
    for z in range(4):
        for xl in range(2):
            for c in range(2):
                for xh in range(2):
                    for y in range(4):
                        out.append((number(z, xl, c, xh, y), number(*change(z, xl, c, xh, y))))
    return out


def start_all(copies):
    for one in copies:
        one.start()
    return copies


def wait_all(copies):
    for one in copies:
        one.wait()


def pack_kernel(start, rows, block, base, out, buf, sems):
    incoming, outgoing = [], []
    for n in range(16):
        c, y, j = n >> 3, (n >> 1) & 3, n & 1
        column = (c * 8 + j * 4 + y) * block
        source = base.at[pl.ds(start, rows), pl.ds(column, block)]
        incoming.append(pltpu.make_async_copy(source, buf.at[n], sems.at[n]))
        outgoing.append(
            pltpu.make_async_copy(buf.at[n], out.at[n >> 1, j], sems.at[16 + n])
        )
    start_all(incoming)
    for one, two in zip(incoming, outgoing):
        one.wait()
        two.start()
    wait_all(outgoing)


def pack(base, start, rows, block):
    size = 8 * 2 * rows * block * 2
    return pl.pallas_call(
        functools.partial(pack_kernel, start, rows, block),
        out_shape=jax.ShapeDtypeStruct((8, 2, rows, block), BF16),
        in_specs=[ANY],
        out_specs=ANY,
        scratch_shapes=[
            pltpu.VMEM((16, rows, block), BF16),
            pltpu.SemaphoreType.DMA((32,)),
        ],
        compiler_params=pltpu.CompilerParams(vmem_limit_bytes=VMEM),
        cost_estimate=pl.CostEstimate(flops=0, bytes_accessed=2 * size, transcendentals=0),
    )(base)


def add_kernel(start, rows, block, first, picks, part, l0, l1, l2, l3, r0, r1, r2, r3, r4, *refs):
    outs = refs[:HALF]
    lbuf, tbuf, rbuf, pbuf, obuf, sems = refs[HALF:]
    core, low_bit = picks[32], picks[first] & 1
    copies = []
    for n in range(8):
        for flip, source in ((0, (l0, l1)), (1, (l2, l3))):
            lane = pl.multiple_of((core ^ flip) * rows, 128)
            copies.append(
                pltpu.make_async_copy(
                    source[n >> 2].at[n & 3, :, :, pl.ds(start, rows)],
                    lbuf.at[:, picks[24 + n], :, pl.ds(lane, rows)],
                    sems.at[n * 2 + flip],
                )
            )
        for c in range(2):
            copies.append(
                pltpu.make_async_copy(
                    (r0, r0, r1, r1, r2, r3, r4, r4)[n].at[
                        0 if n in (4, 5) else n & 1, c, :, low_bit
                    ],
                    rbuf.at[:, :, picks[16 + n], c],
                    sems.at[16 + n * 2 + c],
                )
            )
    stored = [
        pltpu.make_async_copy(
            part.at[c * 4 + picks[first + k], picks[8 + first + k]], pbuf.at[k * 2 + c], sems.at[32 + k * 2 + c]
        )
        for k in range(HALF)
        for c in range(2)
    ]
    start_all(copies + stored)
    wait_all(copies)
    depth = 8 * lbuf.shape[2]
    for p in range(2):
        tbuf[p] = lbuf[p].reshape(depth, 2 * rows).T
    dot = functools.partial(jnp.dot, preferred_element_type=jnp.float32)

    @pl.loop(0, HALF)
    def _(k):
        y = picks[first + k] >> 1
        lanes = pl.ds(pl.multiple_of(picks[8 + first + k] * block, block), block)
        rhigh = rbuf[y, 0, :, :, :, lanes].reshape(depth, block)
        rlow = rbuf[y, 1, :, :, :, lanes].reshape(depth, block)
        for c in range(2):
            n = k * 2 + c
            pltpu.make_async_copy(part.at[0, 0], pbuf.at[n], sems.at[32 + n]).wait()
            lines = pl.ds(c * rows, rows)
            high, low = tbuf[0, lines], tbuf[1, lines]
            delta = dot(high, rhigh) + dot(high, rlow) + dot(low, rhigh)
            obuf[k, c] = (pbuf[n].astype(jnp.float32) + delta).astype(BF16)

    wait_all(
        start_all(
            [pltpu.make_async_copy(obuf.at[k], outs[k], sems.at[k]) for k in range(HALF)]
        )
    )


def add(start, rows, block, first, picks, part, lefts, rights):
    depth = rights[0].shape[5]
    rank = lefts[0].shape[2]
    return pl.pallas_call(
        functools.partial(add_kernel, start, rows, block, first),
        out_shape=[jax.ShapeDtypeStruct((2, rows, block), BF16)] * HALF,
        in_specs=[SMEM] + [ANY] * 10,
        out_specs=[ANY] * HALF,
        scratch_shapes=[
            pltpu.VMEM((2, 8, rank, 2 * rows), BF16),
            pltpu.VMEM((2, 2 * rows, 8 * rank), BF16),
            pltpu.VMEM((2, 2, 8, 2, depth, 2 * block), BF16),
            pltpu.VMEM((8, rows, block), BF16),
            pltpu.VMEM((HALF, 2, rows, block), BF16),
            pltpu.SemaphoreType.DMA((40,)),
        ],
        compiler_params=pltpu.CompilerParams(vmem_limit_bytes=VMEM),
        cost_estimate=pl.CostEstimate(
            flops=2 * 8 * rows * block * 768, bytes_accessed=8 << 20, transcendentals=0
        ),
    )(picks, part, *lefts, *rights)


def place_kernel(start, rows, height, first, slots, *refs):
    got = refs[:HALF]
    out, buf, sems = refs[-3:]
    incoming, outgoing = [], []
    for k in range(HALF):
        incoming.append(pltpu.make_async_copy(got[k], buf.at[k], sems.at[k]))
        for c in range(2):
            row = (slots[first + k] * 2 + c) * height + start
            outgoing.append(
                pltpu.make_async_copy(
                    buf.at[k, c],
                    out.at[pl.ds(pl.multiple_of(row, 128), rows)],
                    sems.at[HALF + k * 2 + c],
                )
            )
    start_all(incoming)
    for k in range(HALF):
        incoming[k].wait()
        start_all(outgoing[2 * k : 2 * k + 2])
    wait_all(outgoing)


def place(start, rows, height, block, first, slots, got, merged):
    old = [] if merged is None else [merged]
    return pl.pallas_call(
        functools.partial(place_kernel, start, rows, height, first),
        out_shape=jax.ShapeDtypeStruct((16 * height, block), BF16),
        in_specs=[SMEM] + [ANY] * (HALF + len(old)),
        out_specs=ANY,
        scratch_shapes=[
            pltpu.VMEM((HALF, 2, rows, block), BF16),
            pltpu.SemaphoreType.DMA((3 * HALF,)),
        ],
        input_output_aliases={HALF + 1: 0} if old else {},
        compiler_params=pltpu.CompilerParams(vmem_limit_bytes=VMEM),
        cost_estimate=pl.CostEstimate(
            flops=0, bytes_accessed=32 * rows * block, transcendentals=0
        ),
    )(slots, *got, *old)


def body(base, left, right):
    height, width = base.shape
    block = width // 16
    depth, rank = right.shape[0], left.shape[1]
    z, xl, c, xh, y = (lax.axis_index(n) for n in AXES)
    tie = lax.optimization_barrier

    def across(value, change):
        return lax.ppermute(value, AXES, moved(change))

    rights = jnp.stack(split(right)).reshape(2, depth, 2, 2, 4, block)
    rights = rights.transpose(2, 4, 0, 1, 3, 5).reshape(8, 2 * depth, 2 * block)
    rights = lax.all_to_all(
        jnp.concatenate([rights, rights]), ("xl", "c", "y"), 0, 0, tiled=True
    ).reshape(2, 8, 2 * depth, 2 * block)
    lefts = jnp.stack(split(left.T))
    lefts = jnp.stack(
        [lefts]
        + [
            across(lefts, lambda z, xl, c, xh, y: (z, xl, c, xh, (y - d) % 4))
            for d in (1, 2, 3)
        ]
    )
    packed = [pack(base, *chunk, block) for chunk in CHUNKS]
    packed[0], lefts, rights = tie((packed[0], lefts, rights))

    def first(i):
        return lax.all_to_all(packed[i], ("c", "y"), 0, 0, tiled=True)

    def down(value):
        return across(value, lambda z, xl, c, xh, y: ((z - 1) % 4, xl, c, xh, y))

    def up(value):
        return across(value, lambda z, xl, c, xh, y: ((z + 1) % 4, xl, c, xh, y))

    above, below = down(rights), up(rights)
    rights = [rights, above, down(above[:1]), up(below[1:]), below]
    rights = [one.reshape(-1, 2, 2, 2, 2, depth, 2 * block) for one in rights]
    lefts = [
        lefts,
        across(lefts, lambda z, xl, c, xh, y: (z, xl, c, xh ^ 1, y)),
        across(lefts, lambda z, xl, c, xh, y: (z, xl, c ^ 1, xh, y)),
        across(lefts, lambda z, xl, c, xh, y: (z, xl, c ^ 1, xh ^ 1, y)),
    ]

    ys, js, zs, ls, slots = [], [], [], [], []
    for n in range(8):
        zs.append(((z + (n >> 1)) & 3) * 2 + (n & 1))
        ls.append((xh ^ (n >> 2)) * 4 + ((y + (n & 3)) & 3))
        k2, k1, k0 = bits(ORDER[n])
        ys.append(((z & 1) ^ k0) * 2 + (xl ^ k1))
        js.append((z >> 1) ^ k2 ^ c)
        slots.append(((xh ^ k2 ^ c) * 2 + ((z & 1) ^ k0)) * 2 + (xl ^ k1))
    picks = jnp.stack([*ys, *js, *zs, *ls, c]).astype(jnp.int32)
    slots = jnp.stack(slots).astype(jnp.int32)

    merged = None
    landed = first(0)

    def total(s, part):
        return [
            one
            for half in (0, HALF)
            for one in add(*CHUNKS[s], block, half, picks, part, lefts, rights)
        ]

    def finish(s, got, merged):
        for half in (0, HALF):
            merged = place(
                *CHUNKS[s], height, block, half, slots, got[half : half + HALF], merged
            )
        return merged

    count = len(CHUNKS)
    packed[1], lefts, rights = tie((packed[1], lefts, rights))
    got, sent = [], total(0, landed)
    arrived = first(1)
    for s in range(count):
        if s:
            got, sent[:HALF] = tie((got, sent[:HALF]))
        new = []
        for k in range(8):
            if k == HALF:
                new[0], sent[HALF:] = tie((new[0], sent[HALF:]))
            new.append(lax.ppermute(sent[k], AXES, pairs(ORDER[k])))
        if got:
            merged = finish(s - 1, got, merged)
        if s + 1 < count:
            landed = arrived
            if s + 2 < count:
                packed[s + 2] = tie((packed[s + 2], landed, new[:AHEAD]))[0]
                arrived = first(s + 2)
            sent = total(s + 1, landed)
        got = new
    return finish(count - 1, got, merged)


def solution(mesh):
    fine = Mesh(mesh.devices.reshape(SIZES), AXES)
    placed = P(("z", "xl", "c"), ("xh", "y"))
    return jax.shard_map(
        body,
        mesh=fine,
        in_specs=(placed, placed, placed),
        out_specs=P(None, AXES),
        check_vma=False,
    )
```

time: 327 us -> 285 us (0.87)
  the two profiles are of different devices: /device:TPU:15 before, /device:TPU:75 now
where the time goes in v3:
time: 285 us; the launch traced here: 284 us
  waiting for transfers between devices  116 us (41%)
  starting transfers between devices  81 us (28%)
  Pallas kernels  78.9 us (28%)
  local copies, waits for them, and re-layouts  3.8 us (1%)
  other arithmetic  3.49 us (1%)
    ppermute x24, waiting for transfers between devices, body(): new.append(lax.ppermute(sent[k], AXES, pairs(ORDER[k])))  68.8 us
    pallas_call x6, Pallas kernels, add(): pl.pallas_call(functools.partial(add_kernel, start, rows, block, first),...  47.7 us
    ppermute x24, starting transfers between devices, body(): new.append(lax.ppermute(sent[k], AXES, pairs(ORDER[k])))  47.2 us
    ppermute x10, waiting for transfers between devices, across(): return lax.ppermute(value, AXES, moved(change))  27.1 us
    all_to_all x3, waiting for transfers between devices, first(): return lax.all_to_all(packed[i], ('c', 'y'), 0, 0, tiled=True)  19.9 us
    pallas_call x6, Pallas kernels, place(): pl.pallas_call(functools.partial(place_kernel, start, rows, height, first...  18.7 us
    all_to_all x3, starting transfers between devices, first(): return lax.all_to_all(packed[i], ('c', 'y'), 0, 0, tiled=True)  17.6 us
    pallas_call x3, Pallas kernels, pack(): pl.pallas_call(functools.partial(pack_kernel, start, rows, block), out_sh...  12.4 us
  transfers between devices with their start and end apart: 38, of which 22 were waited for; matrix products, arithmetic and copies ran while one was open for 1% of the time, Pallas kernels for 27%

profile of v3, /device:TPU:75, one launch (start us, length us, event | category | flops | bytes accessed | tf_op | source)
XLA Modules:
  0.0 283.5 jit_solution(9868359336178552281)
XLA Ops:
  0.0 1.0 reduce-precision_convert_fusion
  2.4 0.9 pad_maximum_fusion
  3.3 6.1 %all-to-all-start = ((bf16[16,32,768]{2,1,0:T(8,128)(2,1)}), bf16[16,32,768]{2,1,0:T(8,128)(2,1)S(1)}, u32[]{:S(2)}, u32[]{:S(2)}) async-start(bf16[16,32,768]{2,1,0:T(8,128)(2,1)} %pad_maximum_fusion), calls=%async_computation | async-start | bytes 1572864 | tf_op jit(solution)/shard_map/all_to_all | solution.py:241
  9.5 0.9 fusion.3
  10.4 1.9 collective-permute-start.1
  12.3 1.2 collective-permute-start
  13.8 3.3 %shard_map.37 = bf16[8,2,256,384]{3,2,1,0:T(8,128)(2,1)} custom-call(bf16[1024,6144]{1,0:T(8,128)(2,1)} %base.5), custom_call_target="tpu_custom_call" | custom-call | bytes 6291456 | tf_op jit(solution)/shard_map/pallas_call | solution.py:91
  17.1 6.5 %collective-permute-done.1 = bf16[2,32,1024]{2,1,0:T(8,128)(2,1)S(1)} collective-permute-done((bf16[2,32,1024]{2,1,0:T(8,128)(2,1)S(1)}, bf16[2,32,1024]{2,1,0:T(8,128)(2,1)S(1)}, u32[]{:S(2)}, u32[]{:S(2)}) %collective-permute-start.1) | collective-permute-done | bytes 131104 | tf_op jit(solution)/shard_map/ppermute | solution.py:237
  23.5 2.2 collective-permute-done
  25.8 6.6 %all-to-all-start.1 = ((bf16[8,2,256,384]{3,2,1,0:T(8,128)(2,1)}), bf16[8,2,256,384]{3,2,1,0:T(8,128)(2,1)}, u32[]{:S(2)}, u32[]{:S(2)}) async-start(bf16[8,2,256,384]{3,2,1,0:T(8,128)(2,1)} %shard_map.37), calls=%async_computation.1 | async-start | bytes 6291456 | tf_op jit(solution)/shard_map/all_to_all | solution.py:256
  32.4 1.3 collective-permute-start.8
  33.9 2.6 collective-permute-start.5
  36.5 1.1 collective-permute-start.3
  37.7 13.6 %collective-permute-done.8 = bf16[2,8,32,768]{3,2,1,0:T(8,128)(2,1)S(1)} collective-permute-done((bf16[2,8,32,768]{3,2,1,0:T(8,128)(2,1)S(1)}, bf16[2,8,32,768]{3,2,1,0:T(8,128)(2,1)S(1)}, u32[]{:S(2)}, u32[]{:S(2)}) %collective-permute-start.8) | collective-permute-done | bytes 786464 | tf_op jit(solution)/shard_map/ppermute | solution.py:237
  51.3 0.8 slice.9
  52.1 1.3 collective-permute-start.9
  53.5 0.8 slice.8
  54.4 4.6 %shard_map.38 = bf16[8,2,384,384]{3,2,1,0:T(8,128)(2,1)} custom-call(bf16[1024,6144]{1,0:T(8,128)(2,1)} %base.5), custom_call_target="tpu_custom_call" | custom-call | bytes 9437184 | tf_op jit(solution)/shard_map/pallas_call | solution.py:91
  59.1 2.2 collective-permute-done.3.l1
  61.3 0.7 collective-permute-done.9
  62.0 1.9 collective-permute-done.7
  63.9 5.3 %all-to-all-done.1.part = bf16[8,2,256,384]{3,2,1,0:T(8,128)(2,1)} async-done(((bf16[8,2,256,384]{3,2,1,0:T(8,128)(2,1)}), bf16[8,2,256,384]{3,2,1,0:T(8,128)(2,1)}, u32[]{:S(2)}, u32[]{:S(2)}) %all-to-all-start.1) | async-done | bytes 3145760 | tf_op jit(solution)/shard_map/all_to_all | solution.py:256
  69.2 5.7 %all-to-all-start.2 = ((bf16[8,2,384,384]{3,2,1,0:T(8,128)(2,1)}), bf16[8,2,384,384]{3,2,1,0:T(8,128)(2,1)}, u32[]{:S(2)}, u32[]{:S(2)}) async-start(bf16[8,2,384,384]{3,2,1,0:T(8,128)(2,1)} %shard_map.38), calls=%async_computation.2 | async-start | bytes 9437184 | tf_op jit(solution)/shard_map/all_to_all | solution.py:256
  75.5 7.1 %shard_map.39 = (bf16[2,256,384]{2,1,0:T(8,128)(2,1)}, bf16[2,256,384]{2,1,0:T(8,128)(2,1)}, bf16[2,256,384]{2,1,0:T(8,128)(2,1)}, bf16[2,256,384]{2,1,0:T(8,128)(2,1)}) custom-call(s32[33]{0:T(128)} %stack.174.picks, bf16[8,2,256,384]{3,2,1,0:T(8,128)(2,1)} %all-to-all-done.1.part, bf16[4,2,32,1024]{3,2,1,0:T(8,128)(2,1)} %copy-done.3, ...), custom_call_target="tpu_custom_call" | custom-call | flops 1207959552 | bytes 8388608 | tf_op jit(solution)/shard_map/pallas_call | solution.py:168
  82.6 1.9 collective-permute-start.10
  84.6 6.4 %collective-permute-start.11 = (bf16[2,256,384]{2,1,0:T(8,128)(2,1)}, bf16[2,256,384]{2,1,0:T(8,128)(2,1)}, u32[]{:S(2)}, u32[]{:S(2)}) collective-permute-start(bf16[2,256,384]{2,1,0:T(8,128)(2,1)} %get-tuple-element.100), channel_id=1, source_target_pairs={{0,4},{1,5},{2,6},{3,7},{4,68},{5,69},{6,70},{7,71},{8,8},{9,9},{1... | collective-permute-start | bytes 1179656 | tf_op jit(solution)/shard_map/ppermute | solution.py:313
  91.1 2.1 collective-permute-start.13
  93.2 7.1 %shard_map.40 = (bf16[2,256,384]{2,1,0:T(8,128)(2,1)}, bf16[2,256,384]{2,1,0:T(8,128)(2,1)}, bf16[2,256,384]{2,1,0:T(8,128)(2,1)}, bf16[2,256,384]{2,1,0:T(8,128)(2,1)}) custom-call(s32[33]{0:T(128)} %stack.174.picks, bf16[8,2,256,384]{3,2,1,0:T(8,128)(2,1)} %all-to-all-done.1.part, bf16[4,2,32,1024]{3,2,1,0:T(8,128)(2,1)} %copy-done.3, ...), custom_call_target="tpu_custom_call" | custom-call | flops 1207959552 | bytes 8388608 | tf_op jit(solution)/shard_map/pallas_call | solution.py:168
  100.6 4.5 %collective-permute-start.15 = (bf16[2,256,384]{2,1,0:T(8,128)(2,1)}, bf16[2,256,384]{2,1,0:T(8,128)(2,1)}, u32[]{:S(2)}, u32[]{:S(2)}) collective-permute-start(bf16[2,256,384]{2,1,0:T(8,128)(2,1)} %get-tuple-element.104), channel_id=1, source_target_pairs={{0,20},{1,21},{2,22},{3,23},{4,84},{5,85},{6,86},{7,87},{8,24},{9,... | collective-permute-start | bytes 1179656 | tf_op jit(solution)/shard_map/ppermute | solution.py:313
  105.2 4.6 %shard_map.43 = bf16[8,2,384,384]{3,2,1,0:T(8,128)(2,1)} custom-call(bf16[1024,6144]{1,0:T(8,128)(2,1)} %base.5), custom_call_target="tpu_custom_call" | custom-call | bytes 9437184 | tf_op jit(solution)/shard_map/pallas_call | solution.py:91
  109.8 6.8 %collective-permute-done.14.refs_0_ = bf16[2,256,384]{2,1,0:T(8,128)(2,1)} collective-permute-done((bf16[2,256,384]{2,1,0:T(8,128)(2,1)}, bf16[2,256,384]{2,1,0:T(8,128)(2,1)}, u32[]{:S(2)}, u32[]{:S(2)}) %collective-permute-start.14) | collective-permute-done | bytes 393248 | tf_op jit(solution)/shard_map/ppermute | solution.py:313
  116.6 3.7 %collective-permute-done.15.refs_1_ = bf16[2,256,384]{2,1,0:T(8,128)(2,1)} collective-permute-done((bf16[2,256,384]{2,1,0:T(8,128)(2,1)}, bf16[2,256,384]{2,1,0:T(8,128)(2,1)}, u32[]{:S(2)}, u32[]{:S(2)}) %collective-permute-start.15) | collective-permute-done | bytes 393248 | tf_op jit(solution)/shard_map/ppermute | solution.py:313
  120.3 4.2 %collective-permute-done.16.refs_2_ = bf16[2,256,384]{2,1,0:T(8,128)(2,1)} collective-permute-done((bf16[2,256,384]{2,1,0:T(8,128)(2,1)}, bf16[2,256,384]{2,1,0:T(8,128)(2,1)}, u32[]{:S(2)}, u32[]{:S(2)}) %collective-permute-start.16) | collective-permute-done | bytes 393248 | tf_op jit(solution)/shard_map/ppermute | solution.py:313
  124.5 4.4 %collective-permute-done.17.refs_3_ = bf16[2,256,384]{2,1,0:T(8,128)(2,1)} collective-permute-done((bf16[2,256,384]{2,1,0:T(8,128)(2,1)}, bf16[2,256,384]{2,1,0:T(8,128)(2,1)}, u32[]{:S(2)}, u32[]{:S(2)}) %collective-permute-start.17) | collective-permute-done | bytes 393248 | tf_op jit(solution)/shard_map/ppermute | solution.py:313
  128.8 5.3 %all-to-all-start.3 = ((bf16[8,2,384,384]{3,2,1,0:T(8,128)(2,1)}), bf16[8,2,384,384]{3,2,1,0:T(8,128)(2,1)}, u32[]{:S(2)}, u32[]{:S(2)}) async-start(bf16[8,2,384,384]{3,2,1,0:T(8,128)(2,1)} %shard_map.43), calls=%async_computation.3 | async-start | bytes 9437184 | tf_op jit(solution)/shard_map/all_to_all | solution.py:256
  134.1 8.4 %shard_map.41 = (bf16[2,384,384]{2,1,0:T(8,128)(2,1)}, bf16[2,384,384]{2,1,0:T(8,128)(2,1)}, bf16[2,384,384]{2,1,0:T(8,128)(2,1)}, bf16[2,384,384]{2,1,0:T(8,128)(2,1)}) custom-call(s32[33]{0:T(128)} %stack.174.picks, bf16[8,2,384,384]{3,2,1,0:T(8,128)(2,1)} %all-to-all-done.2.part, bf16[4,2,32,1024]{3,2,1,0:T(8,128)(2,1)} %copy-done.3, ...), custom_call_target="tpu_custom_call" | custom-call | flops 1811939328 | bytes 8388608 | tf_op jit(solution)/shard_map/pallas_call | solution.py:168
  142.5 1.9 collective-permute-start.18
  144.4 6.4 %collective-permute-start.19 = (bf16[2,384,384]{2,1,0:T(8,128)(2,1)}, bf16[2,384,384]{2,1,0:T(8,128)(2,1)S(1)}, u32[]{:S(2)}, u32[]{:S(2)}) collective-permute-start(bf16[2,384,384]{2,1,0:T(8,128)(2,1)} %get-tuple-element.118), channel_id=1, source_target_pairs={{0,4},{1,5},{2,6},{3,7},{4,68},{5,69},{6,70},{7,71},{8,8},{9,9},{1... | collective-permute-start | bytes 1769480 | tf_op jit(solution)/shard_map/ppermute | solution.py:313
  151.0 0.7 collective-permute-start.21
  151.7 8.4 %shard_map.42 = (bf16[2,384,384]{2,1,0:T(8,128)(2,1)}, bf16[2,384,384]{2,1,0:T(8,128)(2,1)}, bf16[2,384,384]{2,1,0:T(8,128)(2,1)}, bf16[2,384,384]{2,1,0:T(8,128)(2,1)}) custom-call(s32[33]{0:T(128)} %stack.174.picks, bf16[8,2,384,384]{3,2,1,0:T(8,128)(2,1)} %all-to-all-done.2.part, bf16[4,2,32,1024]{3,2,1,0:T(8,128)(2,1)} %copy-done.3, ...), custom_call_target="tpu_custom_call" | custom-call | flops 1811939328 | bytes 8388608 | tf_op jit(solution)/shard_map/pallas_call | solution.py:168
  160.1 1.6 collective-permute-start.22
  161.7 4.5 %collective-permute-start.23 = (bf16[2,384,384]{2,1,0:T(8,128)(2,1)}, bf16[2,384,384]{2,1,0:T(8,128)(2,1)S(1)}, u32[]{:S(2)}, u32[]{:S(2)}) collective-permute-start(bf16[2,384,384]{2,1,0:T(8,128)(2,1)} %get-tuple-element.122), channel_id=1, source_target_pairs={{0,20},{1,21},{2,22},{3,23},{4,84},{5,85},{6,86},{7,87},{8,24},{9,... | collective-permute-start | bytes 1769480 | tf_op jit(solution)/shard_map/ppermute | solution.py:313
  166.3 5.5 %collective-permute-done.20.refs_2_ = bf16[2,384,384]{2,1,0:T(8,128)(2,1)S(1)} collective-permute-done((bf16[2,384,384]{2,1,0:T(8,128)(2,1)}, bf16[2,384,384]{2,1,0:T(8,128)(2,1)S(1)}, u32[]{:S(2)}, u32[]{:S(2)}) %collective-permute-start.20) | collective-permute-done | bytes 589856 | tf_op jit(solution)/shard_map/ppermute | solution.py:313
  171.7 1.7 collective-permute-start.25
  173.5 14.6 %all-to-all-done.3.part = bf16[8,2,384,384]{3,2,1,0:T(8,128)(2,1)} async-done(((bf16[8,2,384,384]{3,2,1,0:T(8,128)(2,1)}), bf16[8,2,384,384]{3,2,1,0:T(8,128)(2,1)}, u32[]{:S(2)}, u32[]{:S(2)}) %all-to-all-start.3) | async-done | bytes 4718624 | tf_op jit(solution)/shard_map/all_to_all | solution.py:256
  188.0 8.4 %shard_map.44 = (bf16[2,384,384]{2,1,0:T(8,128)(2,1)}, bf16[2,384,384]{2,1,0:T(8,128)(2,1)}, bf16[2,384,384]{2,1,0:T(8,128)(2,1)}, bf16[2,384,384]{2,1,0:T(8,128)(2,1)}) custom-call(s32[33]{0:T(128)} %stack.174.picks, bf16[8,2,384,384]{3,2,1,0:T(8,128)(2,1)} %all-to-all-done.3.part, bf16[4,2,32,1024]{3,2,1,0:T(8,128)(2,1)} %copy-done.3, ...), custom_call_target="tpu_custom_call" | custom-call | flops 1811939328 | bytes 8388608 | tf_op jit(solution)/shard_map/pallas_call | solution.py:168
  196.5 2.6 collective-permute-done.23.refs_1_
  199.1 4.9 %collective-permute-done.24.refs_2_ = bf16[2,384,384]{2,1,0:T(8,128)(2,1)} collective-permute-done((bf16[2,384,384]{2,1,0:T(8,128)(2,1)}, bf16[2,384,384]{2,1,0:T(8,128)(2,1)}, u32[]{:S(2)}, u32[]{:S(2)}) %collective-permute-start.24) | collective-permute-done | bytes 589856 | tf_op jit(solution)/shard_map/ppermute | solution.py:313
  204.0 7.2 %collective-permute-done.25.refs_3_ = bf16[2,384,384]{2,1,0:T(8,128)(2,1)} collective-permute-done((bf16[2,384,384]{2,1,0:T(8,128)(2,1)}, bf16[2,384,384]{2,1,0:T(8,128)(2,1)}, u32[]{:S(2)}, u32[]{:S(2)}) %collective-permute-start.25) | collective-permute-done | bytes 589856 | tf_op jit(solution)/shard_map/ppermute | solution.py:313
  211.2 1.9 collective-permute-start.26
  213.2 1.9 collective-permute-start.31
  215.2 8.1 %collective-permute-start.33 = (bf16[2,384,384]{2,1,0:T(8,128)(2,1)}, bf16[2,384,384]{2,1,0:T(8,128)(2,1)}, u32[]{:S(2)}, u32[]{:S(2)}) collective-permute-start(bf16[2,384,384]{2,1,0:T(8,128)(2,1)} %get-tuple-element.142), channel_id=1, source_target_pairs={{0,36},{1,37},{2,38},{3,39},{4,100},{5,101},{6,102},{7,103},{8,40}... | collective-permute-start | bytes 1769480 | tf_op jit(solution)/shard_map/ppermute | solution.py:313
  223.3 8.4 %shard_map.45 = (bf16[2,384,384]{2,1,0:T(8,128)(2,1)}, bf16[2,384,384]{2,1,0:T(8,128)(2,1)}, bf16[2,384,384]{2,1,0:T(8,128)(2,1)}, bf16[2,384,384]{2,1,0:T(8,128)(2,1)}) custom-call(s32[33]{0:T(128)} %stack.174.picks, bf16[8,2,384,384]{3,2,1,0:T(8,128)(2,1)} %all-to-all-done.3.part, bf16[4,2,32,1024]{3,2,1,0:T(8,128)(2,1)} %copy-done.3, ...), custom_call_target="tpu_custom_call" | custom-call | flops 1811939328 | bytes 8388608 | tf_op jit(solution)/shard_map/pallas_call | solution.py:168
  231.7 2.6 collective-permute-start.28
  235.0 5.8 %collective-permute-done.32.refs_2_ = bf16[2,384,384]{2,1,0:T(8,128)(2,1)} collective-permute-done((bf16[2,384,384]{2,1,0:T(8,128)(2,1)}, bf16[2,384,384]{2,1,0:T(8,128)(2,1)}, u32[]{:S(2)}, u32[]{:S(2)}) %collective-permute-start.32) | collective-permute-done | bytes 589856 | tf_op jit(solution)/shard_map/ppermute | solution.py:313
  241.4 2.9 %shard_map.46.refs_4_ = bf16[16384,384]{1,0:T(8,128)(2,1)} custom-call(s32[8]{0:T(128)} %stack.150.slots, bf16[2,256,384]{2,1,0:T(8,128)(2,1)} %collective-permute-done.10.refs_0_, bf16[2,256,384]{2,1,0:T(8,128)(2,1)} %collective-permute-done.11.refs_1_, bf16[2,256,384]{2,1,0:T(8,128)(2,1)} %collective-permute-done.12.refs_2_, ...), custom_call_target="tpu_custom_call" | custom-call | bytes 3145728 | tf_op jit(solution)/shard_map/pallas_call | solution.py:212
  244.3 2.9 %shard_map.47.refs_4_ = bf16[16384,384]{1,0:T(8,128)(2,1)} custom-call(s32[8]{0:T(128)} %stack.150.slots, bf16[2,256,384]{2,1,0:T(8,128)(2,1)} %collective-permute-done.14.refs_0_, bf16[2,256,384]{2,1,0:T(8,128)(2,1)} %collective-permute-done.15.refs_1_, bf16[2,256,384]{2,1,0:T(8,128)(2,1)} %collective-permute-done.16.refs_2_, ...), custom_call_target="tpu_custom_call", output_to_operand_aliasing={{}: (5, {})} | custom-call | bytes 3145728 | tf_op jit(solution)/shard_map/pallas_call | solution.py:212
  247.3 3.2 %shard_map.48.refs_4_ = bf16[16384,384]{1,0:T(8,128)(2,1)} custom-call(s32[8]{0:T(128)} %stack.150.slots, bf16[2,384,384]{2,1,0:T(8,128)(2,1)} %copy-done.6, bf16[2,384,384]{2,1,0:T(8,128)(2,1)} %copy-done.7, bf16[2,384,384]{2,1,0:T(8,128)(2,1)} %copy-done.8, bf16[2,384,384]{2,1,0:T(8,128)(2,1)} %copy-done.9, ...), custom_call_target="tpu_custom_call", output_to_operand_aliasing={{}: (5, {})} | custom-call | bytes 4718592 | tf_op jit(solution)/shard_map/pallas_call | solution.py:212
  250.5 3.2 %shard_map.49.refs_4_ = bf16[16384,384]{1,0:T(8,128)(2,1)} custom-call(s32[8]{0:T(128)} %stack.150.slots, bf16[2,384,384]{2,1,0:T(8,128)(2,1)} %copy-done.10, bf16[2,384,384]{2,1,0:T(8,128)(2,1)} %copy-done.11, bf16[2,384,384]{2,1,0:T(8,128)(2,1)} %collective-permute-done.24.refs_2_, ...), custom_call_target="tpu_custom_call", output_to_operand_aliasing={{}: (5, {})} | custom-call | bytes 4718592 | tf_op jit(solution)/shard_map/pallas_call | solution.py:212
  253.7 3.2 %shard_map.50.refs_4_ = bf16[16384,384]{1,0:T(8,128)(2,1)} custom-call(s32[8]{0:T(128)} %stack.150.slots, bf16[2,384,384]{2,1,0:T(8,128)(2,1)} %collective-permute-done.26.refs_0_, bf16[2,384,384]{2,1,0:T(8,128)(2,1)} %collective-permute-done.31.refs_1_, bf16[2,384,384]{2,1,0:T(8,128)(2,1)} %collective-permute-done.32.refs_2_, ...), custom_call_target="tpu_custom_call", output_to_operand_aliasing={{}: (5, {})} | custom-call | bytes 4718592 | tf_op jit(solution)/shard_map/pallas_call | solution.py:212
  257.2 10.9 %collective-permute-done.28.refs_1_ = bf16[2,384,384]{2,1,0:T(8,128)(2,1)} collective-permute-done((bf16[2,384,384]{2,1,0:T(8,128)(2,1)}, bf16[2,384,384]{2,1,0:T(8,128)(2,1)}, u32[]{:S(2)}, u32[]{:S(2)}) %collective-permute-start.28) | collective-permute-done | bytes 589856 | tf_op jit(solution)/shard_map/ppermute | solution.py:313
  268.1 1.8 collective-permute-done.29.refs_2_
  269.9 10.2 %collective-permute-done.30.refs_3_ = bf16[2,384,384]{2,1,0:T(8,128)(2,1)} collective-permute-done((bf16[2,384,384]{2,1,0:T(8,128)(2,1)}, bf16[2,384,384]{2,1,0:T(8,128)(2,1)}, u32[]{:S(2)}, u32[]{:S(2)}) %collective-permute-start.30) | collective-permute-done | bytes 589856 | tf_op jit(solution)/shard_map/ppermute | solution.py:313
  280.1 3.2 %shard_map.51 = bf16[16384,384]{1,0:T(8,128)(2,1)} custom-call(s32[8]{0:T(128)} %stack.150.slots, bf16[2,384,384]{2,1,0:T(8,128)(2,1)} %collective-permute-done.27.refs_0_, bf16[2,384,384]{2,1,0:T(8,128)(2,1)} %collective-permute-done.28.refs_1_, bf16[2,384,384]{2,1,0:T(8,128)(2,1)} %collective-permute-done.29.refs_2_, ...), custom_call_target="tpu_custom_call", output_to_operand_aliasing={{}: (5, {})} | custom-call | bytes 4718592 | tf_op jit(solution)/shard_map/pallas_call | solution.py:212
  (66 shorter events, 4.7 us)
Async XLA Ops:
  3.3 22.4 %all-to-all-start = ((bf16[16,32,768]{2,1,0:T(8,128)(2,1)}), bf16[16,32,768]{2,1,0:T(8,128)(2,1)S(1)}, u32[]{:S(2)}, u32[]{:S(2)}) async-start(bf16[16,32,768]{2,1,0:T(8,128)(2,1)} %pad_maximum_fusion), calls=%async_computation | async-start | bytes 1572864 | tf_op jit(solution)/shard_map/all_to_all | solution.py:241
  10.4 13.1 %collective-permute-start.1 = (bf16[2,32,1024]{2,1,0:T(8,128)(2,1)S(1)}, bf16[2,32,1024]{2,1,0:T(8,128)(2,1)S(1)}, u32[]{:S(2)}, u32[]{:S(2)}) collective-permute-start(bf16[2,32,1024]{2,1,0:T(8,128)(2,1)S(1)} %get-tuple-element.162), channel_id=1, source_target_pairs={{0,2},{1,3},{2,0},{3,1},{4,6},{5,7},{6,4},{7,5},{8,10},{9,11},{10,... | collective-permute-start | bytes 393224 | tf_op jit(solution)/shard_map/ppermute | solution.py:237
  12.3 13.4 %collective-permute-start = (bf16[2,32,1024]{2,1,0:T(8,128)(2,1)S(1)}, bf16[2,32,1024]{2,1,0:T(8,128)(2,1)S(1)}, u32[]{:S(2)}, u32[]{:S(2)}) collective-permute-start(bf16[2,32,1024]{2,1,0:T(8,128)(2,1)S(1)} %get-tuple-element.162), channel_id=1, source_target_pairs={{0,3},{1,0},{2,1},{3,2},{4,7},{5,4},{6,5},{7,6},{8,11},{9,8},{10,9... | collective-permute-start | bytes 393224 | tf_op jit(solution)/shard_map/ppermute | solution.py:237
  13.5 12.2 %collective-permute-start.2 = (bf16[2,32,1024]{2,1,0:T(8,128)(2,1)S(1)}, bf16[2,32,1024]{2,1,0:T(8,128)(2,1)S(1)}, u32[]{:S(2)}, u32[]{:S(2)}) collective-permute-start(bf16[2,32,1024]{2,1,0:T(8,128)(2,1)S(1)} %get-tuple-element.162), channel_id=1, source_target_pairs={{0,1},{1,2},{2,3},{3,0},{4,5},{5,6},{6,7},{7,4},{8,9},{9,10},{10,1... | collective-permute-start | bytes 393224 | tf_op jit(solution)/shard_map/ppermute | solution.py:237
  25.8 33.2 %copy-start.3 = (bf16[4,2,32,1024]{3,2,1,0:T(8,128)(2,1)}, bf16[4,2,32,1024]{3,2,1,0:T(8,128)(2,1)S(1)}, u32[]{:S(2)}) copy-start(bf16[4,2,32,1024]{3,2,1,0:T(8,128)(2,1)S(1)} %pad_maximum_fusion.1.l0) | copy-start | bytes 1572868
  25.8 33.2 %copy-start = (bf16[16,32,768]{2,1,0:T(8,128)(2,1)}, bf16[16,32,768]{2,1,0:T(8,128)(2,1)S(1)}, u32[]{:S(2)}) copy-start(bf16[16,32,768]{2,1,0:T(8,128)(2,1)S(1)} %all-to-all-done) | copy-start | bytes 2359300
  25.8 43.4 %all-to-all-start.1 = ((bf16[8,2,256,384]{3,2,1,0:T(8,128)(2,1)}), bf16[8,2,256,384]{3,2,1,0:T(8,128)(2,1)}, u32[]{:S(2)}, u32[]{:S(2)}) async-start(bf16[8,2,256,384]{3,2,1,0:T(8,128)(2,1)} %shard_map.37), calls=%async_computation.1 | async-start | bytes 6291456 | tf_op jit(solution)/shard_map/all_to_all | solution.py:256
  32.4 18.9 %collective-permute-start.8 = (bf16[2,8,32,768]{3,2,1,0:T(8,128)(2,1)S(1)}, bf16[2,8,32,768]{3,2,1,0:T(8,128)(2,1)S(1)}, u32[]{:S(2)}, u32[]{:S(2)}) collective-permute-start(bf16[2,8,32,768]{3,2,1,0:T(8,128)(2,1)S(1)} %bitcast.55), channel_id=1, source_target_pairs={{0,32},{1,33},{2,34},{3,35},{4,36},{5,37},{6,38},{7,39},{8,40},{9,... | collective-permute-start | bytes 2359304 | tf_op jit(solution)/shard_map/ppermute | solution.py:237
  33.8 19.7 %collective-permute-start.6 = (bf16[2,8,32,768]{3,2,1,0:T(8,128)(2,1)S(1)}, bf16[2,8,32,768]{3,2,1,0:T(8,128)(2,1)S(1)}, u32[]{:S(2)}, u32[]{:S(2)}) collective-permute-start(bf16[2,8,32,768]{3,2,1,0:T(8,128)(2,1)S(1)} %bitcast.56), channel_id=1, source_target_pairs={{0,96},{1,97},{2,98},{3,99},{4,100},{5,101},{6,102},{7,103},{8,104... | collective-permute-start | bytes 2359304 | tf_op jit(solution)/shard_map/ppermute | solution.py:237
  33.9 25.1 %collective-permute-start.5 = (bf16[4,2,32,1024]{3,2,1,0:T(8,128)(2,1)S(1)}, bf16[4,2,32,1024]{3,2,1,0:T(8,128)(2,1)S(1)}, u32[]{:S(2)}, u32[]{:S(2)}) collective-permute-start(bf16[4,2,32,1024]{3,2,1,0:T(8,128)(2,1)S(1)} %pad_maximum_fusion.1.l0), channel_id=1, source_target_pairs={{0,12},{1,13},{2,14},{3,15},{4,8},{5,9},{6,10},{7,11},{8,4},{9,5},... | collective-permute-start | bytes 1572872 | tf_op jit(solution)/shard_map/ppermute | solution.py:237
  36.5 22.5 %collective-permute-start.4 = (bf16[4,2,32,1024]{3,2,1,0:T(8,128)(2,1)S(1)}, bf16[4,2,32,1024]{3,2,1,0:T(8,128)(2,1)S(1)}, u32[]{:S(2)}, u32[]{:S(2)}) collective-permute-start(bf16[4,2,32,1024]{3,2,1,0:T(8,128)(2,1)S(1)} %pad_maximum_fusion.1.l0), channel_id=1, source_target_pairs={{0,8},{1,9},{2,10},{3,11},{4,12},{5,13},{6,14},{7,15},{8,0},{9,1},... | collective-permute-start | bytes 1572872 | tf_op jit(solution)/shard_map/ppermute | solution.py:237
  36.5 24.7 %collective-permute-start.3 = (bf16[4,2,32,1024]{3,2,1,0:T(8,128)(2,1)S(1)}, bf16[4,2,32,1024]{3,2,1,0:T(8,128)(2,1)}, u32[]{:S(2)}, u32[]{:S(2)}) collective-permute-start(bf16[4,2,32,1024]{3,2,1,0:T(8,128)(2,1)S(1)} %pad_maximum_fusion.1.l0), channel_id=1, source_target_pairs={{0,4},{1,5},{2,6},{3,7},{4,0},{5,1},{6,2},{7,3},{8,12},{9,13},{10,... | collective-permute-start | bytes 1572872 | tf_op jit(solution)/shard_map/ppermute | solution.py:237
  51.3 17.9 %copy-start.1 = (bf16[2,8,32,768]{3,2,1,0:T(8,128)(2,1)}, bf16[2,8,32,768]{3,2,1,0:T(8,128)(2,1)S(1)}, u32[]{:S(2)}) copy-start(bf16[2,8,32,768]{3,2,1,0:T(8,128)(2,1)S(1)} %collective-permute-done.8) | copy-start | bytes 2359300
  52.1 9.8 %collective-permute-start.9 = (bf16[1,8,32,768]{3,2,1,0:T(8,128)(2,1)}, bf16[1,8,32,768]{3,2,1,0:T(8,128)(2,1)}, u32[]{:S(2)}, u32[]{:S(2)}) collective-permute-start(bf16[1,8,32,768]{3,2,1,0:T(8,128)(2,1)} %slice.9), channel_id=1, source_target_pairs={{0,32},{1,33},{2,34},{3,35},{4,36},{5,37},{6,38},{7,39},{8,40},{9,... | collective-permute-start | bytes 1179656 | tf_op jit(solution)/shard_map/ppermute | solution.py:237
  53.5 15.7 %copy-start.2 = (bf16[2,8,32,768]{3,2,1,0:T(8,128)(2,1)}, bf16[2,8,32,768]{3,2,1,0:T(8,128)(2,1)S(1)}, u32[]{:S(2)}) copy-start(bf16[2,8,32,768]{3,2,1,0:T(8,128)(2,1)S(1)} %collective-permute-done.6) | copy-start | bytes 2359300
  54.3 9.6 %collective-permute-start.7 = (bf16[1,8,32,768]{3,2,1,0:T(8,128)(2,1)}, bf16[1,8,32,768]{3,2,1,0:T(8,128)(2,1)}, u32[]{:S(2)}, u32[]{:S(2)}) collective-permute-start(bf16[1,8,32,768]{3,2,1,0:T(8,128)(2,1)} %slice.8), channel_id=1, source_target_pairs={{0,96},{1,97},{2,98},{3,99},{4,100},{5,101},{6,102},{7,103},{8,104... | collective-permute-start | bytes 1179656 | tf_op jit(solution)/shard_map/ppermute | solution.py:237
  59.0 16.5 %copy-start.4 = (bf16[4,2,32,1024]{3,2,1,0:T(8,128)(2,1)}, bf16[4,2,32,1024]{3,2,1,0:T(8,128)(2,1)S(1)}, u32[]{:S(2)}) copy-start(bf16[4,2,32,1024]{3,2,1,0:T(8,128)(2,1)S(1)} %collective-permute-done.5.l3) | copy-start | bytes 1572868
  59.0 2.2 copy-start.5
  69.2 59.6 %all-to-all-start.2 = ((bf16[8,2,384,384]{3,2,1,0:T(8,128)(2,1)}), bf16[8,2,384,384]{3,2,1,0:T(8,128)(2,1)}, u32[]{:S(2)}, u32[]{:S(2)}) async-start(bf16[8,2,384,384]{3,2,1,0:T(8,128)(2,1)} %shard_map.38), calls=%async_computation.2 | async-start | bytes 9437184 | tf_op jit(solution)/shard_map/all_to_all | solution.py:256
  82.6 17.7 %collective-permute-start.10 = (bf16[2,256,384]{2,1,0:T(8,128)(2,1)}, bf16[2,256,384]{2,1,0:T(8,128)(2,1)}, u32[]{:S(2)}, u32[]{:S(2)}) collective-permute-start(bf16[2,256,384]{2,1,0:T(8,128)(2,1)} %get-tuple-element.94), channel_id=1, source_target_pairs={{0,0},{1,1},{2,2},{3,3},{4,64},{5,65},{6,66},{7,67},{8,12},{9,13},... | collective-permute-start | bytes 1179656 | tf_op jit(solution)/shard_map/ppermute | solution.py:313
  84.6 20.6 %collective-permute-start.11 = (bf16[2,256,384]{2,1,0:T(8,128)(2,1)}, bf16[2,256,384]{2,1,0:T(8,128)(2,1)}, u32[]{:S(2)}, u32[]{:S(2)}) collective-permute-start(bf16[2,256,384]{2,1,0:T(8,128)(2,1)} %get-tuple-element.100), channel_id=1, source_target_pairs={{0,4},{1,5},{2,6},{3,7},{4,68},{5,69},{6,70},{7,71},{8,8},{9,9},{1... | collective-permute-start | bytes 1179656 | tf_op jit(solution)/shard_map/ppermute | solution.py:313
  91.0 14.1 %collective-permute-start.12 = (bf16[2,256,384]{2,1,0:T(8,128)(2,1)}, bf16[2,256,384]{2,1,0:T(8,128)(2,1)}, u32[]{:S(2)}, u32[]{:S(2)}) collective-permute-start(bf16[2,256,384]{2,1,0:T(8,128)(2,1)} %get-tuple-element.101), channel_id=1, source_target_pairs={{0,32},{1,33},{2,34},{3,35},{4,96},{5,97},{6,98},{7,99},{8,44},{9,... | collective-permute-start | bytes 1179656 | tf_op jit(solution)/shard_map/ppermute | solution.py:313
  91.1 18.7 %collective-permute-start.13 = (bf16[2,256,384]{2,1,0:T(8,128)(2,1)}, bf16[2,256,384]{2,1,0:T(8,128)(2,1)}, u32[]{:S(2)}, u32[]{:S(2)}) collective-permute-start(bf16[2,256,384]{2,1,0:T(8,128)(2,1)} %get-tuple-element.102), channel_id=1, source_target_pairs={{0,36},{1,37},{2,38},{3,39},{4,100},{5,101},{6,102},{7,103},{8,40}... | collective-permute-start | bytes 1179656 | tf_op jit(solution)/shard_map/ppermute | solution.py:313
  100.4 16.2 %collective-permute-start.14 = (bf16[2,256,384]{2,1,0:T(8,128)(2,1)}, bf16[2,256,384]{2,1,0:T(8,128)(2,1)}, u32[]{:S(2)}, u32[]{:S(2)}) collective-permute-start(bf16[2,256,384]{2,1,0:T(8,128)(2,1)} %get-tuple-element.103), channel_id=1, source_target_pairs={{0,16},{1,17},{2,18},{3,19},{4,80},{5,81},{6,82},{7,83},{8,28},{9,... | collective-permute-start | bytes 1179656 | tf_op jit(solution)/shard_map/ppermute | solution.py:313
  100.6 19.7 %collective-permute-start.15 = (bf16[2,256,384]{2,1,0:T(8,128)(2,1)}, bf16[2,256,384]{2,1,0:T(8,128)(2,1)}, u32[]{:S(2)}, u32[]{:S(2)}) collective-permute-start(bf16[2,256,384]{2,1,0:T(8,128)(2,1)} %get-tuple-element.104), channel_id=1, source_target_pairs={{0,20},{1,21},{2,22},{3,23},{4,84},{5,85},{6,86},{7,87},{8,24},{9,... | collective-permute-start | bytes 1179656 | tf_op jit(solution)/shard_map/ppermute | solution.py:313
  105.1 19.3 %collective-permute-start.16 = (bf16[2,256,384]{2,1,0:T(8,128)(2,1)}, bf16[2,256,384]{2,1,0:T(8,128)(2,1)}, u32[]{:S(2)}, u32[]{:S(2)}) collective-permute-start(bf16[2,256,384]{2,1,0:T(8,128)(2,1)} %get-tuple-element.105), channel_id=1, source_target_pairs={{0,48},{1,49},{2,50},{3,51},{4,112},{5,113},{6,114},{7,115},{8,60}... | collective-permute-start | bytes 1179656 | tf_op jit(solution)/shard_map/ppermute | solution.py:313
  105.1 23.7 %collective-permute-start.17 = (bf16[2,256,384]{2,1,0:T(8,128)(2,1)}, bf16[2,256,384]{2,1,0:T(8,128)(2,1)}, u32[]{:S(2)}, u32[]{:S(2)}) collective-permute-start(bf16[2,256,384]{2,1,0:T(8,128)(2,1)} %get-tuple-element.106), channel_id=1, source_target_pairs={{0,52},{1,53},{2,54},{3,55},{4,116},{5,117},{6,118},{7,119},{8,56}... | collective-permute-start | bytes 1179656 | tf_op jit(solution)/shard_map/ppermute | solution.py:313
  128.8 59.2 %all-to-all-start.3 = ((bf16[8,2,384,384]{3,2,1,0:T(8,128)(2,1)}), bf16[8,2,384,384]{3,2,1,0:T(8,128)(2,1)}, u32[]{:S(2)}, u32[]{:S(2)}) async-start(bf16[8,2,384,384]{3,2,1,0:T(8,128)(2,1)} %shard_map.43), calls=%async_computation.3 | async-start | bytes 9437184 | tf_op jit(solution)/shard_map/all_to_all | solution.py:256
  142.5 17.6 %collective-permute-start.18 = (bf16[2,384,384]{2,1,0:T(8,128)(2,1)}, bf16[2,384,384]{2,1,0:T(8,128)(2,1)S(1)}, u32[]{:S(2)}, u32[]{:S(2)}) collective-permute-start(bf16[2,384,384]{2,1,0:T(8,128)(2,1)} %get-tuple-element.112), channel_id=1, source_target_pairs={{0,0},{1,1},{2,2},{3,3},{4,64},{5,65},{6,66},{7,67},{8,12},{9,13},... | collective-permute-start | bytes 1769480 | tf_op jit(solution)/shard_map/ppermute | solution.py:313
  144.4 21.8 %collective-permute-start.19 = (bf16[2,384,384]{2,1,0:T(8,128)(2,1)}, bf16[2,384,384]{2,1,0:T(8,128)(2,1)S(1)}, u32[]{:S(2)}, u32[]{:S(2)}) collective-permute-start(bf16[2,384,384]{2,1,0:T(8,128)(2,1)} %get-tuple-element.118), channel_id=1, source_target_pairs={{0,4},{1,5},{2,6},{3,7},{4,68},{5,69},{6,70},{7,71},{8,8},{9,9},{1... | collective-permute-start | bytes 1769480 | tf_op jit(solution)/shard_map/ppermute | solution.py:313
  150.9 20.9 %collective-permute-start.20 = (bf16[2,384,384]{2,1,0:T(8,128)(2,1)}, bf16[2,384,384]{2,1,0:T(8,128)(2,1)S(1)}, u32[]{:S(2)}, u32[]{:S(2)}) collective-permute-start(bf16[2,384,384]{2,1,0:T(8,128)(2,1)} %get-tuple-element.119), channel_id=1, source_target_pairs={{0,32},{1,33},{2,34},{3,35},{4,96},{5,97},{6,98},{7,99},{8,44},{9,... | collective-permute-start | bytes 1769480 | tf_op jit(solution)/shard_map/ppermute | solution.py:313
  151.0 45.5 %collective-permute-start.21 = (bf16[2,384,384]{2,1,0:T(8,128)(2,1)}, bf16[2,384,384]{2,1,0:T(8,128)(2,1)S(1)}, u32[]{:S(2)}, u32[]{:S(2)}) collective-permute-start(bf16[2,384,384]{2,1,0:T(8,128)(2,1)} %get-tuple-element.120), channel_id=1, source_target_pairs={{0,36},{1,37},{2,38},{3,39},{4,100},{5,101},{6,102},{7,103},{8,40}... | collective-permute-start | bytes 1769480 | tf_op jit(solution)/shard_map/ppermute | solution.py:313
  160.1 84.2 %copy-start.6 = (bf16[2,384,384]{2,1,0:T(8,128)(2,1)}, bf16[2,384,384]{2,1,0:T(8,128)(2,1)S(1)}, u32[]{:S(2)}) copy-start(bf16[2,384,384]{2,1,0:T(8,128)(2,1)S(1)} %collective-permute-done.18.refs_0_) | copy-start | bytes 1769476
  160.1 36.4 %collective-permute-start.22 = (bf16[2,384,384]{2,1,0:T(8,128)(2,1)}, bf16[2,384,384]{2,1,0:T(8,128)(2,1)S(1)}, u32[]{:S(2)}, u32[]{:S(2)}) collective-permute-start(bf16[2,384,384]{2,1,0:T(8,128)(2,1)} %get-tuple-element.121), channel_id=1, source_target_pairs={{0,16},{1,17},{2,18},{3,19},{4,80},{5,81},{6,82},{7,83},{8,28},{9,... | collective-permute-start | bytes 1769480 | tf_op jit(solution)/shard_map/ppermute | solution.py:313
  161.7 37.4 %collective-permute-start.23 = (bf16[2,384,384]{2,1,0:T(8,128)(2,1)}, bf16[2,384,384]{2,1,0:T(8,128)(2,1)S(1)}, u32[]{:S(2)}, u32[]{:S(2)}) collective-permute-start(bf16[2,384,384]{2,1,0:T(8,128)(2,1)} %get-tuple-element.122), channel_id=1, source_target_pairs={{0,20},{1,21},{2,22},{3,23},{4,84},{5,85},{6,86},{7,87},{8,24},{9,... | collective-permute-start | bytes 1769480 | tf_op jit(solution)/shard_map/ppermute | solution.py:313
  166.2 78.1 %copy-start.7 = (bf16[2,384,384]{2,1,0:T(8,128)(2,1)}, bf16[2,384,384]{2,1,0:T(8,128)(2,1)S(1)}, u32[]{:S(2)}) copy-start(bf16[2,384,384]{2,1,0:T(8,128)(2,1)S(1)} %collective-permute-done.19.refs_1_) | copy-start | bytes 1769476
  166.2 37.8 %collective-permute-start.24 = (bf16[2,384,384]{2,1,0:T(8,128)(2,1)}, bf16[2,384,384]{2,1,0:T(8,128)(2,1)}, u32[]{:S(2)}, u32[]{:S(2)}) collective-permute-start(bf16[2,384,384]{2,1,0:T(8,128)(2,1)} %get-tuple-element.123), channel_id=1, source_target_pairs={{0,48},{1,49},{2,50},{3,51},{4,112},{5,113},{6,114},{7,115},{8,60}... | collective-permute-start | bytes 1769480 | tf_op jit(solution)/shard_map/ppermute | solution.py:313
  171.7 72.6 %copy-start.8 = (bf16[2,384,384]{2,1,0:T(8,128)(2,1)}, bf16[2,384,384]{2,1,0:T(8,128)(2,1)S(1)}, u32[]{:S(2)}) copy-start(bf16[2,384,384]{2,1,0:T(8,128)(2,1)S(1)} %collective-permute-done.20.refs_2_) | copy-start | bytes 1769476
  171.7 39.5 %collective-permute-start.25 = (bf16[2,384,384]{2,1,0:T(8,128)(2,1)}, bf16[2,384,384]{2,1,0:T(8,128)(2,1)}, u32[]{:S(2)}, u32[]{:S(2)}) collective-permute-start(bf16[2,384,384]{2,1,0:T(8,128)(2,1)} %get-tuple-element.124), channel_id=1, source_target_pairs={{0,52},{1,53},{2,54},{3,55},{4,116},{5,117},{6,118},{7,119},{8,56}... | collective-permute-start | bytes 1769480 | tf_op jit(solution)/shard_map/ppermute | solution.py:313
  196.5 50.8 %copy-start.9 = (bf16[2,384,384]{2,1,0:T(8,128)(2,1)}, bf16[2,384,384]{2,1,0:T(8,128)(2,1)S(1)}, u32[]{:S(2)}) copy-start(bf16[2,384,384]{2,1,0:T(8,128)(2,1)S(1)} %collective-permute-done.21.refs_3_) | copy-start | bytes 1769476
  196.5 50.8 %copy-start.10 = (bf16[2,384,384]{2,1,0:T(8,128)(2,1)}, bf16[2,384,384]{2,1,0:T(8,128)(2,1)S(1)}, u32[]{:S(2)}) copy-start(bf16[2,384,384]{2,1,0:T(8,128)(2,1)S(1)} %collective-permute-done.22.refs_0_) | copy-start | bytes 1769476
  199.1 48.2 %copy-start.11 = (bf16[2,384,384]{2,1,0:T(8,128)(2,1)}, bf16[2,384,384]{2,1,0:T(8,128)(2,1)S(1)}, u32[]{:S(2)}) copy-start(bf16[2,384,384]{2,1,0:T(8,128)(2,1)S(1)} %collective-permute-done.23.refs_1_) | copy-start | bytes 1769476
  211.2 20.4 %collective-permute-start.26 = (bf16[2,384,384]{2,1,0:T(8,128)(2,1)}, bf16[2,384,384]{2,1,0:T(8,128)(2,1)}, u32[]{:S(2)}, u32[]{:S(2)}) collective-permute-start(bf16[2,384,384]{2,1,0:T(8,128)(2,1)} %get-tuple-element.130), channel_id=1, source_target_pairs={{0,0},{1,1},{2,2},{3,3},{4,64},{5,65},{6,66},{7,67},{8,12},{9,13},... | collective-permute-start | bytes 1769480 | tf_op jit(solution)/shard_map/ppermute | solution.py:313
  213.2 21.8 %collective-permute-start.31 = (bf16[2,384,384]{2,1,0:T(8,128)(2,1)}, bf16[2,384,384]{2,1,0:T(8,128)(2,1)}, u32[]{:S(2)}, u32[]{:S(2)}) collective-permute-start(bf16[2,384,384]{2,1,0:T(8,128)(2,1)} %get-tuple-element.140), channel_id=1, source_target_pairs={{0,4},{1,5},{2,6},{3,7},{4,68},{5,69},{6,70},{7,71},{8,8},{9,9},{1... | collective-permute-start | bytes 1769480 | tf_op jit(solution)/shard_map/ppermute | solution.py:313
  215.1 25.6 %collective-permute-start.32 = (bf16[2,384,384]{2,1,0:T(8,128)(2,1)}, bf16[2,384,384]{2,1,0:T(8,128)(2,1)}, u32[]{:S(2)}, u32[]{:S(2)}) collective-permute-start(bf16[2,384,384]{2,1,0:T(8,128)(2,1)} %get-tuple-element.141), channel_id=1, source_target_pairs={{0,32},{1,33},{2,34},{3,35},{4,96},{5,97},{6,98},{7,99},{8,44},{9,... | collective-permute-start | bytes 1769480 | tf_op jit(solution)/shard_map/ppermute | solution.py:313
  215.2 38.6 %collective-permute-start.33 = (bf16[2,384,384]{2,1,0:T(8,128)(2,1)}, bf16[2,384,384]{2,1,0:T(8,128)(2,1)}, u32[]{:S(2)}, u32[]{:S(2)}) collective-permute-start(bf16[2,384,384]{2,1,0:T(8,128)(2,1)} %get-tuple-element.142), channel_id=1, source_target_pairs={{0,36},{1,37},{2,38},{3,39},{4,100},{5,101},{6,102},{7,103},{8,40}... | collective-permute-start | bytes 1769480 | tf_op jit(solution)/shard_map/ppermute | solution.py:313
  231.7 25.5 %collective-permute-start.27 = (bf16[2,384,384]{2,1,0:T(8,128)(2,1)}, bf16[2,384,384]{2,1,0:T(8,128)(2,1)}, u32[]{:S(2)}, u32[]{:S(2)}) collective-permute-start(bf16[2,384,384]{2,1,0:T(8,128)(2,1)} %get-tuple-element.135), channel_id=1, source_target_pairs={{0,16},{1,17},{2,18},{3,19},{4,80},{5,81},{6,82},{7,83},{8,28},{9,... | collective-permute-start | bytes 1769480 | tf_op jit(solution)/shard_map/ppermute | solution.py:313
  231.7 36.4 %collective-permute-start.28 = (bf16[2,384,384]{2,1,0:T(8,128)(2,1)}, bf16[2,384,384]{2,1,0:T(8,128)(2,1)}, u32[]{:S(2)}, u32[]{:S(2)}) collective-permute-start(bf16[2,384,384]{2,1,0:T(8,128)(2,1)} %get-tuple-element.136), channel_id=1, source_target_pairs={{0,20},{1,21},{2,22},{3,23},{4,84},{5,85},{6,86},{7,87},{8,24},{9,... | collective-permute-start | bytes 1769480 | tf_op jit(solution)/shard_map/ppermute | solution.py:313
  235.0 35.0 %collective-permute-start.29 = (bf16[2,384,384]{2,1,0:T(8,128)(2,1)}, bf16[2,384,384]{2,1,0:T(8,128)(2,1)}, u32[]{:S(2)}, u32[]{:S(2)}) collective-permute-start(bf16[2,384,384]{2,1,0:T(8,128)(2,1)} %get-tuple-element.137), channel_id=1, source_target_pairs={{0,48},{1,49},{2,50},{3,51},{4,112},{5,113},{6,114},{7,115},{8,60}... | collective-permute-start | bytes 1769480 | tf_op jit(solution)/shard_map/ppermute | solution.py:313
  240.7 39.4 %collective-permute-start.30 = (bf16[2,384,384]{2,1,0:T(8,128)(2,1)}, bf16[2,384,384]{2,1,0:T(8,128)(2,1)}, u32[]{:S(2)}, u32[]{:S(2)}) collective-permute-start(bf16[2,384,384]{2,1,0:T(8,128)(2,1)} %get-tuple-element.138), channel_id=1, source_target_pairs={{0,52},{1,53},{2,54},{3,55},{4,116},{5,117},{6,118},{7,119},{8,56}... | collective-permute-start | bytes 1769480 | tf_op jit(solution)/shard_map/ppermute | solution.py:313

commit v4 on v3

--- a/solution.py
+++ b/solution.py
@@ -12,6 +12,7 @@
 SIZES = (4, 2, 2, 2, 4)
 CHUNKS = ((0, 256), (256, 384), (640, 384))
 HALF = 4
+EARLY = 4
 ORDER = (0, 4, 1, 5, 2, 6, 3, 7)
 AHEAD = 8
 VMEM = 60 << 20
@@ -305,11 +306,13 @@
     arrived = first(1)
     for s in range(count):
         if s:
-            got, sent[:HALF] = tie((got, sent[:HALF]))
+            got[:EARLY], sent[:HALF] = tie((got[:EARLY], sent[:HALF]))
         new = []
         for k in range(8):
             if k == HALF:
-                new[0], sent[HALF:] = tie((new[0], sent[HALF:]))
+                new[0], got[EARLY:], sent[HALF:] = tie(
+                    (new[0], got[EARLY:], sent[HALF:])
+                )
             new.append(lax.ppermute(sent[k], AXES, pairs(ORDER[k])))
         if got:
             merged = finish(s - 1, got, merged)

time: 285 us -> 284 us (level)
  the two profiles are of different devices: /device:TPU:75 before, /device:TPU:15 now
where the time goes in v4:
time: 284 us; the launch traced here: 283 us
  starting transfers between devices  110 us (39%)
  waiting for transfers between devices  84.8 us (30%)
  Pallas kernels  78.9 us (28%)
  local copies, waits for them, and re-layouts  4.14 us (1%)
  other arithmetic  3.49 us (1%)
    ppermute x24, starting transfers between devices, body(): new.append(lax.ppermute(sent[k], AXES, pairs(ORDER[k])))  73.8 us
    pallas_call x6, Pallas kernels, add(): pl.pallas_call(functools.partial(add_kernel, start, rows, block, first),...  47.8 us
    ppermute x24, waiting for transfers between devices, body(): new.append(lax.ppermute(sent[k], AXES, pairs(ORDER[k])))  34.4 us
    ppermute x10, waiting for transfers between devices, across(): return lax.ppermute(value, AXES, moved(change))  25.9 us
    all_to_all x3, waiting for transfers between devices, first(): return lax.all_to_all(packed[i], ('c', 'y'), 0, 0, tiled=True)  24.6 us
    pallas_call x6, Pallas kernels, place(): pl.pallas_call(functools.partial(place_kernel, start, rows, height, first...  18.7 us
    all_to_all x3, starting transfers between devices, first(): return lax.all_to_all(packed[i], ('c', 'y'), 0, 0, tiled=True)  17.3 us
    ppermute x10, starting transfers between devices, across(): return lax.ppermute(value, AXES, moved(change))  13.3 us
  transfers between devices with their start and end apart: 38, of which 15 were waited for; matrix products, arithmetic and copies ran while one was open for 1% of the time, Pallas kernels for 27%

profile of v4, /device:TPU:15, one launch (start us, length us, event | category | flops | bytes accessed | tf_op | source)
XLA Modules:
  0.0 282.5 jit_solution(5289878060455463419)
XLA Ops:
  0.0 1.0 reduce-precision_convert_fusion
  2.4 0.9 pad_maximum_fusion
  3.3 6.1 %all-to-all-start = ((bf16[16,32,768]{2,1,0:T(8,128)(2,1)}), bf16[16,32,768]{2,1,0:T(8,128)(2,1)S(1)}, u32[]{:S(2)}, u32[]{:S(2)}) async-start(bf16[16,32,768]{2,1,0:T(8,128)(2,1)} %pad_maximum_fusion), calls=%async_computation | async-start | bytes 1572864 | tf_op jit(solution)/shard_map/all_to_all | solution.py:242
  9.5 0.9 fusion.3
  10.4 1.9 collective-permute-start.1
  12.3 1.2 collective-permute-start
  13.8 3.3 %shard_map.37 = bf16[8,2,256,384]{3,2,1,0:T(8,128)(2,1)} custom-call(bf16[1024,6144]{1,0:T(8,128)(2,1)} %base.5), custom_call_target="tpu_custom_call" | custom-call | bytes 6291456 | tf_op jit(solution)/shard_map/pallas_call | solution.py:92
  17.1 6.5 %collective-permute-done.1 = bf16[2,32,1024]{2,1,0:T(8,128)(2,1)S(1)} collective-permute-done((bf16[2,32,1024]{2,1,0:T(8,128)(2,1)S(1)}, bf16[2,32,1024]{2,1,0:T(8,128)(2,1)S(1)}, u32[]{:S(2)}, u32[]{:S(2)}) %collective-permute-start.1) | collective-permute-done | bytes 131104 | tf_op jit(solution)/shard_map/ppermute | solution.py:238
  23.5 2.2 collective-permute-done
  25.8 6.6 %all-to-all-start.1 = ((bf16[8,2,256,384]{3,2,1,0:T(8,128)(2,1)}), bf16[8,2,256,384]{3,2,1,0:T(8,128)(2,1)}, u32[]{:S(2)}, u32[]{:S(2)}) async-start(bf16[8,2,256,384]{3,2,1,0:T(8,128)(2,1)} %shard_map.37), calls=%async_computation.1 | async-start | bytes 6291456 | tf_op jit(solution)/shard_map/all_to_all | solution.py:257
  32.4 1.6 collective-permute-start.8
  34.1 2.1 collective-permute-start.6
  36.2 1.6 collective-permute-start.5
  37.8 1.8 collective-permute-start.3
  39.7 14.2 %collective-permute-done.8 = bf16[2,8,32,768]{3,2,1,0:T(8,128)(2,1)S(1)} collective-permute-done((bf16[2,8,32,768]{3,2,1,0:T(8,128)(2,1)S(1)}, bf16[2,8,32,768]{3,2,1,0:T(8,128)(2,1)S(1)}, u32[]{:S(2)}, u32[]{:S(2)}) %collective-permute-start.8) | collective-permute-done | bytes 786464 | tf_op jit(solution)/shard_map/ppermute | solution.py:238
  53.9 0.8 slice.9
  54.7 0.8 slice.8
  55.6 2.7 collective-permute-start.7
  58.2 4.6 %shard_map.38 = bf16[8,2,384,384]{3,2,1,0:T(8,128)(2,1)} custom-call(bf16[1024,6144]{1,0:T(8,128)(2,1)} %base.5), custom_call_target="tpu_custom_call" | custom-call | bytes 9437184 | tf_op jit(solution)/shard_map/pallas_call | solution.py:92
  63.7 2.4 collective-permute-done.9
  66.1 3.0 %all-to-all-done.1.part = bf16[8,2,256,384]{3,2,1,0:T(8,128)(2,1)} async-done(((bf16[8,2,256,384]{3,2,1,0:T(8,128)(2,1)}), bf16[8,2,256,384]{3,2,1,0:T(8,128)(2,1)}, u32[]{:S(2)}, u32[]{:S(2)}) %all-to-all-start.1) | async-done | bytes 3145760 | tf_op jit(solution)/shard_map/all_to_all | solution.py:257
  69.2 5.7 %all-to-all-start.2 = ((bf16[8,2,384,384]{3,2,1,0:T(8,128)(2,1)}), bf16[8,2,384,384]{3,2,1,0:T(8,128)(2,1)}, u32[]{:S(2)}, u32[]{:S(2)}) async-start(bf16[8,2,384,384]{3,2,1,0:T(8,128)(2,1)} %shard_map.38), calls=%async_computation.2 | async-start | bytes 9437184 | tf_op jit(solution)/shard_map/all_to_all | solution.py:257
  74.8 0.7 stack.174.picks
  75.5 7.1 %shard_map.39 = (bf16[2,256,384]{2,1,0:T(8,128)(2,1)}, bf16[2,256,384]{2,1,0:T(8,128)(2,1)}, bf16[2,256,384]{2,1,0:T(8,128)(2,1)}, bf16[2,256,384]{2,1,0:T(8,128)(2,1)}) custom-call(s32[33]{0:T(128)} %stack.174.picks, bf16[8,2,256,384]{3,2,1,0:T(8,128)(2,1)} %all-to-all-done.1.part, bf16[4,2,32,1024]{3,2,1,0:T(8,128)(2,1)} %copy-done.3, ...), custom_call_target="tpu_custom_call" | custom-call | flops 1207959552 | bytes 8388608 | tf_op jit(solution)/shard_map/pallas_call | solution.py:169
  82.7 5.5 %collective-permute-start.10 = (bf16[2,256,384]{2,1,0:T(8,128)(2,1)}, bf16[2,256,384]{2,1,0:T(8,128)(2,1)}, u32[]{:S(2)}, u32[]{:S(2)}) collective-permute-start(bf16[2,256,384]{2,1,0:T(8,128)(2,1)} %get-tuple-element.94), channel_id=1, source_target_pairs={{0,0},{1,1},{2,2},{3,3},{4,64},{5,65},{6,66},{7,67},{8,12},{9,13},... | collective-permute-start | bytes 1179656 | tf_op jit(solution)/shard_map/ppermute | solution.py:316
  88.2 2.8 collective-permute-start.11
  91.0 3.0 %collective-permute-start.12 = (bf16[2,256,384]{2,1,0:T(8,128)(2,1)}, bf16[2,256,384]{2,1,0:T(8,128)(2,1)}, u32[]{:S(2)}, u32[]{:S(2)}) collective-permute-start(bf16[2,256,384]{2,1,0:T(8,128)(2,1)} %get-tuple-element.101), channel_id=1, source_target_pairs={{0,32},{1,33},{2,34},{3,35},{4,96},{5,97},{6,98},{7,99},{8,44},{9,... | collective-permute-start | bytes 1179656 | tf_op jit(solution)/shard_map/ppermute | solution.py:316
  94.0 1.8 collective-permute-start.13
  95.8 7.1 %shard_map.40 = (bf16[2,256,384]{2,1,0:T(8,128)(2,1)}, bf16[2,256,384]{2,1,0:T(8,128)(2,1)}, bf16[2,256,384]{2,1,0:T(8,128)(2,1)}, bf16[2,256,384]{2,1,0:T(8,128)(2,1)}) custom-call(s32[33]{0:T(128)} %stack.174.picks, bf16[8,2,256,384]{3,2,1,0:T(8,128)(2,1)} %all-to-all-done.1.part, bf16[4,2,32,1024]{3,2,1,0:T(8,128)(2,1)} %copy-done.3, ...), custom_call_target="tpu_custom_call" | custom-call | flops 1207959552 | bytes 8388608 | tf_op jit(solution)/shard_map/pallas_call | solution.py:169
  102.9 1.3 collective-permute-start.15
  104.2 0.9 collective-permute-start.16
  105.1 1.7 collective-permute-start.17
  107.0 2.6 collective-permute-start.18
  109.6 4.6 %shard_map.43 = bf16[8,2,384,384]{3,2,1,0:T(8,128)(2,1)} custom-call(bf16[1024,6144]{1,0:T(8,128)(2,1)} %base.5), custom_call_target="tpu_custom_call" | custom-call | bytes 9437184 | tf_op jit(solution)/shard_map/pallas_call | solution.py:92
  114.1 1.6 collective-permute-done.15.refs_0_
  115.7 8.0 %collective-permute-done.16.refs_1_ = bf16[2,256,384]{2,1,0:T(8,128)(2,1)} collective-permute-done((bf16[2,256,384]{2,1,0:T(8,128)(2,1)}, bf16[2,256,384]{2,1,0:T(8,128)(2,1)}, u32[]{:S(2)}, u32[]{:S(2)}) %collective-permute-start.16) | collective-permute-done | bytes 393248 | tf_op jit(solution)/shard_map/ppermute | solution.py:316
  123.7 0.8 collective-permute-done.17.refs_2_
  124.5 4.5 %collective-permute-done.18.refs_3_ = bf16[2,256,384]{2,1,0:T(8,128)(2,1)} collective-permute-done((bf16[2,256,384]{2,1,0:T(8,128)(2,1)}, bf16[2,256,384]{2,1,0:T(8,128)(2,1)}, u32[]{:S(2)}, u32[]{:S(2)}) %collective-permute-start.18) | collective-permute-done | bytes 393248 | tf_op jit(solution)/shard_map/ppermute | solution.py:316
  129.1 5.0 %all-to-all-start.3 = ((bf16[8,2,384,384]{3,2,1,0:T(8,128)(2,1)}), bf16[8,2,384,384]{3,2,1,0:T(8,128)(2,1)}, u32[]{:S(2)}, u32[]{:S(2)}) async-start(bf16[8,2,384,384]{3,2,1,0:T(8,128)(2,1)} %shard_map.43), calls=%async_computation.3 | async-start | bytes 9437184 | tf_op jit(solution)/shard_map/all_to_all | solution.py:257
  134.1 8.5 %shard_map.41 = (bf16[2,384,384]{2,1,0:T(8,128)(2,1)}, bf16[2,384,384]{2,1,0:T(8,128)(2,1)}, bf16[2,384,384]{2,1,0:T(8,128)(2,1)}, bf16[2,384,384]{2,1,0:T(8,128)(2,1)}) custom-call(s32[33]{0:T(128)} %stack.174.picks, bf16[8,2,384,384]{3,2,1,0:T(8,128)(2,1)} %all-to-all-done.2.part, bf16[4,2,32,1024]{3,2,1,0:T(8,128)(2,1)} %copy-done.3, ...), custom_call_target="tpu_custom_call" | custom-call | flops 1811939328 | bytes 8388608 | tf_op jit(solution)/shard_map/pallas_call | solution.py:169
  142.6 5.5 %collective-permute-start.14 = (bf16[2,384,384]{2,1,0:T(8,128)(2,1)}, bf16[2,384,384]{2,1,0:T(8,128)(2,1)S(1)}, u32[]{:S(2)}, u32[]{:S(2)}) collective-permute-start(bf16[2,384,384]{2,1,0:T(8,128)(2,1)} %get-tuple-element.108), channel_id=1, source_target_pairs={{0,0},{1,1},{2,2},{3,3},{4,64},{5,65},{6,66},{7,67},{8,12},{9,13},... | collective-permute-start | bytes 1769480 | tf_op jit(solution)/shard_map/ppermute | solution.py:316
  148.1 2.8 collective-permute-start.19
  151.1 4.6 %collective-permute-start.21 = (bf16[2,384,384]{2,1,0:T(8,128)(2,1)}, bf16[2,384,384]{2,1,0:T(8,128)(2,1)S(1)}, u32[]{:S(2)}, u32[]{:S(2)}) collective-permute-start(bf16[2,384,384]{2,1,0:T(8,128)(2,1)} %get-tuple-element.120), channel_id=1, source_target_pairs={{0,36},{1,37},{2,38},{3,39},{4,100},{5,101},{6,102},{7,103},{8,40}... | collective-permute-start | bytes 1769480 | tf_op jit(solution)/shard_map/ppermute | solution.py:316
  155.7 8.3 %shard_map.42 = (bf16[2,384,384]{2,1,0:T(8,128)(2,1)}, bf16[2,384,384]{2,1,0:T(8,128)(2,1)}, bf16[2,384,384]{2,1,0:T(8,128)(2,1)}, bf16[2,384,384]{2,1,0:T(8,128)(2,1)}) custom-call(s32[33]{0:T(128)} %stack.174.picks, bf16[8,2,384,384]{3,2,1,0:T(8,128)(2,1)} %all-to-all-done.2.part, bf16[4,2,32,1024]{3,2,1,0:T(8,128)(2,1)} %copy-done.3, ...), custom_call_target="tpu_custom_call" | custom-call | flops 1811939328 | bytes 8388608 | tf_op jit(solution)/shard_map/pallas_call | solution.py:169
  164.1 2.3 collective-permute-start.23
  166.4 21.5 %all-to-all-done.3.part = bf16[8,2,384,384]{3,2,1,0:T(8,128)(2,1)} async-done(((bf16[8,2,384,384]{3,2,1,0:T(8,128)(2,1)}), bf16[8,2,384,384]{3,2,1,0:T(8,128)(2,1)}, u32[]{:S(2)}, u32[]{:S(2)}) %all-to-all-start.3) | async-done | bytes 4718624 | tf_op jit(solution)/shard_map/all_to_all | solution.py:257
  187.9 8.4 %shard_map.44 = (bf16[2,384,384]{2,1,0:T(8,128)(2,1)}, bf16[2,384,384]{2,1,0:T(8,128)(2,1)}, bf16[2,384,384]{2,1,0:T(8,128)(2,1)}, bf16[2,384,384]{2,1,0:T(8,128)(2,1)}) custom-call(s32[33]{0:T(128)} %stack.174.picks, bf16[8,2,384,384]{3,2,1,0:T(8,128)(2,1)} %all-to-all-done.3.part, bf16[4,2,32,1024]{3,2,1,0:T(8,128)(2,1)} %copy-done.3, ...), custom_call_target="tpu_custom_call" | custom-call | flops 1811939328 | bytes 8388608 | tf_op jit(solution)/shard_map/pallas_call | solution.py:169
  196.3 3.8 %collective-permute-start.25 = (bf16[2,384,384]{2,1,0:T(8,128)(2,1)}, bf16[2,384,384]{2,1,0:T(8,128)(2,1)}, u32[]{:S(2)}, u32[]{:S(2)}) collective-permute-start(bf16[2,384,384]{2,1,0:T(8,128)(2,1)} %get-tuple-element.129), channel_id=1, source_target_pairs={{0,48},{1,49},{2,50},{3,51},{4,112},{5,113},{6,114},{7,115},{8,60}... | collective-permute-start | bytes 1769480 | tf_op jit(solution)/shard_map/ppermute | solution.py:316
  200.2 3.4 %collective-permute-start.22 = (bf16[2,384,384]{2,1,0:T(8,128)(2,1)}, bf16[2,384,384]{2,1,0:T(8,128)(2,1)}, u32[]{:S(2)}, u32[]{:S(2)}) collective-permute-start(bf16[2,384,384]{2,1,0:T(8,128)(2,1)} %get-tuple-element.126), channel_id=1, source_target_pairs={{0,0},{1,1},{2,2},{3,3},{4,64},{5,65},{6,66},{7,67},{8,12},{9,13},... | collective-permute-start | bytes 1769480 | tf_op jit(solution)/shard_map/ppermute | solution.py:316
  203.6 4.1 %collective-permute-start.31 = (bf16[2,384,384]{2,1,0:T(8,128)(2,1)}, bf16[2,384,384]{2,1,0:T(8,128)(2,1)}, u32[]{:S(2)}, u32[]{:S(2)}) collective-permute-start(bf16[2,384,384]{2,1,0:T(8,128)(2,1)} %get-tuple-element.140), channel_id=1, source_target_pairs={{0,4},{1,5},{2,6},{3,7},{4,68},{5,69},{6,70},{7,71},{8,8},{9,9},{1... | collective-permute-start | bytes 1769480 | tf_op jit(solution)/shard_map/ppermute | solution.py:316
  207.7 5.7 %collective-permute-start.32 = (bf16[2,384,384]{2,1,0:T(8,128)(2,1)}, bf16[2,384,384]{2,1,0:T(8,128)(2,1)}, u32[]{:S(2)}, u32[]{:S(2)}) collective-permute-start(bf16[2,384,384]{2,1,0:T(8,128)(2,1)} %get-tuple-element.141), channel_id=1, source_target_pairs={{0,32},{1,33},{2,34},{3,35},{4,96},{5,97},{6,98},{7,99},{8,44},{9,... | collective-permute-start | bytes 1769480 | tf_op jit(solution)/shard_map/ppermute | solution.py:316
  213.4 8.4 %shard_map.45 = (bf16[2,384,384]{2,1,0:T(8,128)(2,1)}, bf16[2,384,384]{2,1,0:T(8,128)(2,1)}, bf16[2,384,384]{2,1,0:T(8,128)(2,1)}, bf16[2,384,384]{2,1,0:T(8,128)(2,1)}) custom-call(s32[33]{0:T(128)} %stack.174.picks, bf16[8,2,384,384]{3,2,1,0:T(8,128)(2,1)} %all-to-all-done.3.part, bf16[4,2,32,1024]{3,2,1,0:T(8,128)(2,1)} %copy-done.3, ...), custom_call_target="tpu_custom_call" | custom-call | flops 1811939328 | bytes 8388608 | tf_op jit(solution)/shard_map/pallas_call | solution.py:169
  221.9 4.7 %collective-permute-done.22.refs_0_ = bf16[2,384,384]{2,1,0:T(8,128)(2,1)} collective-permute-done((bf16[2,384,384]{2,1,0:T(8,128)(2,1)}, bf16[2,384,384]{2,1,0:T(8,128)(2,1)}, u32[]{:S(2)}, u32[]{:S(2)}) %collective-permute-start.22) | collective-permute-done | bytes 589856 | tf_op jit(solution)/shard_map/ppermute | solution.py:316
  226.6 16.2 %collective-permute-start.27 = (bf16[2,384,384]{2,1,0:T(8,128)(2,1)}, bf16[2,384,384]{2,1,0:T(8,128)(2,1)}, u32[]{:S(2)}, u32[]{:S(2)}) collective-permute-start(bf16[2,384,384]{2,1,0:T(8,128)(2,1)} %get-tuple-element.135), channel_id=1, source_target_pairs={{0,16},{1,17},{2,18},{3,19},{4,80},{5,81},{6,82},{7,83},{8,28},{9,... | collective-permute-start | bytes 1769480 | tf_op jit(solution)/shard_map/ppermute | solution.py:316
  242.8 2.2 collective-permute-start.29
  245.1 3.2 %collective-permute-start.30 = (bf16[2,384,384]{2,1,0:T(8,128)(2,1)}, bf16[2,384,384]{2,1,0:T(8,128)(2,1)}, u32[]{:S(2)}, u32[]{:S(2)}) collective-permute-start(bf16[2,384,384]{2,1,0:T(8,128)(2,1)} %get-tuple-element.138), channel_id=1, source_target_pairs={{0,52},{1,53},{2,54},{3,55},{4,116},{5,117},{6,118},{7,119},{8,56}... | collective-permute-start | bytes 1769480 | tf_op jit(solution)/shard_map/ppermute | solution.py:316
  249.0 2.9 %shard_map.46.refs_4_ = bf16[16384,384]{1,0:T(8,128)(2,1)} custom-call(s32[8]{0:T(128)} %stack.150.slots, bf16[2,256,384]{2,1,0:T(8,128)(2,1)} %collective-permute-done.10.refs_0_, bf16[2,256,384]{2,1,0:T(8,128)(2,1)} %collective-permute-done.11.refs_1_, bf16[2,256,384]{2,1,0:T(8,128)(2,1)} %collective-permute-done.12.refs_2_, ...), custom_call_target="tpu_custom_call" | custom-call | bytes 3145728 | tf_op jit(solution)/shard_map/pallas_call | solution.py:213
  251.9 2.9 %shard_map.47.refs_4_ = bf16[16384,384]{1,0:T(8,128)(2,1)} custom-call(s32[8]{0:T(128)} %stack.150.slots, bf16[2,256,384]{2,1,0:T(8,128)(2,1)} %collective-permute-done.15.refs_0_, bf16[2,256,384]{2,1,0:T(8,128)(2,1)} %collective-permute-done.16.refs_1_, bf16[2,256,384]{2,1,0:T(8,128)(2,1)} %collective-permute-done.17.refs_2_, ...), custom_call_target="tpu_custom_call", output_to_operand_aliasing={{}: (5, {})} | custom-call | bytes 3145728 | tf_op jit(solution)/shard_map/pallas_call | solution.py:213
  254.8 3.2 %shard_map.48.refs_4_ = bf16[16384,384]{1,0:T(8,128)(2,1)} custom-call(s32[8]{0:T(128)} %stack.150.slots, bf16[2,384,384]{2,1,0:T(8,128)(2,1)} %copy-done.6, bf16[2,384,384]{2,1,0:T(8,128)(2,1)} %copy-done.7, bf16[2,384,384]{2,1,0:T(8,128)(2,1)} %copy-done.8, bf16[2,384,384]{2,1,0:T(8,128)(2,1)} %copy-done.9, ...), custom_call_target="tpu_custom_call", output_to_operand_aliasing={{}: (5, {})} | custom-call | bytes 4718592 | tf_op jit(solution)/shard_map/pallas_call | solution.py:213
  258.1 3.2 %shard_map.49.refs_4_ = bf16[16384,384]{1,0:T(8,128)(2,1)} custom-call(s32[8]{0:T(128)} %stack.150.slots, bf16[2,384,384]{2,1,0:T(8,128)(2,1)} %copy-done.10, bf16[2,384,384]{2,1,0:T(8,128)(2,1)} %copy-done.11, bf16[2,384,384]{2,1,0:T(8,128)(2,1)} %collective-permute-done.25.refs_2_, ...), custom_call_target="tpu_custom_call", output_to_operand_aliasing={{}: (5, {})} | custom-call | bytes 4718592 | tf_op jit(solution)/shard_map/pallas_call | solution.py:213
  261.3 3.2 %shard_map.50.refs_4_ = bf16[16384,384]{1,0:T(8,128)(2,1)} custom-call(s32[8]{0:T(128)} %stack.150.slots, bf16[2,384,384]{2,1,0:T(8,128)(2,1)} %collective-permute-done.22.refs_0_, bf16[2,384,384]{2,1,0:T(8,128)(2,1)} %collective-permute-done.31.refs_1_, bf16[2,384,384]{2,1,0:T(8,128)(2,1)} %collective-permute-done.32.refs_2_, ...), custom_call_target="tpu_custom_call", output_to_operand_aliasing={{}: (5, {})} | custom-call | bytes 4718592 | tf_op jit(solution)/shard_map/pallas_call | solution.py:213
  264.6 3.6 %collective-permute-done.29.refs_2_ = bf16[2,384,384]{2,1,0:T(8,128)(2,1)} collective-permute-done((bf16[2,384,384]{2,1,0:T(8,128)(2,1)}, bf16[2,384,384]{2,1,0:T(8,128)(2,1)}, u32[]{:S(2)}, u32[]{:S(2)}) %collective-permute-start.29) | collective-permute-done | bytes 589856 | tf_op jit(solution)/shard_map/ppermute | solution.py:316
  268.2 10.9 %collective-permute-done.30.refs_3_ = bf16[2,384,384]{2,1,0:T(8,128)(2,1)} collective-permute-done((bf16[2,384,384]{2,1,0:T(8,128)(2,1)}, bf16[2,384,384]{2,1,0:T(8,128)(2,1)}, u32[]{:S(2)}, u32[]{:S(2)}) %collective-permute-start.30) | collective-permute-done | bytes 589856 | tf_op jit(solution)/shard_map/ppermute | solution.py:316
  279.1 3.2 %shard_map.51 = bf16[16384,384]{1,0:T(8,128)(2,1)} custom-call(s32[8]{0:T(128)} %stack.150.slots, bf16[2,384,384]{2,1,0:T(8,128)(2,1)} %collective-permute-done.27.refs_0_, bf16[2,384,384]{2,1,0:T(8,128)(2,1)} %collective-permute-done.28.refs_1_, bf16[2,384,384]{2,1,0:T(8,128)(2,1)} %collective-permute-done.29.refs_2_, ...), custom_call_target="tpu_custom_call", output_to_operand_aliasing={{}: (5, {})} | custom-call | bytes 4718592 | tf_op jit(solution)/shard_map/pallas_call | solution.py:213
  (66 shorter events, 3.8 us)
Async XLA Ops:
  3.3 22.4 %all-to-all-start = ((bf16[16,32,768]{2,1,0:T(8,128)(2,1)}), bf16[16,32,768]{2,1,0:T(8,128)(2,1)S(1)}, u32[]{:S(2)}, u32[]{:S(2)}) async-start(bf16[16,32,768]{2,1,0:T(8,128)(2,1)} %pad_maximum_fusion), calls=%async_computation | async-start | bytes 1572864 | tf_op jit(solution)/shard_map/all_to_all | solution.py:242
  10.4 13.1 %collective-permute-start.1 = (bf16[2,32,1024]{2,1,0:T(8,128)(2,1)S(1)}, bf16[2,32,1024]{2,1,0:T(8,128)(2,1)S(1)}, u32[]{:S(2)}, u32[]{:S(2)}) collective-permute-start(bf16[2,32,1024]{2,1,0:T(8,128)(2,1)S(1)} %get-tuple-element.162), channel_id=1, source_target_pairs={{0,2},{1,3},{2,0},{3,1},{4,6},{5,7},{6,4},{7,5},{8,10},{9,11},{10,... | collective-permute-start | bytes 393224 | tf_op jit(solution)/shard_map/ppermute | solution.py:238
  12.3 13.4 %collective-permute-start = (bf16[2,32,1024]{2,1,0:T(8,128)(2,1)S(1)}, bf16[2,32,1024]{2,1,0:T(8,128)(2,1)S(1)}, u32[]{:S(2)}, u32[]{:S(2)}) collective-permute-start(bf16[2,32,1024]{2,1,0:T(8,128)(2,1)S(1)} %get-tuple-element.162), channel_id=1, source_target_pairs={{0,3},{1,0},{2,1},{3,2},{4,7},{5,4},{6,5},{7,6},{8,11},{9,8},{10,9... | collective-permute-start | bytes 393224 | tf_op jit(solution)/shard_map/ppermute | solution.py:238
  13.5 12.2 %collective-permute-start.2 = (bf16[2,32,1024]{2,1,0:T(8,128)(2,1)S(1)}, bf16[2,32,1024]{2,1,0:T(8,128)(2,1)S(1)}, u32[]{:S(2)}, u32[]{:S(2)}) collective-permute-start(bf16[2,32,1024]{2,1,0:T(8,128)(2,1)S(1)} %get-tuple-element.162), channel_id=1, source_target_pairs={{0,1},{1,2},{2,3},{3,0},{4,5},{5,6},{6,7},{7,4},{8,9},{9,10},{10,1... | collective-permute-start | bytes 393224 | tf_op jit(solution)/shard_map/ppermute | solution.py:238
  25.8 37.1 %copy-start.3 = (bf16[4,2,32,1024]{3,2,1,0:T(8,128)(2,1)}, bf16[4,2,32,1024]{3,2,1,0:T(8,128)(2,1)S(1)}, u32[]{:S(2)}) copy-start(bf16[4,2,32,1024]{3,2,1,0:T(8,128)(2,1)S(1)} %pad_maximum_fusion.1.l0) | copy-start | bytes 1572868
  25.8 37.0 %copy-start = (bf16[16,32,768]{2,1,0:T(8,128)(2,1)}, bf16[16,32,768]{2,1,0:T(8,128)(2,1)S(1)}, u32[]{:S(2)}) copy-start(bf16[16,32,768]{2,1,0:T(8,128)(2,1)S(1)} %all-to-all-done) | copy-start | bytes 2359300
  25.8 43.4 %all-to-all-start.1 = ((bf16[8,2,256,384]{3,2,1,0:T(8,128)(2,1)}), bf16[8,2,256,384]{3,2,1,0:T(8,128)(2,1)}, u32[]{:S(2)}, u32[]{:S(2)}) async-start(bf16[8,2,256,384]{3,2,1,0:T(8,128)(2,1)} %shard_map.37), calls=%async_computation.1 | async-start | bytes 6291456 | tf_op jit(solution)/shard_map/all_to_all | solution.py:257
  32.4 21.5 %collective-permute-start.8 = (bf16[2,8,32,768]{3,2,1,0:T(8,128)(2,1)S(1)}, bf16[2,8,32,768]{3,2,1,0:T(8,128)(2,1)S(1)}, u32[]{:S(2)}, u32[]{:S(2)}) collective-permute-start(bf16[2,8,32,768]{3,2,1,0:T(8,128)(2,1)S(1)} %bitcast.55), channel_id=1, source_target_pairs={{0,32},{1,33},{2,34},{3,35},{4,36},{5,37},{6,38},{7,39},{8,40},{9,... | collective-permute-start | bytes 2359304 | tf_op jit(solution)/shard_map/ppermute | solution.py:238
  34.1 20.7 %collective-permute-start.6 = (bf16[2,8,32,768]{3,2,1,0:T(8,128)(2,1)S(1)}, bf16[2,8,32,768]{3,2,1,0:T(8,128)(2,1)S(1)}, u32[]{:S(2)}, u32[]{:S(2)}) collective-permute-start(bf16[2,8,32,768]{3,2,1,0:T(8,128)(2,1)S(1)} %bitcast.56), channel_id=1, source_target_pairs={{0,96},{1,97},{2,98},{3,99},{4,100},{5,101},{6,102},{7,103},{8,104... | collective-permute-start | bytes 2359304 | tf_op jit(solution)/shard_map/ppermute | solution.py:238
  36.2 26.7 %collective-permute-start.5 = (bf16[4,2,32,1024]{3,2,1,0:T(8,128)(2,1)S(1)}, bf16[4,2,32,1024]{3,2,1,0:T(8,128)(2,1)S(1)}, u32[]{:S(2)}, u32[]{:S(2)}) collective-permute-start(bf16[4,2,32,1024]{3,2,1,0:T(8,128)(2,1)S(1)} %pad_maximum_fusion.1.l0), channel_id=1, source_target_pairs={{0,12},{1,13},{2,14},{3,15},{4,8},{5,9},{6,10},{7,11},{8,4},{9,5},... | collective-permute-start | bytes 1572872 | tf_op jit(solution)/shard_map/ppermute | solution.py:238
  37.8 25.0 %collective-permute-start.4 = (bf16[4,2,32,1024]{3,2,1,0:T(8,128)(2,1)S(1)}, bf16[4,2,32,1024]{3,2,1,0:T(8,128)(2,1)S(1)}, u32[]{:S(2)}, u32[]{:S(2)}) collective-permute-start(bf16[4,2,32,1024]{3,2,1,0:T(8,128)(2,1)S(1)} %pad_maximum_fusion.1.l0), channel_id=1, source_target_pairs={{0,8},{1,9},{2,10},{3,11},{4,12},{5,13},{6,14},{7,15},{8,0},{9,1},... | collective-permute-start | bytes 1572872 | tf_op jit(solution)/shard_map/ppermute | solution.py:238
  37.8 25.6 %collective-permute-start.3 = (bf16[4,2,32,1024]{3,2,1,0:T(8,128)(2,1)S(1)}, bf16[4,2,32,1024]{3,2,1,0:T(8,128)(2,1)}, u32[]{:S(2)}, u32[]{:S(2)}) collective-permute-start(bf16[4,2,32,1024]{3,2,1,0:T(8,128)(2,1)S(1)} %pad_maximum_fusion.1.l0), channel_id=1, source_target_pairs={{0,4},{1,5},{2,6},{3,7},{4,0},{5,1},{6,2},{7,3},{8,12},{9,13},{10,... | collective-permute-start | bytes 1572872 | tf_op jit(solution)/shard_map/ppermute | solution.py:238
  53.9 15.3 %copy-start.1 = (bf16[2,8,32,768]{3,2,1,0:T(8,128)(2,1)}, bf16[2,8,32,768]{3,2,1,0:T(8,128)(2,1)S(1)}, u32[]{:S(2)}) copy-start(bf16[2,8,32,768]{3,2,1,0:T(8,128)(2,1)S(1)} %collective-permute-done.8) | copy-start | bytes 2359300
  54.7 11.4 %collective-permute-start.9 = (bf16[1,8,32,768]{3,2,1,0:T(8,128)(2,1)}, bf16[1,8,32,768]{3,2,1,0:T(8,128)(2,1)}, u32[]{:S(2)}, u32[]{:S(2)}) collective-permute-start(bf16[1,8,32,768]{3,2,1,0:T(8,128)(2,1)} %slice.9), channel_id=1, source_target_pairs={{0,32},{1,33},{2,34},{3,35},{4,36},{5,37},{6,38},{7,39},{8,40},{9,... | collective-permute-start | bytes 1179656 | tf_op jit(solution)/shard_map/ppermute | solution.py:238
  54.7 14.5 %copy-start.2 = (bf16[2,8,32,768]{3,2,1,0:T(8,128)(2,1)}, bf16[2,8,32,768]{3,2,1,0:T(8,128)(2,1)S(1)}, u32[]{:S(2)}) copy-start(bf16[2,8,32,768]{3,2,1,0:T(8,128)(2,1)S(1)} %collective-permute-done.6) | copy-start | bytes 2359300
  55.6 10.6 %collective-permute-start.7 = (bf16[1,8,32,768]{3,2,1,0:T(8,128)(2,1)}, bf16[1,8,32,768]{3,2,1,0:T(8,128)(2,1)}, u32[]{:S(2)}, u32[]{:S(2)}) collective-permute-start(bf16[1,8,32,768]{3,2,1,0:T(8,128)(2,1)} %slice.8), channel_id=1, source_target_pairs={{0,96},{1,97},{2,98},{3,99},{4,100},{5,101},{6,102},{7,103},{8,104... | collective-permute-start | bytes 1179656 | tf_op jit(solution)/shard_map/ppermute | solution.py:238
  62.8 12.7 %copy-start.4 = (bf16[4,2,32,1024]{3,2,1,0:T(8,128)(2,1)}, bf16[4,2,32,1024]{3,2,1,0:T(8,128)(2,1)S(1)}, u32[]{:S(2)}) copy-start(bf16[4,2,32,1024]{3,2,1,0:T(8,128)(2,1)S(1)} %collective-permute-done.5.l3) | copy-start | bytes 1572868
  62.9 0.9 copy-start.5
  69.2 59.9 %all-to-all-start.2 = ((bf16[8,2,384,384]{3,2,1,0:T(8,128)(2,1)}), bf16[8,2,384,384]{3,2,1,0:T(8,128)(2,1)}, u32[]{:S(2)}, u32[]{:S(2)}) async-start(bf16[8,2,384,384]{3,2,1,0:T(8,128)(2,1)} %shard_map.38), calls=%async_computation.2 | async-start | bytes 9437184 | tf_op jit(solution)/shard_map/all_to_all | solution.py:257
  82.7 20.3 %collective-permute-start.10 = (bf16[2,256,384]{2,1,0:T(8,128)(2,1)}, bf16[2,256,384]{2,1,0:T(8,128)(2,1)}, u32[]{:S(2)}, u32[]{:S(2)}) collective-permute-start(bf16[2,256,384]{2,1,0:T(8,128)(2,1)} %get-tuple-element.94), channel_id=1, source_target_pairs={{0,0},{1,1},{2,2},{3,3},{4,64},{5,65},{6,66},{7,67},{8,12},{9,13},... | collective-permute-start | bytes 1179656 | tf_op jit(solution)/shard_map/ppermute | solution.py:316
  88.2 16.9 %collective-permute-start.11 = (bf16[2,256,384]{2,1,0:T(8,128)(2,1)}, bf16[2,256,384]{2,1,0:T(8,128)(2,1)}, u32[]{:S(2)}, u32[]{:S(2)}) collective-permute-start(bf16[2,256,384]{2,1,0:T(8,128)(2,1)} %get-tuple-element.100), channel_id=1, source_target_pairs={{0,4},{1,5},{2,6},{3,7},{4,68},{5,69},{6,70},{7,71},{8,8},{9,9},{1... | collective-permute-start | bytes 1179656 | tf_op jit(solution)/shard_map/ppermute | solution.py:316
  91.0 16.0 %collective-permute-start.12 = (bf16[2,256,384]{2,1,0:T(8,128)(2,1)}, bf16[2,256,384]{2,1,0:T(8,128)(2,1)}, u32[]{:S(2)}, u32[]{:S(2)}) collective-permute-start(bf16[2,256,384]{2,1,0:T(8,128)(2,1)} %get-tuple-element.101), channel_id=1, source_target_pairs={{0,32},{1,33},{2,34},{3,35},{4,96},{5,97},{6,98},{7,99},{8,44},{9,... | collective-permute-start | bytes 1179656 | tf_op jit(solution)/shard_map/ppermute | solution.py:316
  94.0 20.2 %collective-permute-start.13 = (bf16[2,256,384]{2,1,0:T(8,128)(2,1)}, bf16[2,256,384]{2,1,0:T(8,128)(2,1)}, u32[]{:S(2)}, u32[]{:S(2)}) collective-permute-start(bf16[2,256,384]{2,1,0:T(8,128)(2,1)} %get-tuple-element.102), channel_id=1, source_target_pairs={{0,36},{1,37},{2,38},{3,39},{4,100},{5,101},{6,102},{7,103},{8,40}... | collective-permute-start | bytes 1179656 | tf_op jit(solution)/shard_map/ppermute | solution.py:316
  102.9 12.8 %collective-permute-start.15 = (bf16[2,256,384]{2,1,0:T(8,128)(2,1)}, bf16[2,256,384]{2,1,0:T(8,128)(2,1)}, u32[]{:S(2)}, u32[]{:S(2)}) collective-permute-start(bf16[2,256,384]{2,1,0:T(8,128)(2,1)} %get-tuple-element.109), channel_id=1, source_target_pairs={{0,16},{1,17},{2,18},{3,19},{4,80},{5,81},{6,82},{7,83},{8,28},{9,... | collective-permute-start | bytes 1179656 | tf_op jit(solution)/shard_map/ppermute | solution.py:316
  104.2 19.4 %collective-permute-start.16 = (bf16[2,256,384]{2,1,0:T(8,128)(2,1)}, bf16[2,256,384]{2,1,0:T(8,128)(2,1)}, u32[]{:S(2)}, u32[]{:S(2)}) collective-permute-start(bf16[2,256,384]{2,1,0:T(8,128)(2,1)} %get-tuple-element.110), channel_id=1, source_target_pairs={{0,20},{1,21},{2,22},{3,23},{4,84},{5,85},{6,86},{7,87},{8,24},{9,... | collective-permute-start | bytes 1179656 | tf_op jit(solution)/shard_map/ppermute | solution.py:316
  105.1 19.4 %collective-permute-start.17 = (bf16[2,256,384]{2,1,0:T(8,128)(2,1)}, bf16[2,256,384]{2,1,0:T(8,128)(2,1)}, u32[]{:S(2)}, u32[]{:S(2)}) collective-permute-start(bf16[2,256,384]{2,1,0:T(8,128)(2,1)} %get-tuple-element.111), channel_id=1, source_target_pairs={{0,48},{1,49},{2,50},{3,51},{4,112},{5,113},{6,114},{7,115},{8,60}... | collective-permute-start | bytes 1179656 | tf_op jit(solution)/shard_map/ppermute | solution.py:316
  107.0 22.1 %collective-permute-start.18 = (bf16[2,256,384]{2,1,0:T(8,128)(2,1)}, bf16[2,256,384]{2,1,0:T(8,128)(2,1)}, u32[]{:S(2)}, u32[]{:S(2)}) collective-permute-start(bf16[2,256,384]{2,1,0:T(8,128)(2,1)} %get-tuple-element.112), channel_id=1, source_target_pairs={{0,52},{1,53},{2,54},{3,55},{4,116},{5,117},{6,118},{7,119},{8,56}... | collective-permute-start | bytes 1179656 | tf_op jit(solution)/shard_map/ppermute | solution.py:316
  129.1 58.9 %all-to-all-start.3 = ((bf16[8,2,384,384]{3,2,1,0:T(8,128)(2,1)}), bf16[8,2,384,384]{3,2,1,0:T(8,128)(2,1)}, u32[]{:S(2)}, u32[]{:S(2)}) async-start(bf16[8,2,384,384]{3,2,1,0:T(8,128)(2,1)} %shard_map.43), calls=%async_computation.3 | async-start | bytes 9437184 | tf_op jit(solution)/shard_map/all_to_all | solution.py:257
  142.6 21.5 %collective-permute-start.14 = (bf16[2,384,384]{2,1,0:T(8,128)(2,1)}, bf16[2,384,384]{2,1,0:T(8,128)(2,1)S(1)}, u32[]{:S(2)}, u32[]{:S(2)}) collective-permute-start(bf16[2,384,384]{2,1,0:T(8,128)(2,1)} %get-tuple-element.108), channel_id=1, source_target_pairs={{0,0},{1,1},{2,2},{3,3},{4,64},{5,65},{6,66},{7,67},{8,12},{9,13},... | collective-permute-start | bytes 1769480 | tf_op jit(solution)/shard_map/ppermute | solution.py:316
  148.1 48.2 %collective-permute-start.19 = (bf16[2,384,384]{2,1,0:T(8,128)(2,1)}, bf16[2,384,384]{2,1,0:T(8,128)(2,1)S(1)}, u32[]{:S(2)}, u32[]{:S(2)}) collective-permute-start(bf16[2,384,384]{2,1,0:T(8,128)(2,1)} %get-tuple-element.118), channel_id=1, source_target_pairs={{0,4},{1,5},{2,6},{3,7},{4,68},{5,69},{6,70},{7,71},{8,8},{9,9},{1... | collective-permute-start | bytes 1769480 | tf_op jit(solution)/shard_map/ppermute | solution.py:316
  150.9 49.3 %collective-permute-start.20 = (bf16[2,384,384]{2,1,0:T(8,128)(2,1)}, bf16[2,384,384]{2,1,0:T(8,128)(2,1)S(1)}, u32[]{:S(2)}, u32[]{:S(2)}) collective-permute-start(bf16[2,384,384]{2,1,0:T(8,128)(2,1)} %get-tuple-element.119), channel_id=1, source_target_pairs={{0,32},{1,33},{2,34},{3,35},{4,96},{5,97},{6,98},{7,99},{8,44},{9,... | collective-permute-start | bytes 1769480 | tf_op jit(solution)/shard_map/ppermute | solution.py:316
  151.1 49.1 %collective-permute-start.21 = (bf16[2,384,384]{2,1,0:T(8,128)(2,1)}, bf16[2,384,384]{2,1,0:T(8,128)(2,1)S(1)}, u32[]{:S(2)}, u32[]{:S(2)}) collective-permute-start(bf16[2,384,384]{2,1,0:T(8,128)(2,1)} %get-tuple-element.120), channel_id=1, source_target_pairs={{0,36},{1,37},{2,38},{3,39},{4,100},{5,101},{6,102},{7,103},{8,40}... | collective-permute-start | bytes 1769480 | tf_op jit(solution)/shard_map/ppermute | solution.py:316
  164.1 87.8 %copy-start.6 = (bf16[2,384,384]{2,1,0:T(8,128)(2,1)}, bf16[2,384,384]{2,1,0:T(8,128)(2,1)S(1)}, u32[]{:S(2)}) copy-start(bf16[2,384,384]{2,1,0:T(8,128)(2,1)S(1)} %collective-permute-done.14.refs_0_) | copy-start | bytes 1769476
  164.1 39.5 %collective-permute-start.23 = (bf16[2,384,384]{2,1,0:T(8,128)(2,1)}, bf16[2,384,384]{2,1,0:T(8,128)(2,1)S(1)}, u32[]{:S(2)}, u32[]{:S(2)}) collective-permute-start(bf16[2,384,384]{2,1,0:T(8,128)(2,1)} %get-tuple-element.127), channel_id=1, source_target_pairs={{0,16},{1,17},{2,18},{3,19},{4,80},{5,81},{6,82},{7,83},{8,28},{9,... | collective-permute-start | bytes 1769480 | tf_op jit(solution)/shard_map/ppermute | solution.py:316
  166.4 41.3 %collective-permute-start.24 = (bf16[2,384,384]{2,1,0:T(8,128)(2,1)}, bf16[2,384,384]{2,1,0:T(8,128)(2,1)S(1)}, u32[]{:S(2)}, u32[]{:S(2)}) collective-permute-start(bf16[2,384,384]{2,1,0:T(8,128)(2,1)} %get-tuple-element.128), channel_id=1, source_target_pairs={{0,20},{1,21},{2,22},{3,23},{4,84},{5,85},{6,86},{7,87},{8,24},{9,... | collective-permute-start | bytes 1769480 | tf_op jit(solution)/shard_map/ppermute | solution.py:316
  196.3 58.5 %copy-start.7 = (bf16[2,384,384]{2,1,0:T(8,128)(2,1)}, bf16[2,384,384]{2,1,0:T(8,128)(2,1)S(1)}, u32[]{:S(2)}) copy-start(bf16[2,384,384]{2,1,0:T(8,128)(2,1)S(1)} %collective-permute-done.19.refs_1_) | copy-start | bytes 1769476
  196.3 25.5 %collective-permute-start.25 = (bf16[2,384,384]{2,1,0:T(8,128)(2,1)}, bf16[2,384,384]{2,1,0:T(8,128)(2,1)}, u32[]{:S(2)}, u32[]{:S(2)}) collective-permute-start(bf16[2,384,384]{2,1,0:T(8,128)(2,1)} %get-tuple-element.129), channel_id=1, source_target_pairs={{0,48},{1,49},{2,50},{3,51},{4,112},{5,113},{6,114},{7,115},{8,60}... | collective-permute-start | bytes 1769480 | tf_op jit(solution)/shard_map/ppermute | solution.py:316
  200.1 54.6 %copy-start.8 = (bf16[2,384,384]{2,1,0:T(8,128)(2,1)}, bf16[2,384,384]{2,1,0:T(8,128)(2,1)S(1)}, u32[]{:S(2)}) copy-start(bf16[2,384,384]{2,1,0:T(8,128)(2,1)S(1)} %collective-permute-done.20.refs_2_) | copy-start | bytes 1769476
  200.2 21.8 %collective-permute-start.26 = (bf16[2,384,384]{2,1,0:T(8,128)(2,1)}, bf16[2,384,384]{2,1,0:T(8,128)(2,1)}, u32[]{:S(2)}, u32[]{:S(2)}) collective-permute-start(bf16[2,384,384]{2,1,0:T(8,128)(2,1)} %get-tuple-element.130), channel_id=1, source_target_pairs={{0,52},{1,53},{2,54},{3,55},{4,116},{5,117},{6,118},{7,119},{8,56}... | collective-permute-start | bytes 1769480 | tf_op jit(solution)/shard_map/ppermute | solution.py:316
  200.2 54.6 %copy-start.9 = (bf16[2,384,384]{2,1,0:T(8,128)(2,1)}, bf16[2,384,384]{2,1,0:T(8,128)(2,1)S(1)}, u32[]{:S(2)}) copy-start(bf16[2,384,384]{2,1,0:T(8,128)(2,1)S(1)} %collective-permute-done.21.refs_3_) | copy-start | bytes 1769476
  200.2 26.4 %collective-permute-start.22 = (bf16[2,384,384]{2,1,0:T(8,128)(2,1)}, bf16[2,384,384]{2,1,0:T(8,128)(2,1)}, u32[]{:S(2)}, u32[]{:S(2)}) collective-permute-start(bf16[2,384,384]{2,1,0:T(8,128)(2,1)} %get-tuple-element.126), channel_id=1, source_target_pairs={{0,0},{1,1},{2,2},{3,3},{4,64},{5,65},{6,66},{7,67},{8,12},{9,13},... | collective-permute-start | bytes 1769480 | tf_op jit(solution)/shard_map/ppermute | solution.py:316
  203.6 51.2 %copy-start.10 = (bf16[2,384,384]{2,1,0:T(8,128)(2,1)}, bf16[2,384,384]{2,1,0:T(8,128)(2,1)S(1)}, u32[]{:S(2)}) copy-start(bf16[2,384,384]{2,1,0:T(8,128)(2,1)S(1)} %collective-permute-done.23.refs_0_) | copy-start | bytes 1769476
  203.6 39.2 %collective-permute-start.31 = (bf16[2,384,384]{2,1,0:T(8,128)(2,1)}, bf16[2,384,384]{2,1,0:T(8,128)(2,1)}, u32[]{:S(2)}, u32[]{:S(2)}) collective-permute-start(bf16[2,384,384]{2,1,0:T(8,128)(2,1)} %get-tuple-element.140), channel_id=1, source_target_pairs={{0,4},{1,5},{2,6},{3,7},{4,68},{5,69},{6,70},{7,71},{8,8},{9,9},{1... | collective-permute-start | bytes 1769480 | tf_op jit(solution)/shard_map/ppermute | solution.py:316
  207.7 47.1 %copy-start.11 = (bf16[2,384,384]{2,1,0:T(8,128)(2,1)}, bf16[2,384,384]{2,1,0:T(8,128)(2,1)S(1)}, u32[]{:S(2)}) copy-start(bf16[2,384,384]{2,1,0:T(8,128)(2,1)S(1)} %collective-permute-done.24.refs_1_) | copy-start | bytes 1769476
  207.7 37.3 %collective-permute-start.32 = (bf16[2,384,384]{2,1,0:T(8,128)(2,1)}, bf16[2,384,384]{2,1,0:T(8,128)(2,1)}, u32[]{:S(2)}, u32[]{:S(2)}) collective-permute-start(bf16[2,384,384]{2,1,0:T(8,128)(2,1)} %get-tuple-element.141), channel_id=1, source_target_pairs={{0,32},{1,33},{2,34},{3,35},{4,96},{5,97},{6,98},{7,99},{8,44},{9,... | collective-permute-start | bytes 1769480 | tf_op jit(solution)/shard_map/ppermute | solution.py:316
  221.8 39.5 %collective-permute-start.33 = (bf16[2,384,384]{2,1,0:T(8,128)(2,1)}, bf16[2,384,384]{2,1,0:T(8,128)(2,1)}, u32[]{:S(2)}, u32[]{:S(2)}) collective-permute-start(bf16[2,384,384]{2,1,0:T(8,128)(2,1)} %get-tuple-element.142), channel_id=1, source_target_pairs={{0,36},{1,37},{2,38},{3,39},{4,100},{5,101},{6,102},{7,103},{8,40}... | collective-permute-start | bytes 1769480 | tf_op jit(solution)/shard_map/ppermute | solution.py:316
  226.6 37.9 %collective-permute-start.27 = (bf16[2,384,384]{2,1,0:T(8,128)(2,1)}, bf16[2,384,384]{2,1,0:T(8,128)(2,1)}, u32[]{:S(2)}, u32[]{:S(2)}) collective-permute-start(bf16[2,384,384]{2,1,0:T(8,128)(2,1)} %get-tuple-element.135), channel_id=1, source_target_pairs={{0,16},{1,17},{2,18},{3,19},{4,80},{5,81},{6,82},{7,83},{8,28},{9,... | collective-permute-start | bytes 1769480 | tf_op jit(solution)/shard_map/ppermute | solution.py:316
  242.8 21.7 %collective-permute-start.28 = (bf16[2,384,384]{2,1,0:T(8,128)(2,1)}, bf16[2,384,384]{2,1,0:T(8,128)(2,1)}, u32[]{:S(2)}, u32[]{:S(2)}) collective-permute-start(bf16[2,384,384]{2,1,0:T(8,128)(2,1)} %get-tuple-element.136), channel_id=1, source_target_pairs={{0,20},{1,21},{2,22},{3,23},{4,84},{5,85},{6,86},{7,87},{8,24},{9,... | collective-permute-start | bytes 1769480 | tf_op jit(solution)/shard_map/ppermute | solution.py:316
  242.8 25.3 %collective-permute-start.29 = (bf16[2,384,384]{2,1,0:T(8,128)(2,1)}, bf16[2,384,384]{2,1,0:T(8,128)(2,1)}, u32[]{:S(2)}, u32[]{:S(2)}) collective-permute-start(bf16[2,384,384]{2,1,0:T(8,128)(2,1)} %get-tuple-element.137), channel_id=1, source_target_pairs={{0,48},{1,49},{2,50},{3,51},{4,112},{5,113},{6,114},{7,115},{8,60}... | collective-permute-start | bytes 1769480 | tf_op jit(solution)/shard_map/ppermute | solution.py:316
  245.1 34.1 %collective-permute-start.30 = (bf16[2,384,384]{2,1,0:T(8,128)(2,1)}, bf16[2,384,384]{2,1,0:T(8,128)(2,1)}, u32[]{:S(2)}, u32[]{:S(2)}) collective-permute-start(bf16[2,384,384]{2,1,0:T(8,128)(2,1)} %get-tuple-element.138), channel_id=1, source_target_pairs={{0,52},{1,53},{2,54},{3,55},{4,116},{5,117},{6,118},{7,119},{8,56}... | collective-permute-start | bytes 1769480 | tf_op jit(solution)/shard_map/ppermute | solution.py:316

commit v5 on v4

--- a/solution.py
+++ b/solution.py
@@ -12,7 +12,7 @@
 SIZES = (4, 2, 2, 2, 4)
 CHUNKS = ((0, 256), (256, 384), (640, 384))
 HALF = 4
-EARLY = 4
+EARLY = 2
 ORDER = (0, 4, 1, 5, 2, 6, 3, 7)
 AHEAD = 8
 VMEM = 60 << 20

time: 284 us -> 284 us (level)
  no operation moved by 1% of the time
where the time goes in v5:
time: 284 us; the launch traced here: 283 us
  starting transfers between devices  110 us (39%)
  waiting for transfers between devices  84.8 us (30%)
  Pallas kernels  78.9 us (28%)
  local copies, waits for them, and re-layouts  4.14 us (1%)
  other arithmetic  3.49 us (1%)
    ppermute x24, starting transfers between devices, body(): new.append(lax.ppermute(sent[k], AXES, pairs(ORDER[k])))  73.8 us
    pallas_call x6, Pallas kernels, add(): pl.pallas_call(functools.partial(add_kernel, start, rows, block, first),...  47.8 us
    ppermute x24, waiting for transfers between devices, body(): new.append(lax.ppermute(sent[k], AXES, pairs(ORDER[k])))  34.4 us
    ppermute x10, waiting for transfers between devices, across(): return lax.ppermute(value, AXES, moved(change))  25.9 us
    all_to_all x3, waiting for transfers between devices, first(): return lax.all_to_all(packed[i], ('c', 'y'), 0, 0, tiled=True)  24.6 us
    pallas_call x6, Pallas kernels, place(): pl.pallas_call(functools.partial(place_kernel, start, rows, height, first...  18.7 us
    all_to_all x3, starting transfers between devices, first(): return lax.all_to_all(packed[i], ('c', 'y'), 0, 0, tiled=True)  17.3 us
    ppermute x10, starting transfers between devices, across(): return lax.ppermute(value, AXES, moved(change))  13.3 us
  transfers between devices with their start and end apart: 38, of which 15 were waited for; matrix products, arithmetic and copies ran while one was open for 1% of the time, Pallas kernels for 27%

profile of v5, /device:TPU:15, one launch (start us, length us, event | category | flops | bytes accessed | tf_op | source)
XLA Modules:
  0.0 282.5 jit_solution(15609989214577320472)
XLA Ops:
  0.0 1.0 reduce-precision_convert_fusion
  2.4 0.9 pad_maximum_fusion
  3.3 6.1 %all-to-all-start = ((bf16[16,32,768]{2,1,0:T(8,128)(2,1)}), bf16[16,32,768]{2,1,0:T(8,128)(2,1)S(1)}, u32[]{:S(2)}, u32[]{:S(2)}) async-start(bf16[16,32,768]{2,1,0:T(8,128)(2,1)} %pad_maximum_fusion), calls=%async_computation | async-start | bytes 1572864 | tf_op jit(solution)/shard_map/all_to_all | solution.py:242
  9.5 0.9 fusion.3
  10.4 1.9 collective-permute-start.1
  12.3 1.2 collective-permute-start
  13.8 3.3 %shard_map.37 = bf16[8,2,256,384]{3,2,1,0:T(8,128)(2,1)} custom-call(bf16[1024,6144]{1,0:T(8,128)(2,1)} %base.5), custom_call_target="tpu_custom_call" | custom-call | bytes 6291456 | tf_op jit(solution)/shard_map/pallas_call | solution.py:92
  17.1 6.5 %collective-permute-done.1 = bf16[2,32,1024]{2,1,0:T(8,128)(2,1)S(1)} collective-permute-done((bf16[2,32,1024]{2,1,0:T(8,128)(2,1)S(1)}, bf16[2,32,1024]{2,1,0:T(8,128)(2,1)S(1)}, u32[]{:S(2)}, u32[]{:S(2)}) %collective-permute-start.1) | collective-permute-done | bytes 131104 | tf_op jit(solution)/shard_map/ppermute | solution.py:238
  23.5 2.2 collective-permute-done
  25.8 6.6 %all-to-all-start.1 = ((bf16[8,2,256,384]{3,2,1,0:T(8,128)(2,1)}), bf16[8,2,256,384]{3,2,1,0:T(8,128)(2,1)}, u32[]{:S(2)}, u32[]{:S(2)}) async-start(bf16[8,2,256,384]{3,2,1,0:T(8,128)(2,1)} %shard_map.37), calls=%async_computation.1 | async-start | bytes 6291456 | tf_op jit(solution)/shard_map/all_to_all | solution.py:257
  32.4 1.6 collective-permute-start.8
  34.1 2.1 collective-permute-start.6
  36.2 1.6 collective-permute-start.5
  37.8 1.8 collective-permute-start.3
  39.7 14.2 %collective-permute-done.8 = bf16[2,8,32,768]{3,2,1,0:T(8,128)(2,1)S(1)} collective-permute-done((bf16[2,8,32,768]{3,2,1,0:T(8,128)(2,1)S(1)}, bf16[2,8,32,768]{3,2,1,0:T(8,128)(2,1)S(1)}, u32[]{:S(2)}, u32[]{:S(2)}) %collective-permute-start.8) | collective-permute-done | bytes 786464 | tf_op jit(solution)/shard_map/ppermute | solution.py:238
  53.9 0.8 slice.9
  54.7 0.8 slice.8
  55.6 2.7 collective-permute-start.7
  58.2 4.6 %shard_map.38 = bf16[8,2,384,384]{3,2,1,0:T(8,128)(2,1)} custom-call(bf16[1024,6144]{1,0:T(8,128)(2,1)} %base.5), custom_call_target="tpu_custom_call" | custom-call | bytes 9437184 | tf_op jit(solution)/shard_map/pallas_call | solution.py:92
  63.7 2.4 collective-permute-done.9
  66.1 3.0 %all-to-all-done.1.part = bf16[8,2,256,384]{3,2,1,0:T(8,128)(2,1)} async-done(((bf16[8,2,256,384]{3,2,1,0:T(8,128)(2,1)}), bf16[8,2,256,384]{3,2,1,0:T(8,128)(2,1)}, u32[]{:S(2)}, u32[]{:S(2)}) %all-to-all-start.1) | async-done | bytes 3145760 | tf_op jit(solution)/shard_map/all_to_all | solution.py:257
  69.2 5.7 %all-to-all-start.2 = ((bf16[8,2,384,384]{3,2,1,0:T(8,128)(2,1)}), bf16[8,2,384,384]{3,2,1,0:T(8,128)(2,1)}, u32[]{:S(2)}, u32[]{:S(2)}) async-start(bf16[8,2,384,384]{3,2,1,0:T(8,128)(2,1)} %shard_map.38), calls=%async_computation.2 | async-start | bytes 9437184 | tf_op jit(solution)/shard_map/all_to_all | solution.py:257
  74.8 0.7 stack.174.picks
  75.5 7.1 %shard_map.39 = (bf16[2,256,384]{2,1,0:T(8,128)(2,1)}, bf16[2,256,384]{2,1,0:T(8,128)(2,1)}, bf16[2,256,384]{2,1,0:T(8,128)(2,1)}, bf16[2,256,384]{2,1,0:T(8,128)(2,1)}) custom-call(s32[33]{0:T(128)} %stack.174.picks, bf16[8,2,256,384]{3,2,1,0:T(8,128)(2,1)} %all-to-all-done.1.part, bf16[4,2,32,1024]{3,2,1,0:T(8,128)(2,1)} %copy-done.3, ...), custom_call_target="tpu_custom_call" | custom-call | flops 1207959552 | bytes 8388608 | tf_op jit(solution)/shard_map/pallas_call | solution.py:169
  82.7 5.5 %collective-permute-start.10 = (bf16[2,256,384]{2,1,0:T(8,128)(2,1)}, bf16[2,256,384]{2,1,0:T(8,128)(2,1)}, u32[]{:S(2)}, u32[]{:S(2)}) collective-permute-start(bf16[2,256,384]{2,1,0:T(8,128)(2,1)} %get-tuple-element.94), channel_id=1, source_target_pairs={{0,0},{1,1},{2,2},{3,3},{4,64},{5,65},{6,66},{7,67},{8,12},{9,13},... | collective-permute-start | bytes 1179656 | tf_op jit(solution)/shard_map/ppermute | solution.py:316
  88.2 2.8 collective-permute-start.11
  91.0 3.0 %collective-permute-start.13 = (bf16[2,256,384]{2,1,0:T(8,128)(2,1)}, bf16[2,256,384]{2,1,0:T(8,128)(2,1)}, u32[]{:S(2)}, u32[]{:S(2)}) collective-permute-start(bf16[2,256,384]{2,1,0:T(8,128)(2,1)} %get-tuple-element.107), channel_id=1, source_target_pairs={{0,32},{1,33},{2,34},{3,35},{4,96},{5,97},{6,98},{7,99},{8,44},{9,... | collective-permute-start | bytes 1179656 | tf_op jit(solution)/shard_map/ppermute | solution.py:316
  94.0 1.8 collective-permute-start.14
  95.8 7.1 %shard_map.40 = (bf16[2,256,384]{2,1,0:T(8,128)(2,1)}, bf16[2,256,384]{2,1,0:T(8,128)(2,1)}, bf16[2,256,384]{2,1,0:T(8,128)(2,1)}, bf16[2,256,384]{2,1,0:T(8,128)(2,1)}) custom-call(s32[33]{0:T(128)} %stack.174.picks, bf16[8,2,256,384]{3,2,1,0:T(8,128)(2,1)} %all-to-all-done.1.part, bf16[4,2,32,1024]{3,2,1,0:T(8,128)(2,1)} %copy-done.3, ...), custom_call_target="tpu_custom_call" | custom-call | flops 1207959552 | bytes 8388608 | tf_op jit(solution)/shard_map/pallas_call | solution.py:169
  102.9 1.3 collective-permute-start.15
  104.2 0.9 collective-permute-start.16
  105.1 1.7 collective-permute-start.17
  107.0 2.6 collective-permute-start.18
  109.6 4.6 %shard_map.43 = bf16[8,2,384,384]{3,2,1,0:T(8,128)(2,1)} custom-call(bf16[1024,6144]{1,0:T(8,128)(2,1)} %base.5), custom_call_target="tpu_custom_call" | custom-call | bytes 9437184 | tf_op jit(solution)/shard_map/pallas_call | solution.py:92
  114.1 1.6 collective-permute-done.15.refs_0_
  115.7 8.0 %collective-permute-done.16.refs_1_ = bf16[2,256,384]{2,1,0:T(8,128)(2,1)} collective-permute-done((bf16[2,256,384]{2,1,0:T(8,128)(2,1)}, bf16[2,256,384]{2,1,0:T(8,128)(2,1)}, u32[]{:S(2)}, u32[]{:S(2)}) %collective-permute-start.16) | collective-permute-done | bytes 393248 | tf_op jit(solution)/shard_map/ppermute | solution.py:316
  123.7 0.8 collective-permute-done.17.refs_2_
  124.5 4.5 %collective-permute-done.18.refs_3_ = bf16[2,256,384]{2,1,0:T(8,128)(2,1)} collective-permute-done((bf16[2,256,384]{2,1,0:T(8,128)(2,1)}, bf16[2,256,384]{2,1,0:T(8,128)(2,1)}, u32[]{:S(2)}, u32[]{:S(2)}) %collective-permute-start.18) | collective-permute-done | bytes 393248 | tf_op jit(solution)/shard_map/ppermute | solution.py:316
  129.1 5.0 %all-to-all-start.3 = ((bf16[8,2,384,384]{3,2,1,0:T(8,128)(2,1)}), bf16[8,2,384,384]{3,2,1,0:T(8,128)(2,1)}, u32[]{:S(2)}, u32[]{:S(2)}) async-start(bf16[8,2,384,384]{3,2,1,0:T(8,128)(2,1)} %shard_map.43), calls=%async_computation.3 | async-start | bytes 9437184 | tf_op jit(solution)/shard_map/all_to_all | solution.py:257
  134.1 8.5 %shard_map.41 = (bf16[2,384,384]{2,1,0:T(8,128)(2,1)}, bf16[2,384,384]{2,1,0:T(8,128)(2,1)}, bf16[2,384,384]{2,1,0:T(8,128)(2,1)}, bf16[2,384,384]{2,1,0:T(8,128)(2,1)}) custom-call(s32[33]{0:T(128)} %stack.174.picks, bf16[8,2,384,384]{3,2,1,0:T(8,128)(2,1)} %all-to-all-done.2.part, bf16[4,2,32,1024]{3,2,1,0:T(8,128)(2,1)} %copy-done.3, ...), custom_call_target="tpu_custom_call" | custom-call | flops 1811939328 | bytes 8388608 | tf_op jit(solution)/shard_map/pallas_call | solution.py:169
  142.6 5.5 %collective-permute-start.12 = (bf16[2,384,384]{2,1,0:T(8,128)(2,1)}, bf16[2,384,384]{2,1,0:T(8,128)(2,1)S(1)}, u32[]{:S(2)}, u32[]{:S(2)}) collective-permute-start(bf16[2,384,384]{2,1,0:T(8,128)(2,1)} %get-tuple-element.106), channel_id=1, source_target_pairs={{0,0},{1,1},{2,2},{3,3},{4,64},{5,65},{6,66},{7,67},{8,12},{9,13},... | collective-permute-start | bytes 1769480 | tf_op jit(solution)/shard_map/ppermute | solution.py:316
  148.1 2.8 collective-permute-start.19
  151.1 4.6 %collective-permute-start.22 = (bf16[2,384,384]{2,1,0:T(8,128)(2,1)}, bf16[2,384,384]{2,1,0:T(8,128)(2,1)S(1)}, u32[]{:S(2)}, u32[]{:S(2)}) collective-permute-start(bf16[2,384,384]{2,1,0:T(8,128)(2,1)} %get-tuple-element.126), channel_id=1, source_target_pairs={{0,36},{1,37},{2,38},{3,39},{4,100},{5,101},{6,102},{7,103},{8,40}... | collective-permute-start | bytes 1769480 | tf_op jit(solution)/shard_map/ppermute | solution.py:316
  155.7 8.3 %shard_map.42 = (bf16[2,384,384]{2,1,0:T(8,128)(2,1)}, bf16[2,384,384]{2,1,0:T(8,128)(2,1)}, bf16[2,384,384]{2,1,0:T(8,128)(2,1)}, bf16[2,384,384]{2,1,0:T(8,128)(2,1)}) custom-call(s32[33]{0:T(128)} %stack.174.picks, bf16[8,2,384,384]{3,2,1,0:T(8,128)(2,1)} %all-to-all-done.2.part, bf16[4,2,32,1024]{3,2,1,0:T(8,128)(2,1)} %copy-done.3, ...), custom_call_target="tpu_custom_call" | custom-call | flops 1811939328 | bytes 8388608 | tf_op jit(solution)/shard_map/pallas_call | solution.py:169
  164.1 2.3 collective-permute-start.23
  166.4 21.5 %all-to-all-done.3.part = bf16[8,2,384,384]{3,2,1,0:T(8,128)(2,1)} async-done(((bf16[8,2,384,384]{3,2,1,0:T(8,128)(2,1)}), bf16[8,2,384,384]{3,2,1,0:T(8,128)(2,1)}, u32[]{:S(2)}, u32[]{:S(2)}) %all-to-all-start.3) | async-done | bytes 4718624 | tf_op jit(solution)/shard_map/all_to_all | solution.py:257
  187.9 8.4 %shard_map.44 = (bf16[2,384,384]{2,1,0:T(8,128)(2,1)}, bf16[2,384,384]{2,1,0:T(8,128)(2,1)}, bf16[2,384,384]{2,1,0:T(8,128)(2,1)}, bf16[2,384,384]{2,1,0:T(8,128)(2,1)}) custom-call(s32[33]{0:T(128)} %stack.174.picks, bf16[8,2,384,384]{3,2,1,0:T(8,128)(2,1)} %all-to-all-done.3.part, bf16[4,2,32,1024]{3,2,1,0:T(8,128)(2,1)} %copy-done.3, ...), custom_call_target="tpu_custom_call" | custom-call | flops 1811939328 | bytes 8388608 | tf_op jit(solution)/shard_map/pallas_call | solution.py:169
  196.3 3.8 %collective-permute-start.25 = (bf16[2,384,384]{2,1,0:T(8,128)(2,1)}, bf16[2,384,384]{2,1,0:T(8,128)(2,1)}, u32[]{:S(2)}, u32[]{:S(2)}) collective-permute-start(bf16[2,384,384]{2,1,0:T(8,128)(2,1)} %get-tuple-element.129), channel_id=1, source_target_pairs={{0,48},{1,49},{2,50},{3,51},{4,112},{5,113},{6,114},{7,115},{8,60}... | collective-permute-start | bytes 1769480 | tf_op jit(solution)/shard_map/ppermute | solution.py:316
  200.2 3.4 %collective-permute-start.20 = (bf16[2,384,384]{2,1,0:T(8,128)(2,1)}, bf16[2,384,384]{2,1,0:T(8,128)(2,1)}, u32[]{:S(2)}, u32[]{:S(2)}) collective-permute-start(bf16[2,384,384]{2,1,0:T(8,128)(2,1)} %get-tuple-element.124), channel_id=1, source_target_pairs={{0,0},{1,1},{2,2},{3,3},{4,64},{5,65},{6,66},{7,67},{8,12},{9,13},... | collective-permute-start | bytes 1769480 | tf_op jit(solution)/shard_map/ppermute | solution.py:316
  203.6 4.1 %collective-permute-start.31 = (bf16[2,384,384]{2,1,0:T(8,128)(2,1)}, bf16[2,384,384]{2,1,0:T(8,128)(2,1)}, u32[]{:S(2)}, u32[]{:S(2)}) collective-permute-start(bf16[2,384,384]{2,1,0:T(8,128)(2,1)} %get-tuple-element.140), channel_id=1, source_target_pairs={{0,4},{1,5},{2,6},{3,7},{4,68},{5,69},{6,70},{7,71},{8,8},{9,9},{1... | collective-permute-start | bytes 1769480 | tf_op jit(solution)/shard_map/ppermute | solution.py:316
  207.7 5.7 %collective-permute-start.32 = (bf16[2,384,384]{2,1,0:T(8,128)(2,1)}, bf16[2,384,384]{2,1,0:T(8,128)(2,1)}, u32[]{:S(2)}, u32[]{:S(2)}) collective-permute-start(bf16[2,384,384]{2,1,0:T(8,128)(2,1)} %get-tuple-element.141), channel_id=1, source_target_pairs={{0,32},{1,33},{2,34},{3,35},{4,96},{5,97},{6,98},{7,99},{8,44},{9,... | collective-permute-start | bytes 1769480 | tf_op jit(solution)/shard_map/ppermute | solution.py:316
  213.4 8.4 %shard_map.45 = (bf16[2,384,384]{2,1,0:T(8,128)(2,1)}, bf16[2,384,384]{2,1,0:T(8,128)(2,1)}, bf16[2,384,384]{2,1,0:T(8,128)(2,1)}, bf16[2,384,384]{2,1,0:T(8,128)(2,1)}) custom-call(s32[33]{0:T(128)} %stack.174.picks, bf16[8,2,384,384]{3,2,1,0:T(8,128)(2,1)} %all-to-all-done.3.part, bf16[4,2,32,1024]{3,2,1,0:T(8,128)(2,1)} %copy-done.3, ...), custom_call_target="tpu_custom_call" | custom-call | flops 1811939328 | bytes 8388608 | tf_op jit(solution)/shard_map/pallas_call | solution.py:169
  221.9 4.7 %collective-permute-done.20.refs_0_ = bf16[2,384,384]{2,1,0:T(8,128)(2,1)} collective-permute-done((bf16[2,384,384]{2,1,0:T(8,128)(2,1)}, bf16[2,384,384]{2,1,0:T(8,128)(2,1)}, u32[]{:S(2)}, u32[]{:S(2)}) %collective-permute-start.20) | collective-permute-done | bytes 589856 | tf_op jit(solution)/shard_map/ppermute | solution.py:316
  226.6 16.2 %collective-permute-start.27 = (bf16[2,384,384]{2,1,0:T(8,128)(2,1)}, bf16[2,384,384]{2,1,0:T(8,128)(2,1)}, u32[]{:S(2)}, u32[]{:S(2)}) collective-permute-start(bf16[2,384,384]{2,1,0:T(8,128)(2,1)} %get-tuple-element.135), channel_id=1, source_target_pairs={{0,16},{1,17},{2,18},{3,19},{4,80},{5,81},{6,82},{7,83},{8,28},{9,... | collective-permute-start | bytes 1769480 | tf_op jit(solution)/shard_map/ppermute | solution.py:316
  242.8 2.2 collective-permute-start.29
  245.1 3.2 %collective-permute-start.30 = (bf16[2,384,384]{2,1,0:T(8,128)(2,1)}, bf16[2,384,384]{2,1,0:T(8,128)(2,1)}, u32[]{:S(2)}, u32[]{:S(2)}) collective-permute-start(bf16[2,384,384]{2,1,0:T(8,128)(2,1)} %get-tuple-element.138), channel_id=1, source_target_pairs={{0,52},{1,53},{2,54},{3,55},{4,116},{5,117},{6,118},{7,119},{8,56}... | collective-permute-start | bytes 1769480 | tf_op jit(solution)/shard_map/ppermute | solution.py:316
  249.0 2.9 %shard_map.46.refs_4_ = bf16[16384,384]{1,0:T(8,128)(2,1)} custom-call(s32[8]{0:T(128)} %stack.150.slots, bf16[2,256,384]{2,1,0:T(8,128)(2,1)} %collective-permute-done.10.refs_0_, bf16[2,256,384]{2,1,0:T(8,128)(2,1)} %collective-permute-done.11.refs_1_, bf16[2,256,384]{2,1,0:T(8,128)(2,1)} %collective-permute-done.13.refs_2_, ...), custom_call_target="tpu_custom_call" | custom-call | bytes 3145728 | tf_op jit(solution)/shard_map/pallas_call | solution.py:213
  251.9 2.9 %shard_map.47.refs_4_ = bf16[16384,384]{1,0:T(8,128)(2,1)} custom-call(s32[8]{0:T(128)} %stack.150.slots, bf16[2,256,384]{2,1,0:T(8,128)(2,1)} %collective-permute-done.15.refs_0_, bf16[2,256,384]{2,1,0:T(8,128)(2,1)} %collective-permute-done.16.refs_1_, bf16[2,256,384]{2,1,0:T(8,128)(2,1)} %collective-permute-done.17.refs_2_, ...), custom_call_target="tpu_custom_call", output_to_operand_aliasing={{}: (5, {})} | custom-call | bytes 3145728 | tf_op jit(solution)/shard_map/pallas_call | solution.py:213
  254.8 3.2 %shard_map.48.refs_4_ = bf16[16384,384]{1,0:T(8,128)(2,1)} custom-call(s32[8]{0:T(128)} %stack.150.slots, bf16[2,384,384]{2,1,0:T(8,128)(2,1)} %copy-done.6, bf16[2,384,384]{2,1,0:T(8,128)(2,1)} %copy-done.7, bf16[2,384,384]{2,1,0:T(8,128)(2,1)} %copy-done.8, bf16[2,384,384]{2,1,0:T(8,128)(2,1)} %copy-done.9, ...), custom_call_target="tpu_custom_call", output_to_operand_aliasing={{}: (5, {})} | custom-call | bytes 4718592 | tf_op jit(solution)/shard_map/pallas_call | solution.py:213
  258.1 3.2 %shard_map.49.refs_4_ = bf16[16384,384]{1,0:T(8,128)(2,1)} custom-call(s32[8]{0:T(128)} %stack.150.slots, bf16[2,384,384]{2,1,0:T(8,128)(2,1)} %copy-done.10, bf16[2,384,384]{2,1,0:T(8,128)(2,1)} %copy-done.11, bf16[2,384,384]{2,1,0:T(8,128)(2,1)} %collective-permute-done.25.refs_2_, ...), custom_call_target="tpu_custom_call", output_to_operand_aliasing={{}: (5, {})} | custom-call | bytes 4718592 | tf_op jit(solution)/shard_map/pallas_call | solution.py:213
  261.3 3.2 %shard_map.50.refs_4_ = bf16[16384,384]{1,0:T(8,128)(2,1)} custom-call(s32[8]{0:T(128)} %stack.150.slots, bf16[2,384,384]{2,1,0:T(8,128)(2,1)} %collective-permute-done.20.refs_0_, bf16[2,384,384]{2,1,0:T(8,128)(2,1)} %collective-permute-done.31.refs_1_, bf16[2,384,384]{2,1,0:T(8,128)(2,1)} %collective-permute-done.32.refs_2_, ...), custom_call_target="tpu_custom_call", output_to_operand_aliasing={{}: (5, {})} | custom-call | bytes 4718592 | tf_op jit(solution)/shard_map/pallas_call | solution.py:213
  264.6 3.6 %collective-permute-done.29.refs_2_ = bf16[2,384,384]{2,1,0:T(8,128)(2,1)} collective-permute-done((bf16[2,384,384]{2,1,0:T(8,128)(2,1)}, bf16[2,384,384]{2,1,0:T(8,128)(2,1)}, u32[]{:S(2)}, u32[]{:S(2)}) %collective-permute-start.29) | collective-permute-done | bytes 589856 | tf_op jit(solution)/shard_map/ppermute | solution.py:316
  268.2 10.9 %collective-permute-done.30.refs_3_ = bf16[2,384,384]{2,1,0:T(8,128)(2,1)} collective-permute-done((bf16[2,384,384]{2,1,0:T(8,128)(2,1)}, bf16[2,384,384]{2,1,0:T(8,128)(2,1)}, u32[]{:S(2)}, u32[]{:S(2)}) %collective-permute-start.30) | collective-permute-done | bytes 589856 | tf_op jit(solution)/shard_map/ppermute | solution.py:316
  279.1 3.2 %shard_map.51 = bf16[16384,384]{1,0:T(8,128)(2,1)} custom-call(s32[8]{0:T(128)} %stack.150.slots, bf16[2,384,384]{2,1,0:T(8,128)(2,1)} %collective-permute-done.27.refs_0_, bf16[2,384,384]{2,1,0:T(8,128)(2,1)} %collective-permute-done.28.refs_1_, bf16[2,384,384]{2,1,0:T(8,128)(2,1)} %collective-permute-done.29.refs_2_, ...), custom_call_target="tpu_custom_call", output_to_operand_aliasing={{}: (5, {})} | custom-call | bytes 4718592 | tf_op jit(solution)/shard_map/pallas_call | solution.py:213
  (66 shorter events, 3.8 us)
Async XLA Ops:
  3.3 22.4 %all-to-all-start = ((bf16[16,32,768]{2,1,0:T(8,128)(2,1)}), bf16[16,32,768]{2,1,0:T(8,128)(2,1)S(1)}, u32[]{:S(2)}, u32[]{:S(2)}) async-start(bf16[16,32,768]{2,1,0:T(8,128)(2,1)} %pad_maximum_fusion), calls=%async_computation | async-start | bytes 1572864 | tf_op jit(solution)/shard_map/all_to_all | solution.py:242
  10.4 13.1 %collective-permute-start.1 = (bf16[2,32,1024]{2,1,0:T(8,128)(2,1)S(1)}, bf16[2,32,1024]{2,1,0:T(8,128)(2,1)S(1)}, u32[]{:S(2)}, u32[]{:S(2)}) collective-permute-start(bf16[2,32,1024]{2,1,0:T(8,128)(2,1)S(1)} %get-tuple-element.162), channel_id=1, source_target_pairs={{0,2},{1,3},{2,0},{3,1},{4,6},{5,7},{6,4},{7,5},{8,10},{9,11},{10,... | collective-permute-start | bytes 393224 | tf_op jit(solution)/shard_map/ppermute | solution.py:238
  12.3 13.4 %collective-permute-start = (bf16[2,32,1024]{2,1,0:T(8,128)(2,1)S(1)}, bf16[2,32,1024]{2,1,0:T(8,128)(2,1)S(1)}, u32[]{:S(2)}, u32[]{:S(2)}) collective-permute-start(bf16[2,32,1024]{2,1,0:T(8,128)(2,1)S(1)} %get-tuple-element.162), channel_id=1, source_target_pairs={{0,3},{1,0},{2,1},{3,2},{4,7},{5,4},{6,5},{7,6},{8,11},{9,8},{10,9... | collective-permute-start | bytes 393224 | tf_op jit(solution)/shard_map/ppermute | solution.py:238
  13.5 12.2 %collective-permute-start.2 = (bf16[2,32,1024]{2,1,0:T(8,128)(2,1)S(1)}, bf16[2,32,1024]{2,1,0:T(8,128)(2,1)S(1)}, u32[]{:S(2)}, u32[]{:S(2)}) collective-permute-start(bf16[2,32,1024]{2,1,0:T(8,128)(2,1)S(1)} %get-tuple-element.162), channel_id=1, source_target_pairs={{0,1},{1,2},{2,3},{3,0},{4,5},{5,6},{6,7},{7,4},{8,9},{9,10},{10,1... | collective-permute-start | bytes 393224 | tf_op jit(solution)/shard_map/ppermute | solution.py:238
  25.8 37.1 %copy-start.3 = (bf16[4,2,32,1024]{3,2,1,0:T(8,128)(2,1)}, bf16[4,2,32,1024]{3,2,1,0:T(8,128)(2,1)S(1)}, u32[]{:S(2)}) copy-start(bf16[4,2,32,1024]{3,2,1,0:T(8,128)(2,1)S(1)} %pad_maximum_fusion.1.l0) | copy-start | bytes 1572868
  25.8 37.0 %copy-start = (bf16[16,32,768]{2,1,0:T(8,128)(2,1)}, bf16[16,32,768]{2,1,0:T(8,128)(2,1)S(1)}, u32[]{:S(2)}) copy-start(bf16[16,32,768]{2,1,0:T(8,128)(2,1)S(1)} %all-to-all-done) | copy-start | bytes 2359300
  25.8 43.4 %all-to-all-start.1 = ((bf16[8,2,256,384]{3,2,1,0:T(8,128)(2,1)}), bf16[8,2,256,384]{3,2,1,0:T(8,128)(2,1)}, u32[]{:S(2)}, u32[]{:S(2)}) async-start(bf16[8,2,256,384]{3,2,1,0:T(8,128)(2,1)} %shard_map.37), calls=%async_computation.1 | async-start | bytes 6291456 | tf_op jit(solution)/shard_map/all_to_all | solution.py:257
  32.4 21.5 %collective-permute-start.8 = (bf16[2,8,32,768]{3,2,1,0:T(8,128)(2,1)S(1)}, bf16[2,8,32,768]{3,2,1,0:T(8,128)(2,1)S(1)}, u32[]{:S(2)}, u32[]{:S(2)}) collective-permute-start(bf16[2,8,32,768]{3,2,1,0:T(8,128)(2,1)S(1)} %bitcast.55), channel_id=1, source_target_pairs={{0,32},{1,33},{2,34},{3,35},{4,36},{5,37},{6,38},{7,39},{8,40},{9,... | collective-permute-start | bytes 2359304 | tf_op jit(solution)/shard_map/ppermute | solution.py:238
  34.1 20.7 %collective-permute-start.6 = (bf16[2,8,32,768]{3,2,1,0:T(8,128)(2,1)S(1)}, bf16[2,8,32,768]{3,2,1,0:T(8,128)(2,1)S(1)}, u32[]{:S(2)}, u32[]{:S(2)}) collective-permute-start(bf16[2,8,32,768]{3,2,1,0:T(8,128)(2,1)S(1)} %bitcast.56), channel_id=1, source_target_pairs={{0,96},{1,97},{2,98},{3,99},{4,100},{5,101},{6,102},{7,103},{8,104... | collective-permute-start | bytes 2359304 | tf_op jit(solution)/shard_map/ppermute | solution.py:238
  36.2 26.7 %collective-permute-start.5 = (bf16[4,2,32,1024]{3,2,1,0:T(8,128)(2,1)S(1)}, bf16[4,2,32,1024]{3,2,1,0:T(8,128)(2,1)S(1)}, u32[]{:S(2)}, u32[]{:S(2)}) collective-permute-start(bf16[4,2,32,1024]{3,2,1,0:T(8,128)(2,1)S(1)} %pad_maximum_fusion.1.l0), channel_id=1, source_target_pairs={{0,12},{1,13},{2,14},{3,15},{4,8},{5,9},{6,10},{7,11},{8,4},{9,5},... | collective-permute-start | bytes 1572872 | tf_op jit(solution)/shard_map/ppermute | solution.py:238
  37.8 25.0 %collective-permute-start.4 = (bf16[4,2,32,1024]{3,2,1,0:T(8,128)(2,1)S(1)}, bf16[4,2,32,1024]{3,2,1,0:T(8,128)(2,1)S(1)}, u32[]{:S(2)}, u32[]{:S(2)}) collective-permute-start(bf16[4,2,32,1024]{3,2,1,0:T(8,128)(2,1)S(1)} %pad_maximum_fusion.1.l0), channel_id=1, source_target_pairs={{0,8},{1,9},{2,10},{3,11},{4,12},{5,13},{6,14},{7,15},{8,0},{9,1},... | collective-permute-start | bytes 1572872 | tf_op jit(solution)/shard_map/ppermute | solution.py:238
  37.8 25.6 %collective-permute-start.3 = (bf16[4,2,32,1024]{3,2,1,0:T(8,128)(2,1)S(1)}, bf16[4,2,32,1024]{3,2,1,0:T(8,128)(2,1)}, u32[]{:S(2)}, u32[]{:S(2)}) collective-permute-start(bf16[4,2,32,1024]{3,2,1,0:T(8,128)(2,1)S(1)} %pad_maximum_fusion.1.l0), channel_id=1, source_target_pairs={{0,4},{1,5},{2,6},{3,7},{4,0},{5,1},{6,2},{7,3},{8,12},{9,13},{10,... | collective-permute-start | bytes 1572872 | tf_op jit(solution)/shard_map/ppermute | solution.py:238
  53.9 15.3 %copy-start.1 = (bf16[2,8,32,768]{3,2,1,0:T(8,128)(2,1)}, bf16[2,8,32,768]{3,2,1,0:T(8,128)(2,1)S(1)}, u32[]{:S(2)}) copy-start(bf16[2,8,32,768]{3,2,1,0:T(8,128)(2,1)S(1)} %collective-permute-done.8) | copy-start | bytes 2359300
  54.7 11.4 %collective-permute-start.9 = (bf16[1,8,32,768]{3,2,1,0:T(8,128)(2,1)}, bf16[1,8,32,768]{3,2,1,0:T(8,128)(2,1)}, u32[]{:S(2)}, u32[]{:S(2)}) collective-permute-start(bf16[1,8,32,768]{3,2,1,0:T(8,128)(2,1)} %slice.9), channel_id=1, source_target_pairs={{0,32},{1,33},{2,34},{3,35},{4,36},{5,37},{6,38},{7,39},{8,40},{9,... | collective-permute-start | bytes 1179656 | tf_op jit(solution)/shard_map/ppermute | solution.py:238
  54.7 14.5 %copy-start.2 = (bf16[2,8,32,768]{3,2,1,0:T(8,128)(2,1)}, bf16[2,8,32,768]{3,2,1,0:T(8,128)(2,1)S(1)}, u32[]{:S(2)}) copy-start(bf16[2,8,32,768]{3,2,1,0:T(8,128)(2,1)S(1)} %collective-permute-done.6) | copy-start | bytes 2359300
  55.6 10.6 %collective-permute-start.7 = (bf16[1,8,32,768]{3,2,1,0:T(8,128)(2,1)}, bf16[1,8,32,768]{3,2,1,0:T(8,128)(2,1)}, u32[]{:S(2)}, u32[]{:S(2)}) collective-permute-start(bf16[1,8,32,768]{3,2,1,0:T(8,128)(2,1)} %slice.8), channel_id=1, source_target_pairs={{0,96},{1,97},{2,98},{3,99},{4,100},{5,101},{6,102},{7,103},{8,104... | collective-permute-start | bytes 1179656 | tf_op jit(solution)/shard_map/ppermute | solution.py:238
  62.8 12.7 %copy-start.4 = (bf16[4,2,32,1024]{3,2,1,0:T(8,128)(2,1)}, bf16[4,2,32,1024]{3,2,1,0:T(8,128)(2,1)S(1)}, u32[]{:S(2)}) copy-start(bf16[4,2,32,1024]{3,2,1,0:T(8,128)(2,1)S(1)} %collective-permute-done.5.l3) | copy-start | bytes 1572868
  62.9 0.9 copy-start.5
  69.2 59.9 %all-to-all-start.2 = ((bf16[8,2,384,384]{3,2,1,0:T(8,128)(2,1)}), bf16[8,2,384,384]{3,2,1,0:T(8,128)(2,1)}, u32[]{:S(2)}, u32[]{:S(2)}) async-start(bf16[8,2,384,384]{3,2,1,0:T(8,128)(2,1)} %shard_map.38), calls=%async_computation.2 | async-start | bytes 9437184 | tf_op jit(solution)/shard_map/all_to_all | solution.py:257
  82.7 20.3 %collective-permute-start.10 = (bf16[2,256,384]{2,1,0:T(8,128)(2,1)}, bf16[2,256,384]{2,1,0:T(8,128)(2,1)}, u32[]{:S(2)}, u32[]{:S(2)}) collective-permute-start(bf16[2,256,384]{2,1,0:T(8,128)(2,1)} %get-tuple-element.94), channel_id=1, source_target_pairs={{0,0},{1,1},{2,2},{3,3},{4,64},{5,65},{6,66},{7,67},{8,12},{9,13},... | collective-permute-start | bytes 1179656 | tf_op jit(solution)/shard_map/ppermute | solution.py:316
  88.2 16.9 %collective-permute-start.11 = (bf16[2,256,384]{2,1,0:T(8,128)(2,1)}, bf16[2,256,384]{2,1,0:T(8,128)(2,1)}, u32[]{:S(2)}, u32[]{:S(2)}) collective-permute-start(bf16[2,256,384]{2,1,0:T(8,128)(2,1)} %get-tuple-element.100), channel_id=1, source_target_pairs={{0,4},{1,5},{2,6},{3,7},{4,68},{5,69},{6,70},{7,71},{8,8},{9,9},{1... | collective-permute-start | bytes 1179656 | tf_op jit(solution)/shard_map/ppermute | solution.py:316
  91.0 16.0 %collective-permute-start.13 = (bf16[2,256,384]{2,1,0:T(8,128)(2,1)}, bf16[2,256,384]{2,1,0:T(8,128)(2,1)}, u32[]{:S(2)}, u32[]{:S(2)}) collective-permute-start(bf16[2,256,384]{2,1,0:T(8,128)(2,1)} %get-tuple-element.107), channel_id=1, source_target_pairs={{0,32},{1,33},{2,34},{3,35},{4,96},{5,97},{6,98},{7,99},{8,44},{9,... | collective-permute-start | bytes 1179656 | tf_op jit(solution)/shard_map/ppermute | solution.py:316
  94.0 20.2 %collective-permute-start.14 = (bf16[2,256,384]{2,1,0:T(8,128)(2,1)}, bf16[2,256,384]{2,1,0:T(8,128)(2,1)}, u32[]{:S(2)}, u32[]{:S(2)}) collective-permute-start(bf16[2,256,384]{2,1,0:T(8,128)(2,1)} %get-tuple-element.108), channel_id=1, source_target_pairs={{0,36},{1,37},{2,38},{3,39},{4,100},{5,101},{6,102},{7,103},{8,40}... | collective-permute-start | bytes 1179656 | tf_op jit(solution)/shard_map/ppermute | solution.py:316
  102.9 12.8 %collective-permute-start.15 = (bf16[2,256,384]{2,1,0:T(8,128)(2,1)}, bf16[2,256,384]{2,1,0:T(8,128)(2,1)}, u32[]{:S(2)}, u32[]{:S(2)}) collective-permute-start(bf16[2,256,384]{2,1,0:T(8,128)(2,1)} %get-tuple-element.109), channel_id=1, source_target_pairs={{0,16},{1,17},{2,18},{3,19},{4,80},{5,81},{6,82},{7,83},{8,28},{9,... | collective-permute-start | bytes 1179656 | tf_op jit(solution)/shard_map/ppermute | solution.py:316
  104.2 19.4 %collective-permute-start.16 = (bf16[2,256,384]{2,1,0:T(8,128)(2,1)}, bf16[2,256,384]{2,1,0:T(8,128)(2,1)}, u32[]{:S(2)}, u32[]{:S(2)}) collective-permute-start(bf16[2,256,384]{2,1,0:T(8,128)(2,1)} %get-tuple-element.110), channel_id=1, source_target_pairs={{0,20},{1,21},{2,22},{3,23},{4,84},{5,85},{6,86},{7,87},{8,24},{9,... | collective-permute-start | bytes 1179656 | tf_op jit(solution)/shard_map/ppermute | solution.py:316
  105.1 19.4 %collective-permute-start.17 = (bf16[2,256,384]{2,1,0:T(8,128)(2,1)}, bf16[2,256,384]{2,1,0:T(8,128)(2,1)}, u32[]{:S(2)}, u32[]{:S(2)}) collective-permute-start(bf16[2,256,384]{2,1,0:T(8,128)(2,1)} %get-tuple-element.111), channel_id=1, source_target_pairs={{0,48},{1,49},{2,50},{3,51},{4,112},{5,113},{6,114},{7,115},{8,60}... | collective-permute-start | bytes 1179656 | tf_op jit(solution)/shard_map/ppermute | solution.py:316
  107.0 22.1 %collective-permute-start.18 = (bf16[2,256,384]{2,1,0:T(8,128)(2,1)}, bf16[2,256,384]{2,1,0:T(8,128)(2,1)}, u32[]{:S(2)}, u32[]{:S(2)}) collective-permute-start(bf16[2,256,384]{2,1,0:T(8,128)(2,1)} %get-tuple-element.112), channel_id=1, source_target_pairs={{0,52},{1,53},{2,54},{3,55},{4,116},{5,117},{6,118},{7,119},{8,56}... | collective-permute-start | bytes 1179656 | tf_op jit(solution)/shard_map/ppermute | solution.py:316
  129.1 58.9 %all-to-all-start.3 = ((bf16[8,2,384,384]{3,2,1,0:T(8,128)(2,1)}), bf16[8,2,384,384]{3,2,1,0:T(8,128)(2,1)}, u32[]{:S(2)}, u32[]{:S(2)}) async-start(bf16[8,2,384,384]{3,2,1,0:T(8,128)(2,1)} %shard_map.43), calls=%async_computation.3 | async-start | bytes 9437184 | tf_op jit(solution)/shard_map/all_to_all | solution.py:257
  142.6 21.5 %collective-permute-start.12 = (bf16[2,384,384]{2,1,0:T(8,128)(2,1)}, bf16[2,384,384]{2,1,0:T(8,128)(2,1)S(1)}, u32[]{:S(2)}, u32[]{:S(2)}) collective-permute-start(bf16[2,384,384]{2,1,0:T(8,128)(2,1)} %get-tuple-element.106), channel_id=1, source_target_pairs={{0,0},{1,1},{2,2},{3,3},{4,64},{5,65},{6,66},{7,67},{8,12},{9,13},... | collective-permute-start | bytes 1769480 | tf_op jit(solution)/shard_map/ppermute | solution.py:316
  148.1 48.2 %collective-permute-start.19 = (bf16[2,384,384]{2,1,0:T(8,128)(2,1)}, bf16[2,384,384]{2,1,0:T(8,128)(2,1)S(1)}, u32[]{:S(2)}, u32[]{:S(2)}) collective-permute-start(bf16[2,384,384]{2,1,0:T(8,128)(2,1)} %get-tuple-element.118), channel_id=1, source_target_pairs={{0,4},{1,5},{2,6},{3,7},{4,68},{5,69},{6,70},{7,71},{8,8},{9,9},{1... | collective-permute-start | bytes 1769480 | tf_op jit(solution)/shard_map/ppermute | solution.py:316
  150.9 49.3 %collective-permute-start.21 = (bf16[2,384,384]{2,1,0:T(8,128)(2,1)}, bf16[2,384,384]{2,1,0:T(8,128)(2,1)S(1)}, u32[]{:S(2)}, u32[]{:S(2)}) collective-permute-start(bf16[2,384,384]{2,1,0:T(8,128)(2,1)} %get-tuple-element.125), channel_id=1, source_target_pairs={{0,32},{1,33},{2,34},{3,35},{4,96},{5,97},{6,98},{7,99},{8,44},{9,... | collective-permute-start | bytes 1769480 | tf_op jit(solution)/shard_map/ppermute | solution.py:316
  151.1 49.1 %collective-permute-start.22 = (bf16[2,384,384]{2,1,0:T(8,128)(2,1)}, bf16[2,384,384]{2,1,0:T(8,128)(2,1)S(1)}, u32[]{:S(2)}, u32[]{:S(2)}) collective-permute-start(bf16[2,384,384]{2,1,0:T(8,128)(2,1)} %get-tuple-element.126), channel_id=1, source_target_pairs={{0,36},{1,37},{2,38},{3,39},{4,100},{5,101},{6,102},{7,103},{8,40}... | collective-permute-start | bytes 1769480 | tf_op jit(solution)/shard_map/ppermute | solution.py:316
  164.1 87.8 %copy-start.6 = (bf16[2,384,384]{2,1,0:T(8,128)(2,1)}, bf16[2,384,384]{2,1,0:T(8,128)(2,1)S(1)}, u32[]{:S(2)}) copy-start(bf16[2,384,384]{2,1,0:T(8,128)(2,1)S(1)} %collective-permute-done.12.refs_0_) | copy-start | bytes 1769476
  164.1 39.5 %collective-permute-start.23 = (bf16[2,384,384]{2,1,0:T(8,128)(2,1)}, bf16[2,384,384]{2,1,0:T(8,128)(2,1)S(1)}, u32[]{:S(2)}, u32[]{:S(2)}) collective-permute-start(bf16[2,384,384]{2,1,0:T(8,128)(2,1)} %get-tuple-element.127), channel_id=1, source_target_pairs={{0,16},{1,17},{2,18},{3,19},{4,80},{5,81},{6,82},{7,83},{8,28},{9,... | collective-permute-start | bytes 1769480 | tf_op jit(solution)/shard_map/ppermute | solution.py:316
  166.4 41.3 %collective-permute-start.24 = (bf16[2,384,384]{2,1,0:T(8,128)(2,1)}, bf16[2,384,384]{2,1,0:T(8,128)(2,1)S(1)}, u32[]{:S(2)}, u32[]{:S(2)}) collective-permute-start(bf16[2,384,384]{2,1,0:T(8,128)(2,1)} %get-tuple-element.128), channel_id=1, source_target_pairs={{0,20},{1,21},{2,22},{3,23},{4,84},{5,85},{6,86},{7,87},{8,24},{9,... | collective-permute-start | bytes 1769480 | tf_op jit(solution)/shard_map/ppermute | solution.py:316
  196.3 58.5 %copy-start.7 = (bf16[2,384,384]{2,1,0:T(8,128)(2,1)}, bf16[2,384,384]{2,1,0:T(8,128)(2,1)S(1)}, u32[]{:S(2)}) copy-start(bf16[2,384,384]{2,1,0:T(8,128)(2,1)S(1)} %collective-permute-done.19.refs_1_) | copy-start | bytes 1769476
  196.3 25.5 %collective-permute-start.25 = (bf16[2,384,384]{2,1,0:T(8,128)(2,1)}, bf16[2,384,384]{2,1,0:T(8,128)(2,1)}, u32[]{:S(2)}, u32[]{:S(2)}) collective-permute-start(bf16[2,384,384]{2,1,0:T(8,128)(2,1)} %get-tuple-element.129), channel_id=1, source_target_pairs={{0,48},{1,49},{2,50},{3,51},{4,112},{5,113},{6,114},{7,115},{8,60}... | collective-permute-start | bytes 1769480 | tf_op jit(solution)/shard_map/ppermute | solution.py:316
  200.1 54.6 %copy-start.8 = (bf16[2,384,384]{2,1,0:T(8,128)(2,1)}, bf16[2,384,384]{2,1,0:T(8,128)(2,1)S(1)}, u32[]{:S(2)}) copy-start(bf16[2,384,384]{2,1,0:T(8,128)(2,1)S(1)} %collective-permute-done.21.refs_2_) | copy-start | bytes 1769476
  200.2 21.8 %collective-permute-start.26 = (bf16[2,384,384]{2,1,0:T(8,128)(2,1)}, bf16[2,384,384]{2,1,0:T(8,128)(2,1)}, u32[]{:S(2)}, u32[]{:S(2)}) collective-permute-start(bf16[2,384,384]{2,1,0:T(8,128)(2,1)} %get-tuple-element.130), channel_id=1, source_target_pairs={{0,52},{1,53},{2,54},{3,55},{4,116},{5,117},{6,118},{7,119},{8,56}... | collective-permute-start | bytes 1769480 | tf_op jit(solution)/shard_map/ppermute | solution.py:316
  200.2 54.6 %copy-start.9 = (bf16[2,384,384]{2,1,0:T(8,128)(2,1)}, bf16[2,384,384]{2,1,0:T(8,128)(2,1)S(1)}, u32[]{:S(2)}) copy-start(bf16[2,384,384]{2,1,0:T(8,128)(2,1)S(1)} %collective-permute-done.22.refs_3_) | copy-start | bytes 1769476
  200.2 26.4 %collective-permute-start.20 = (bf16[2,384,384]{2,1,0:T(8,128)(2,1)}, bf16[2,384,384]{2,1,0:T(8,128)(2,1)}, u32[]{:S(2)}, u32[]{:S(2)}) collective-permute-start(bf16[2,384,384]{2,1,0:T(8,128)(2,1)} %get-tuple-element.124), channel_id=1, source_target_pairs={{0,0},{1,1},{2,2},{3,3},{4,64},{5,65},{6,66},{7,67},{8,12},{9,13},... | collective-permute-start | bytes 1769480 | tf_op jit(solution)/shard_map/ppermute | solution.py:316
  203.6 51.2 %copy-start.10 = (bf16[2,384,384]{2,1,0:T(8,128)(2,1)}, bf16[2,384,384]{2,1,0:T(8,128)(2,1)S(1)}, u32[]{:S(2)}) copy-start(bf16[2,384,384]{2,1,0:T(8,128)(2,1)S(1)} %collective-permute-done.23.refs_0_) | copy-start | bytes 1769476
  203.6 39.2 %collective-permute-start.31 = (bf16[2,384,384]{2,1,0:T(8,128)(2,1)}, bf16[2,384,384]{2,1,0:T(8,128)(2,1)}, u32[]{:S(2)}, u32[]{:S(2)}) collective-permute-start(bf16[2,384,384]{2,1,0:T(8,128)(2,1)} %get-tuple-element.140), channel_id=1, source_target_pairs={{0,4},{1,5},{2,6},{3,7},{4,68},{5,69},{6,70},{7,71},{8,8},{9,9},{1... | collective-permute-start | bytes 1769480 | tf_op jit(solution)/shard_map/ppermute | solution.py:316
  207.7 47.1 %copy-start.11 = (bf16[2,384,384]{2,1,0:T(8,128)(2,1)}, bf16[2,384,384]{2,1,0:T(8,128)(2,1)S(1)}, u32[]{:S(2)}) copy-start(bf16[2,384,384]{2,1,0:T(8,128)(2,1)S(1)} %collective-permute-done.24.refs_1_) | copy-start | bytes 1769476
  207.7 37.3 %collective-permute-start.32 = (bf16[2,384,384]{2,1,0:T(8,128)(2,1)}, bf16[2,384,384]{2,1,0:T(8,128)(2,1)}, u32[]{:S(2)}, u32[]{:S(2)}) collective-permute-start(bf16[2,384,384]{2,1,0:T(8,128)(2,1)} %get-tuple-element.141), channel_id=1, source_target_pairs={{0,32},{1,33},{2,34},{3,35},{4,96},{5,97},{6,98},{7,99},{8,44},{9,... | collective-permute-start | bytes 1769480 | tf_op jit(solution)/shard_map/ppermute | solution.py:316
  221.8 39.5 %collective-permute-start.33 = (bf16[2,384,384]{2,1,0:T(8,128)(2,1)}, bf16[2,384,384]{2,1,0:T(8,128)(2,1)}, u32[]{:S(2)}, u32[]{:S(2)}) collective-permute-start(bf16[2,384,384]{2,1,0:T(8,128)(2,1)} %get-tuple-element.142), channel_id=1, source_target_pairs={{0,36},{1,37},{2,38},{3,39},{4,100},{5,101},{6,102},{7,103},{8,40}... | collective-permute-start | bytes 1769480 | tf_op jit(solution)/shard_map/ppermute | solution.py:316
  226.6 37.9 %collective-permute-start.27 = (bf16[2,384,384]{2,1,0:T(8,128)(2,1)}, bf16[2,384,384]{2,1,0:T(8,128)(2,1)}, u32[]{:S(2)}, u32[]{:S(2)}) collective-permute-start(bf16[2,384,384]{2,1,0:T(8,128)(2,1)} %get-tuple-element.135), channel_id=1, source_target_pairs={{0,16},{1,17},{2,18},{3,19},{4,80},{5,81},{6,82},{7,83},{8,28},{9,... | collective-permute-start | bytes 1769480 | tf_op jit(solution)/shard_map/ppermute | solution.py:316
  242.8 21.7 %collective-permute-start.28 = (bf16[2,384,384]{2,1,0:T(8,128)(2,1)}, bf16[2,384,384]{2,1,0:T(8,128)(2,1)}, u32[]{:S(2)}, u32[]{:S(2)}) collective-permute-start(bf16[2,384,384]{2,1,0:T(8,128)(2,1)} %get-tuple-element.136), channel_id=1, source_target_pairs={{0,20},{1,21},{2,22},{3,23},{4,84},{5,85},{6,86},{7,87},{8,24},{9,... | collective-permute-start | bytes 1769480 | tf_op jit(solution)/shard_map/ppermute | solution.py:316
  242.8 25.3 %collective-permute-start.29 = (bf16[2,384,384]{2,1,0:T(8,128)(2,1)}, bf16[2,384,384]{2,1,0:T(8,128)(2,1)}, u32[]{:S(2)}, u32[]{:S(2)}) collective-permute-start(bf16[2,384,384]{2,1,0:T(8,128)(2,1)} %get-tuple-element.137), channel_id=1, source_target_pairs={{0,48},{1,49},{2,50},{3,51},{4,112},{5,113},{6,114},{7,115},{8,60}... | collective-permute-start | bytes 1769480 | tf_op jit(solution)/shard_map/ppermute | solution.py:316
  245.1 34.1 %collective-permute-start.30 = (bf16[2,384,384]{2,1,0:T(8,128)(2,1)}, bf16[2,384,384]{2,1,0:T(8,128)(2,1)}, u32[]{:S(2)}, u32[]{:S(2)}) collective-permute-start(bf16[2,384,384]{2,1,0:T(8,128)(2,1)} %get-tuple-element.138), channel_id=1, source_target_pairs={{0,52},{1,53},{2,54},{3,55},{4,116},{5,117},{6,118},{7,119},{8,56}... | collective-permute-start | bytes 1769480 | tf_op jit(solution)/shard_map/ppermute | solution.py:316
